TPU v7x, 256 devices: a whole 4x4x8 slice. The times are simulated.
256 devices in a mesh: seq: 64 (over y, x_hi, z), head: 4 (over x_lo, core).
Axes of the slice: x: 4 (x_hi: 2, x_lo: 2; x = x_hi * 2 + x_lo), y: 4, z: 8, core: 2. Of those that a mesh axis runs over, the one named last changes fastest.
Arguments:
- qkv: bfloat16 [3, 49152, 1536], P(None, ('seq', 'head')), may hold values from -5 to 5
- key_tiles: int32 [12, 128, 27], P('head', 'seq'), may hold values from -1 to 127, as said below
Outputs:
- attended: bfloat16 [49152, 1536], P(('seq', 'head'))
Inputs may be any that keep to these rules, and one draw needn't show every extreme that they name: Each list key_tiles[n, g] names distinct tiles, the query tile g among them, each differing from g by at most 1 in the time tile, the tile row and the tile column; named tiles come first and -1 fills the rest of the list.
All inputs are finite; a program needn't handle non-finite values.
Results may differ from a plain program's by a relative error of at most 0.0035.
Values may be sent and summed in bfloat16 or wider, within the bound.
No kernel may reach another device: no remote copies, remote signals or barrier semaphores. Data moves between devices by JAX's collectives and lax.ppermute only.
A program may use at most 192 MiB of HBM per device.

v0:
```python
import jax
import jax.numpy as jnp
from jax import lax
from jax.sharding import PartitionSpec as P

TIME_TILES = 4
TILE_ROWS = 4


def from_behind(x, axis, by):
    length = lax.axis_size(axis)
    pairs = [(i, i + by) for i in range(length) if 0 <= i + by < length]
    return lax.ppermute(x, axis, pairs)


def swapped(value, axis, distance):
    mask = 2**distance
    pairs = [(source, source ^ mask) for source in range(lax.axis_size(axis))]
    return lax.ppermute(value, axis, pairs)


def attend(query_rows, keys, values, named_mask):
    blocks, slot_count, row_count, head_feature_width = keys.shape
    key_matrix_rows = keys.reshape(blocks, slot_count * row_count, head_feature_width)
    value_matrix_rows = values.reshape(blocks, slot_count * row_count, head_feature_width)
    logit_matrix = jnp.einsum(
        "jxg,jog->jxo", query_rows, key_matrix_rows, preferred_element_type=jnp.float32
    ) * head_feature_width ** (-0.5)
    score_mask = jnp.repeat(named_mask, row_count, axis=1)[:, None, :]
    logit_matrix = jnp.where(score_mask, logit_matrix, -jnp.inf)
    row_max = jnp.max(logit_matrix, axis=-1, keepdims=True)
    weights = jnp.exp(logit_matrix - row_max)
    row_total = jnp.sum(weights, axis=-1, keepdims=True)
    weighted_value_sum = jnp.einsum(
        "aop,ape->aoe",
        weights.astype(jnp.bfloat16),
        value_matrix_rows,
        preferred_element_type=jnp.float32,
    )
    return (weighted_value_sum / row_total).astype(jnp.bfloat16)


def pass_along(block, step_by):
    return from_behind(block, "seq", step_by)


def local(qkv, key_tiles):
    head_count = key_tiles.shape[0]
    col_count = lax.axis_size("seq") * 2 // (TIME_TILES * TILE_ROWS)
    time_stride = 1
    col_stride = 2 * TIME_TILES
    near_cols = 3
    seq_index = lax.axis_index("seq")
    own_time = seq_index % TIME_TILES
    own_pair = seq_index // TIME_TILES % 2
    own_col = seq_index // (2 * TIME_TILES)
    spread = lax.all_to_all(qkv, "head", split_axis=2, concat_axis=1, tiled=True)
    tile_tokens = spread.shape[1] // 2
    head_feature_width = spread.shape[2] // head_count
    query_rows = (
        spread[0].reshape(2, tile_tokens, head_count, head_feature_width).transpose(2, 0, 1, 3)
    )
    kv_pairs = (
        spread[1:3]
        .reshape(2, 2, tile_tokens, head_count, head_feature_width)
        .transpose(0, 3, 1, 2, 4)
    )
    side_bricks = [pass_along(kv_pairs, step_by) for step_by in (col_stride, -col_stride)]
    columns = jnp.stack([side_bricks[0], kv_pairs, side_bricks[1]], axis=2)
    edge_send = jnp.where(own_pair == 0, columns[:, :, :, 1], columns[:, :, :, 0])
    partner_rows = swapped(edge_send, "seq", 2)
    row_stack = jnp.concatenate(
        [partner_rows[:, :, :, None], columns, partner_rows[:, :, :, None]], axis=3
    )
    time_after, time_before = [
        pass_along(row_stack, step_by) for step_by in (-time_stride, time_stride)
    ]
    key_pool = jnp.stack([time_before, row_stack, time_after], axis=2)
    pool_size = 3 * near_cols * 4
    key_flat = key_pool[0].reshape(head_count * pool_size, tile_tokens, head_feature_width)
    value_flat = key_pool[1].reshape(head_count * pool_size, tile_tokens, head_feature_width)
    named_mask = key_tiles >= 0
    safe_tiles = jnp.where(named_mask, key_tiles, 0)
    tile_time = safe_tiles // 2 % TIME_TILES
    tile_row = safe_tiles // (2 * TIME_TILES) % 2 * 2 + safe_tiles % 2
    tile_col = safe_tiles // (4 * TIME_TILES)
    local_index = (
        ((tile_time - own_time + 1) * near_cols + tile_col - own_col + near_cols // 2) * 4
        + tile_row
        - 2 * own_pair
        + 1
    )
    head_base = (jnp.arange(head_count, dtype=jnp.int32) * pool_size)[:, None, None]
    pool_index = jnp.where(named_mask, local_index, 0) + head_base

    def full_block(operands):
        these_queries, these_index, these_named = operands
        return attend(these_queries, key_flat[these_index], value_flat[these_index], these_named)

    attended_tiles = lax.map(full_block, (query_rows, pool_index, named_mask))
    brick_out = attended_tiles.transpose(1, 2, 0, 3).reshape(
        2 * tile_tokens, head_count * head_feature_width
    )
    return lax.all_to_all(brick_out, "head", split_axis=0, concat_axis=1, tiled=True)


def solution(mesh):
    placed = (P(None, ("seq", "head"), None), P("head", "seq", None))
    return jax.shard_map(
        local, mesh=mesh, in_specs=placed, out_specs=P(("seq", "head"), None), check_vma=False
    )
```

profile of v0, /device:TPU:8, one launch (start us, length us, event | category | flops | bytes accessed | tf_op | source)
XLA Modules:
  0.0 655.9 jit_solution(152715509326859987)
XLA Ops:
  0.0 5.5 copy.21
  5.5 40.6 %all_to_all.34 = bf16[3,192,1536]{1,0,2:T(4,128)(2,1)S(1)} all-to-all(bf16[3,192,1536]{1,0,2:T(4,128)(2,1)} %copy.21), channel_id=1, replica_groups=mesh['seq'=64,'head'=4] {'head'}, dimensions={2} | all-to-all | bytes 3538944 | tf_op jit(solution)/shard_map/all_to_all | solution.py:57
  46.1 3.4 copy.22
  49.5 1.4 slice.31
  51.3 1.2 copy.23
  52.5 4.8 collective-permute-start.1
  57.3 2.5 collective-permute-start
  59.9 25.2 %collective-permute-done.1 = bf16[2,3,2,384,128]{4,3,2,1,0:T(8,128)(2,1)} collective-permute-done((bf16[2,3,2,384,128]{4,3,2,1,0:T(8,128)(2,1)}, bf16[2,3,2,384,128]{4,3,2,1,0:T(8,128)(2,1)}, u32[]{:S(2)}, u32[]{:S(2)}) %collective-permute-start.1) | collective-permute-done | bytes 1179680 | tf_op jit(solution)/shard_map/ppermute | solution.py:13
  85.1 2.3 copy.48
  87.4 23.1 %collective-permute-done = bf16[2,3,2,384,128]{4,3,2,1,0:T(8,128)(2,1)} collective-permute-done((bf16[2,3,2,384,128]{4,3,2,1,0:T(8,128)(2,1)}, bf16[2,3,2,384,128]{4,3,2,1,0:T(8,128)(2,1)}, u32[]{:S(2)}, u32[]{:S(2)}) %collective-permute-start) | collective-permute-done | bytes 1179680 | tf_op jit(solution)/shard_map/ppermute | solution.py:13
  110.4 2.3 copy.49
  112.7 4.0 pad_maximum_fusion.2
  118.4 5.5 collective-permute-start.2
  123.9 74.0 %collective-permute-done.2 = bf16[2,3,3,384,128]{4,3,2,1,0:T(8,128)(2,1)S(1)} collective-permute-done((bf16[2,3,3,384,128]{4,3,2,1,0:T(8,128)(2,1)S(1)}, bf16[2,3,3,384,128]{4,3,2,1,0:T(8,128)(2,1)S(1)}, u32[]{:S(2)}, u32[]{:S(2)}) %collective-permute-start.2) | collective-permute-done | bytes 1769504 | tf_op jit(solution)/shard_map/ppermute | solution.py:19
  197.9 1.5 copy.47
  199.5 1.4 copy-done.2
  200.9 9.4 %pad_maximum_fusion.1 = bf16[2,3,3,4,384,128]{5,1,4,3,0,2:T(4,128)(2,1)} fusion(bf16[2,3,3,1,384,128]{5,1,4,3,0,2:T(4,128)(2,1)S(1)} %bitcast.96, bf16[2,3,1,2,384,128]{5,1,4,3,0,2:T(4,128)(2,1)S(1)} %bitcast.91, bf16[2,3,1,2,384,128]{5,1,4,3,0,2:T(4,128)(2,1)S(1)} %bitcast.83, bf16[2,3,1,2,384,128]{5,1,4,3,0,2:T(4,128)(2,1)S(1)} %bitcast.94), kind=kLoop, calls=%fused_computation.24 | loop fusion | flops 14155776 | bytes 12386304 | tf_op jit(solution)/shard_map/concatenate | solution.py:72
  210.3 8.5 %copy.29 = bf16[2,3,3,4,384,128]{5,4,3,2,1,0:T(8,128)(2,1)} copy(bf16[2,3,3,4,384,128]{5,1,4,3,0,2:T(4,128)(2,1)} %pad_maximum_fusion.1) | data formatting | bytes 14155776 | tf_op jit(solution)/shard_map/concatenate | solution.py:72
  218.8 1.9 collective-permute-start.4
  220.7 4.7 collective-permute-start.3
  225.6 2.0 slice.30
  227.6 2.6 reshape_squeeze.9
  230.2 2.0 copy.35
  232.2 10.5 %fusion.37 = bf16[2,3,1,3,4,384,128]{6,1,5,4,0,3,2:T(4,128)(2,1)S(1)} fusion(bf16[2,3,3,1,384,128]{5,1,4,3,0,2:T(4,128)(2,1)} %bitcast.97, bf16[2,3,1,2,384,128]{5,1,4,3,0,2:T(4,128)(2,1)S(1)} %bitcast.92, bf16[2,3,1,2,384,128]{5,1,4,3,0,2:T(4,128)(2,1)S(1)} %bitcast.84, bf16[2,3,1,2,384,128]{5,1,4,3,0,2:T(4,128)(2,1)} %bitcast.95), kind=kLoop, calls=%fused_computation.63 | loop fusion | flops 14155776 | bytes 12386304 | tf_op jit(solution)/shard_map/stack | solution.py:78
  242.8 131.2 %collective-permute-done.4 = bf16[2,3,3,4,384,128]{5,4,3,2,1,0:T(8,128)(2,1)} collective-permute-done((bf16[2,3,3,4,384,128]{5,4,3,2,1,0:T(8,128)(2,1)}, bf16[2,3,3,4,384,128]{5,4,3,2,1,0:T(8,128)(2,1)}, u32[]{:S(2)}, u32[]{:S(2)}) %collective-permute-start.4) | collective-permute-done | bytes 7077920 | tf_op jit(solution)/shard_map/ppermute | solution.py:13
  373.9 10.3 %copy.45 = bf16[2,3,3,4,384,128]{5,1,4,3,0,2:T(4,128)(2,1)S(1)} copy(bf16[2,3,3,4,384,128]{5,4,3,2,1,0:T(8,128)(2,1)} %collective-permute-done.4) | data formatting | bytes 14155776 | tf_op jit(solution)/shard_map/ppermute | solution.py:13
  384.3 11.0 %copy.46 = bf16[2,3,3,4,384,128]{5,1,4,3,0,2:T(4,128)(2,1)} copy(bf16[2,3,3,4,384,128]{5,4,3,2,1,0:T(8,128)(2,1)} %collective-permute-done.3) | data formatting | bytes 14155776 | tf_op jit(solution)/shard_map/ppermute | solution.py:13
  395.3 27.2 %pad_maximum_fusion = bf16[2,3,3,3,4,384,128]{6,1,5,4,0,3,2:T(4,128)(2,1)} fusion(bf16[2,3,1,3,4,384,128]{6,1,5,4,0,3,2:T(4,128)(2,1)S(1)} %bitcast.85, bf16[2,3,1,3,4,384,128]{6,1,5,4,0,3,2:T(4,128)(2,1)S(1)} %fusion.37, bf16[2,3,1,3,4,384,128]{6,1,5,4,0,3,2:T(4,128)(2,1)} %bitcast.86), kind=kLoop, calls=%fused_computation.23 | loop fusion | flops 21233664 | bytes 42467328 | tf_op jit(solution)/shard_map/stack | solution.py:78
  422.5 19.9 %fusion.34 = (bf16[1,3,3,3,4,384,128]{6,1,5,4,0,3,2:T(4,128)(2,1)}, bf16[1,3,3,3,4,384,128]{6,1,5,4,0,3,2:T(4,128)(2,1)}) fusion(bf16[2,3,3,3,4,384,128]{6,1,5,4,0,3,2:T(4,128)(2,1)} %pad_maximum_fusion), kind=kLoop, calls=%fused_computation.62 | loop fusion | bytes 42467328 | tf_op jit(solution)/shard_map/slice | solution.py:81
  442.3 12.1 %copy.33 = bf16[1,3,3,3,4,384,128]{6,5,4,3,2,1,0:T(8,128)(2,1)} copy(bf16[1,3,3,3,4,384,128]{6,1,5,4,0,3,2:T(4,128)(2,1)} %get-tuple-element.81) | data formatting | bytes 21233664 | tf_op jit(solution)/shard_map/slice | solution.py:80
  455.5 5.7 copy.34
  461.1 180.4 %while.10 = (s32[]{:T(128)}, bf16[3,2,384,128]{3,2,1,0:T(8,128)(2,1)S(1)}, pred[3,2,27]{2,1,0:T(4,128)(4,1)S(1)}, bf16[3,2,384,128]{3,2,1,0:T(8,128)(2,1)}, s32[...) while((s32[]{:T(128)}, ...), condition=%wide.region_3.4_spmd, body=%wide.region_0.3_spmd.sunk | while | flops 4164648448 | bytes 127962088 | solution.py:100
  461.2 7.7 %gather_fusion.1 = bf16[54,384,128]{2,1,0:T(8,128)(2,1)} fusion(bf16[108,384,128]{2,1,0:T(8,128)(2,1)} %get-tuple-element.150, s32[1024]{0:T(1024)S(1)} %pad_clamp_fusion.2), kind=kCustom, calls=%fused_computation.clone.1 | custom fusion | bytes 10617048 | tf_op jit(solution)/shard_map/while/body/eval_jaxpr/gather | solution.py:98
  469.0 14.9 %fusion.47 = (f32[2,384]{1,0:T(2,128)S(1)}, f32[2,384,10368]{2,1,0:T(8,128)}) fusion(pred[2,10368]{1,0:T(4,128)(4,1)S(1)} %bitcast.87, bf16[2,10368,128]{2,1,0:T(8,128)(2,1)} %bitcast.77, bf16[3,2,384,128]{3,2,1,0:T(8,128)(2,1)} %get-tuple-element.148, s32[]{:T(128)} %get-tuple-element.137), kind=kOutput, calls=%fused_computation.4.clone.1 | convolution fusion | flops 2062318848 | bytes 37379840 | tf_op jit(solution)/shard_map/while/body/eval_jaxpr/jxg,jog->jxo/dot_general | solution.py:26
  483.9 14.3 %fusion.48 = f32[2,384]{1,0:T(2,128)S(1)} fusion(f32[2,384,10368]{2,1,0:T(8,128)} %get-tuple-element.127, f32[2,384]{1,0:T(2,128)S(1)} %get-tuple-element.128, pred[2,10368]{1,0:T(4,128)(4,1)S(1)} %bitcast.88), kind=kLoop, calls=%fused_computation.5.clone.1 | loop fusion | flops 31849728 | bytes 31877376 | tf_op jit(solution)/shard_map/while/body/eval_jaxpr/reduce_sum | solution.py:33
  498.2 7.7 %gather_fusion = bf16[54,384,128]{2,1,0:T(8,128)(2,1)} fusion(bf16[108,384,128]{2,1,0:T(8,128)(2,1)} %get-tuple-element.151, s32[1024]{0:T(1024)S(1)} %pad_clamp_fusion.2), kind=kCustom, calls=%fused_computation.1.clone.1 | custom fusion | bytes 10617048 | tf_op jit(solution)/shard_map/while/body/eval_jaxpr/gather | solution.py:98
  505.8 15.4 %fusion.49 = bf16[3,2,384,128]{3,2,1,0:T(8,128)(2,1)S(1)} fusion(bf16[3,2,384,128]{3,2,1,0:T(8,128)(2,1)S(1)} %get-tuple-element.138, s32[]{:T(128)} %get-tuple-element.137, bf16[2,10368,128]{2,1,0:T(8,128)(2,1)} %bitcast.78, f32[2,384,10368]{2,1,0:T(8,128)} %get-tuple-element.127, f32[2,384]{1,0:T(2,128)S(1)} %get-tuple-element.128, ...), kind=kOutput, calls=%fused_computation.12.clone.1 | convolution fusion | flops 2070478848 | bytes 37403140 | tf_op jit(solution)/shard_map/while/body/eval_jaxpr/aop,ape->aoe/dot_general | solution.py:34
  521.4 7.7 %gather_fusion.1 = bf16[54,384,128]{2,1,0:T(8,128)(2,1)} fusion(bf16[108,384,128]{2,1,0:T(8,128)(2,1)} %get-tuple-element.150, s32[1024]{0:T(1024)S(1)} %pad_clamp_fusion.2), kind=kCustom, calls=%fused_computation.clone.1 | custom fusion | bytes 10617048 | tf_op jit(solution)/shard_map/while/body/eval_jaxpr/gather | solution.py:98
  529.2 14.9 %fusion.47 = (f32[2,384]{1,0:T(2,128)S(1)}, f32[2,384,10368]{2,1,0:T(8,128)}) fusion(pred[2,10368]{1,0:T(4,128)(4,1)S(1)} %bitcast.87, bf16[2,10368,128]{2,1,0:T(8,128)(2,1)} %bitcast.77, bf16[3,2,384,128]{3,2,1,0:T(8,128)(2,1)} %get-tuple-element.148, s32[]{:T(128)} %get-tuple-element.137), kind=kOutput, calls=%fused_computation.4.clone.1 | convolution fusion | flops 2062318848 | bytes 37379840 | tf_op jit(solution)/shard_map/while/body/eval_jaxpr/jxg,jog->jxo/dot_general | solution.py:26
  544.1 14.3 %fusion.48 = f32[2,384]{1,0:T(2,128)S(1)} fusion(f32[2,384,10368]{2,1,0:T(8,128)} %get-tuple-element.127, f32[2,384]{1,0:T(2,128)S(1)} %get-tuple-element.128, pred[2,10368]{1,0:T(4,128)(4,1)S(1)} %bitcast.88), kind=kLoop, calls=%fused_computation.5.clone.1 | loop fusion | flops 31849728 | bytes 31877376 | tf_op jit(solution)/shard_map/while/body/eval_jaxpr/reduce_sum | solution.py:33
  558.3 7.7 %gather_fusion = bf16[54,384,128]{2,1,0:T(8,128)(2,1)} fusion(bf16[108,384,128]{2,1,0:T(8,128)(2,1)} %get-tuple-element.151, s32[1024]{0:T(1024)S(1)} %pad_clamp_fusion.2), kind=kCustom, calls=%fused_computation.1.clone.1 | custom fusion | bytes 10617048 | tf_op jit(solution)/shard_map/while/body/eval_jaxpr/gather | solution.py:98
  566.0 15.4 %fusion.49 = bf16[3,2,384,128]{3,2,1,0:T(8,128)(2,1)S(1)} fusion(bf16[3,2,384,128]{3,2,1,0:T(8,128)(2,1)S(1)} %get-tuple-element.138, s32[]{:T(128)} %get-tuple-element.137, bf16[2,10368,128]{2,1,0:T(8,128)(2,1)} %bitcast.78, f32[2,384,10368]{2,1,0:T(8,128)} %get-tuple-element.127, f32[2,384]{1,0:T(2,128)S(1)} %get-tuple-element.128, ...), kind=kOutput, calls=%fused_computation.12.clone.1 | convolution fusion | flops 2070478848 | bytes 37403140 | tf_op jit(solution)/shard_map/while/body/eval_jaxpr/aop,ape->aoe/dot_general | solution.py:34
  581.5 7.7 %gather_fusion.1 = bf16[54,384,128]{2,1,0:T(8,128)(2,1)} fusion(bf16[108,384,128]{2,1,0:T(8,128)(2,1)} %get-tuple-element.150, s32[1024]{0:T(1024)S(1)} %pad_clamp_fusion.2), kind=kCustom, calls=%fused_computation.clone.1 | custom fusion | bytes 10617048 | tf_op jit(solution)/shard_map/while/body/eval_jaxpr/gather | solution.py:98
  589.3 14.9 %fusion.47 = (f32[2,384]{1,0:T(2,128)S(1)}, f32[2,384,10368]{2,1,0:T(8,128)}) fusion(pred[2,10368]{1,0:T(4,128)(4,1)S(1)} %bitcast.87, bf16[2,10368,128]{2,1,0:T(8,128)(2,1)} %bitcast.77, bf16[3,2,384,128]{3,2,1,0:T(8,128)(2,1)} %get-tuple-element.148, s32[]{:T(128)} %get-tuple-element.137), kind=kOutput, calls=%fused_computation.4.clone.1 | convolution fusion | flops 2062318848 | bytes 37379840 | tf_op jit(solution)/shard_map/while/body/eval_jaxpr/jxg,jog->jxo/dot_general | solution.py:26
  604.2 14.3 %fusion.48 = f32[2,384]{1,0:T(2,128)S(1)} fusion(f32[2,384,10368]{2,1,0:T(8,128)} %get-tuple-element.127, f32[2,384]{1,0:T(2,128)S(1)} %get-tuple-element.128, pred[2,10368]{1,0:T(4,128)(4,1)S(1)} %bitcast.88), kind=kLoop, calls=%fused_computation.5.clone.1 | loop fusion | flops 31849728 | bytes 31877376 | tf_op jit(solution)/shard_map/while/body/eval_jaxpr/reduce_sum | solution.py:33
  618.5 7.7 %gather_fusion = bf16[54,384,128]{2,1,0:T(8,128)(2,1)} fusion(bf16[108,384,128]{2,1,0:T(8,128)(2,1)} %get-tuple-element.151, s32[1024]{0:T(1024)S(1)} %pad_clamp_fusion.2), kind=kCustom, calls=%fused_computation.1.clone.1 | custom fusion | bytes 10617048 | tf_op jit(solution)/shard_map/while/body/eval_jaxpr/gather | solution.py:98
  626.1 15.4 %fusion.49 = bf16[3,2,384,128]{3,2,1,0:T(8,128)(2,1)S(1)} fusion(bf16[3,2,384,128]{3,2,1,0:T(8,128)(2,1)S(1)} %get-tuple-element.138, s32[]{:T(128)} %get-tuple-element.137, bf16[2,10368,128]{2,1,0:T(8,128)(2,1)} %bitcast.78, f32[2,384,10368]{2,1,0:T(8,128)} %get-tuple-element.127, f32[2,384]{1,0:T(2,128)S(1)} %get-tuple-element.128, ...), kind=kOutput, calls=%fused_computation.12.clone.1 | convolution fusion | flops 2070478848 | bytes 37403140 | tf_op jit(solution)/shard_map/while/body/eval_jaxpr/aop,ape->aoe/dot_general | solution.py:34
  642.7 12.4 %all_to_all.35 = bf16[4,192,384]{2,1,0:T(8,128)(2,1)S(1)} all-to-all(bf16[4,192,384]{2,1,0:T(8,128)(2,1)S(1)} %all_to_all.28), channel_id=1, replica_groups=mesh['seq'=64,'head'=4] {'head'}, dimensions={0} | all-to-all | bytes 1179648 | tf_op jit(solution)/shard_map/all_to_all | solution.py:104
  (38 shorter events, 5.7 us)
Async XLA Ops:
  52.5 32.6 %collective-permute-start.1 = (bf16[2,3,2,384,128]{4,3,2,1,0:T(8,128)(2,1)}, bf16[2,3,2,384,128]{4,3,2,1,0:T(8,128)(2,1)}, u32[]{:S(2)}, u32[]{:S(2)}) collective-permute-start(bf16[2,3,2,384,128]{4,3,2,1,0:T(8,128)(2,1)} %copy.23), channel_id=1, source_target_pairs={{32,0},{36,4},{40,8},{44,12},{48,16},{52,20},{56,24},{60,28},{64,3... | collective-permute-start | bytes 3538952 | tf_op jit(solution)/shard_map/ppermute | solution.py:13
  57.3 53.1 %collective-permute-start = (bf16[2,3,2,384,128]{4,3,2,1,0:T(8,128)(2,1)}, bf16[2,3,2,384,128]{4,3,2,1,0:T(8,128)(2,1)}, u32[]{:S(2)}, u32[]{:S(2)}) collective-permute-start(bf16[2,3,2,384,128]{4,3,2,1,0:T(8,128)(2,1)} %copy.23), channel_id=1, source_target_pairs={{0,32},{4,36},{8,40},{12,44},{16,48},{20,52},{24,56},{28,60},{32,6... | collective-permute-start | bytes 3538952 | tf_op jit(solution)/shard_map/ppermute | solution.py:13
  112.7 86.7 %copy-start.1 = (bf16[2,3,2,384,128]{4,1,3,2,0:T(4,128)(2,1)}, bf16[2,3,2,384,128]{4,1,3,2,0:T(4,128)(2,1)S(1)}, u32[]{:S(2)}) copy-start(bf16[2,3,2,384,128]{4,1,3,2,0:T(4,128)(2,1)S(1)} %copy.49) | copy-start | bytes 3538948
  118.4 79.6 %collective-permute-start.2 = (bf16[2,3,3,384,128]{4,3,2,1,0:T(8,128)(2,1)S(1)}, bf16[2,3,3,384,128]{4,3,2,1,0:T(8,128)(2,1)S(1)}, u32[]{:S(2)}, u32[]{:S(2)}) collective-permute-start(bf16[2,3,3,384,128]{4,3,2,1,0:T(8,128)(2,1)S(1)} %copy.27), channel_id=1, source_target_pairs={{0,16},{4,20},{8,24},{12,28},{16,0},{20,4},{24,8},{28,12},{32,48},... | collective-permute-start | bytes 5308424 | tf_op jit(solution)/shard_map/ppermute | solution.py:19
  199.4 1.5 copy-start.2
  210.3 15.2 %copy-start.4 = (s32[3,2,27]{2,1,0:T(2,128)S(1)}, s32[3,2,27]{2,1,0:T(2,128)}, u32[]{:S(2)}) copy-start(s32[3,2,27]{2,1,0:T(2,128)} %param.5) | copy-start | bytes 1948
  218.8 155.1 %collective-permute-start.4 = (bf16[2,3,3,4,384,128]{5,4,3,2,1,0:T(8,128)(2,1)}, bf16[2,3,3,4,384,128]{5,4,3,2,1,0:T(8,128)(2,1)}, u32[]{:S(2)}, u32[]{:S(2)}) collective-permute-start(bf16[2,3,3,4,384,128]{5,4,3,2,1,0:T(8,128)(2,1)} %copy.29), channel_id=1, source_target_pairs={{4,0},{8,4},{12,8},{16,12},{20,16},{24,20},{28,24},{32,28},{36,32}... | collective-permute-start | bytes 21233672 | tf_op jit(solution)/shard_map/ppermute | solution.py:13
  220.7 163.5 %collective-permute-start.3 = (bf16[2,3,3,4,384,128]{5,4,3,2,1,0:T(8,128)(2,1)}, bf16[2,3,3,4,384,128]{5,4,3,2,1,0:T(8,128)(2,1)}, u32[]{:S(2)}, u32[]{:S(2)}) collective-permute-start(bf16[2,3,3,4,384,128]{5,4,3,2,1,0:T(8,128)(2,1)} %copy.29), channel_id=1, source_target_pairs={{0,4},{4,8},{8,12},{12,16},{16,20},{20,24},{24,28},{28,32},{32,36}... | collective-permute-start | bytes 21233672 | tf_op jit(solution)/shard_map/ppermute | solution.py:13
  442.3 13.1 %copy-start = (bf16[1,3,3,3,4,384,128]{6,1,5,4,0,3,2:T(4,128)(2,1)S(1)}, bf16[1,3,3,3,4,384,128]{6,1,5,4,0,3,2:T(4,128)(2,1)}, u32[]{:S(2)}) copy-start(bf16[1,3,3,3,4,384,128]{6,1,5,4,0,3,2:T(4,128)(2,1)} %get-tuple-element.80) | copy-start | bytes 31850500
  455.5 5.7 copy-start.3
where the time goes:
time: 658 us; the launch traced here: 656 us
  waiting for transfers between devices  253 us (38%)
  local copies, waits for them, and re-layouts  143 us (22%)
  other arithmetic  95.3 us (14%)
  matrix products  90.9 us (14%)
  blocking collectives  53 us (8%)
  starting transfers between devices  19.5 us (3%)
    ppermute x4, waiting for transfers between devices, from_behind(): return lax.ppermute(x, axis, pairs)  179 us
    ppermute x1, waiting for transfers between devices, swapped(): return lax.ppermute(value, axis, pairs)  74 us
    dot_general x3, matrix products, attend(): jnp.einsum('aop,ape->aoe', weights.astype(jnp.bfloat16), value_matrix_row...  46.3 us
    dot_general x3, matrix products, attend(): jnp.einsum('jxg,jog->jxo', query_rows, key_matrix_rows, preferred_element...  44.6 us
    reduce_sum x3, other arithmetic, attend(): row_total = jnp.sum(weights, axis=-1, keepdims=True)  42.8 us
    all_to_all x1, blocking collectives, local(): lax.all_to_all(qkv, 'head', split_axis=2, concat_axis=1, tiled=True)  40.6 us
    another operation x2, other arithmetic, local(): key_pool = jnp.stack([time_before, row_stack, time_after], axis=2)  37.7 us
    ppermute x4, local copies, waits for them, and re-layouts, from_behind(): return lax.ppermute(x, axis, pairs)  25.9 us
  transfers between devices with their start and end apart: 5, of which 4 were waited for; matrix products, arithmetic and copies ran while one was open for 5% of the time, Pallas kernels for 0%

commit v1 on v0

v1 whole, which is shorter than its diff:
```python
import functools
import math

import jax
import jax.numpy as jnp
from jax import lax
from jax.experimental import pallas as pl
from jax.experimental.pallas import tpu as pltpu
from jax.sharding import PartitionSpec as P

TIME_TILES = 4
ROWS_PER_BRICK = 2
AXES = ("seq", "head")
FAR = -1e30
VMEM_LIMIT = 40 * 2**20


def linear(y, xh, z, xl, core):
    return ((y * 2 + xh) * 8 + z) * 4 + xl * 2 + core


def devices():
    for y in range(4):
        for xh in range(2):
            for z in range(8):
                for xl in range(2):
                    for core in range(2):
                        yield y, xh, z, xl, core


def spread_pairs(k):
    pairs = []
    for y, xh, z, xl, core in devices():
        group = (2 * xl + core) ^ k
        pairs.append((linear(y, xh, z, xl, core), linear(y, group >> 1, z, group & 1, xh)))
    return pairs


def gather_pairs(k):
    return [(b, a) for a, b in spread_pairs(k)]


def edge_pairs(k):
    pairs = []
    for y, xh, z, xl, core in devices():
        if xl == 1 - z // 4:
            group = (2 * xl + core) ^ k
            pairs.append((linear(y, xh, z, xl, core), linear(y, group >> 1, z ^ 4, group & 1, xh)))
    return pairs


def core_pairs():
    return [(linear(y, xh, z, xl, c), linear(y, xh, z, xl, 1 - c)) for y, xh, z, xl, c in devices()]


def column_pairs():
    pairs = []
    for y, xh, z, xl, core in devices():
        to = y + (1 if core == 1 else -1)
        if 0 <= to < 4:
            pairs.append((linear(y, xh, z, xl, core), linear(to, xh, z, xl, 1 - core)))
    return pairs


def time_pairs(by):
    pairs = []
    for y, xh, z, xl, core in devices():
        if 0 <= z % TIME_TILES + by < TIME_TILES:
            pairs.append((linear(y, xh, z, xl, core), linear(y, xh, z + by, xl, core)))
    return pairs


def list_pairs(by):
    pairs = []
    for y, xh, z, xl, core in devices():
        if 0 <= z % TIME_TILES + by < TIME_TILES:
            pairs.append((linear(y, xh, z, xl, core), linear(y, xl, z + by, core, xh)))
    return pairs


def send(x, pairs):
    return lax.ppermute(x, AXES, pairs)


def split_kernel(at_ref, qkv_ref, *rest):
    outs, sems = rest[:8], rest[8]
    width = outs[0].shape[-1]
    copies = []
    for k in range(4):
        start = pl.multiple_of((at_ref[0] ^ k) * width, 128)
        copies.append(pltpu.make_async_copy(qkv_ref.at[0, :, pl.ds(start, width)], outs[k], sems.at[k]))
        copies.append(
            pltpu.make_async_copy(qkv_ref.at[pl.ds(1, 2), :, pl.ds(start, width)], outs[4 + k], sems.at[4 + k])
        )
    for copy in copies:
        copy.start()
    for copy in copies:
        copy.wait()


def split(at, qkv):
    _, rows, columns = qkv.shape
    width = columns // 4
    hbm = pl.BlockSpec(memory_space=pl.ANY)
    shapes = [jax.ShapeDtypeStruct((rows, width), qkv.dtype)] * 4
    shapes += [jax.ShapeDtypeStruct((2, rows, width), qkv.dtype)] * 4
    return pl.pallas_call(
        split_kernel,
        out_shape=shapes,
        in_specs=[pl.BlockSpec(memory_space=pltpu.SMEM), hbm],
        out_specs=[hbm] * 8,
        scratch_shapes=[pltpu.SemaphoreType.DMA((8,))],
        name="split",
    )(at, qkv)


def join_kernel(at_ref, *rest):
    parts, out_ref, sems = rest[:4], rest[4], rest[5]
    width = parts[0].shape[-1]
    copies = []
    for k in range(4):
        start = pl.multiple_of((at_ref[0] ^ k) * width, 128)
        copies.append(pltpu.make_async_copy(parts[k], out_ref.at[:, pl.ds(start, width)], sems.at[k]))
    for copy in copies:
        copy.start()
    for copy in copies:
        copy.wait()


def join(at, parts):
    rows, width = parts[0].shape
    hbm = pl.BlockSpec(memory_space=pl.ANY)
    return pl.pallas_call(
        join_kernel,
        out_shape=jax.ShapeDtypeStruct((rows, 4 * width), parts[0].dtype),
        in_specs=[pl.BlockSpec(memory_space=pltpu.SMEM)] + [hbm] * 4,
        out_specs=hbm,
        scratch_shapes=[pltpu.SemaphoreType.DMA((4,))],
        name="join",
    )(at, *parts)


def attend_kernel(mask_ref, *refs, sets, heads, tile, dim, sub):
    queries = refs[:sets]
    bodies = refs[sets : sets + 3]
    edges = refs[sets + 3 : sets + 6]
    outs = refs[sets + 6 : 2 * sets + 6]
    lses = refs[2 * sets + 6 : 3 * sets + 6]
    pool, held, max_ref, sum_ref, acc_ref, sems = refs[3 * sets + 6 :]
    copies = []
    for n in range(sets):
        copies.append(pltpu.make_async_copy(queries[n], held.at[n], sems.at[n]))
    for c in range(3):
        copies.append(pltpu.make_async_copy(bodies[c], pool.at[c, :, pl.ds(0, 2 * tile)], sems.at[sets + c]))
        copies.append(pltpu.make_async_copy(edges[c], pool.at[c, :, pl.ds(2 * tile, tile)], sems.at[sets + 3 + c]))
    for copy in copies:
        copy.start()
    for copy in copies:
        copy.wait()
    scale = dim**-0.5
    factor = scale * math.log2(math.e)
    for n in range(sets):
        lses[n][...] = jnp.zeros_like(lses[n])

        def per_head(h, carry, n=n):
            lanes = pl.ds(pl.multiple_of(h * dim, dim), dim)

            def per_tile(p, carry):
                max_ref[...] = jnp.full_like(max_ref, FAR)
                sum_ref[...] = jnp.zeros_like(sum_ref)
                acc_ref[...] = jnp.zeros_like(acc_ref)

                def per_key_tile(j, carry):
                    c = j // 3
                    start = pl.multiple_of((j - 3 * c) * tile, tile)

                    @pl.when(mask_ref[((n * heads + h) * 2 + p) * 9 + j] > 0)
                    def _():
                        keys = pool[c, 0, pl.ds(start, tile), lanes]
                        values = pool[c, 1, pl.ds(start, tile), lanes]
                        for b in range(tile // sub):
                            rows = pl.ds(b * sub, sub)
                            q = held[n, pl.ds(pl.multiple_of(p * tile + b * sub, sub), sub), lanes]
                            scores = lax.dot_general(
                                q, keys, (((1,), (1,)), ((), ())), preferred_element_type=jnp.float32
                            )
                            old = max_ref[rows, :]
                            new = jnp.maximum(old, jnp.max(scores, axis=1, keepdims=True))
                            shrink = jnp.exp2((old - new) * factor)
                            weights = jnp.exp2((scores - new[:, :1]) * factor)
                            total = sum_ref[rows, :] * shrink
                            for i in range(tile // dim):
                                total = total + weights[:, i * dim : (i + 1) * dim]
                            max_ref[rows, :] = new
                            sum_ref[rows, :] = total
                            acc_ref[rows, :] = acc_ref[rows, :] * shrink + lax.dot_general(
                                weights.astype(jnp.bfloat16),
                                values,
                                (((1,), (0,)), ((), ())),
                                preferred_element_type=jnp.float32,
                            )

                    return carry

                lax.fori_loop(0, 9, per_key_tile, 0)
                total = jnp.maximum(jnp.sum(sum_ref[...], axis=1, keepdims=True), 1e-30)
                at = pl.multiple_of(p * tile, tile)
                outs[n][pl.ds(at, tile), lanes] = (acc_ref[...] / total).astype(outs[n].dtype)
                lse = max_ref[...] * scale + jnp.log(total)
                lses[n][pl.ds(h, 1), pl.ds(at, tile)] = jnp.transpose(lse)[:1, :]
                return carry

            return lax.fori_loop(0, 2, per_tile, carry)

        lax.fori_loop(0, heads, per_head, 0)


def attend(mask, queries, bodies, edges, heads, out_dtype):
    sets = len(queries)
    brick, width = queries[0].shape
    tile = brick // 2
    dim = width // heads
    hbm = pl.BlockSpec(memory_space=pl.ANY)
    vmem = pl.BlockSpec(memory_space=pltpu.VMEM)
    outs = pl.pallas_call(
        functools.partial(attend_kernel, sets=sets, heads=heads, tile=tile, dim=dim, sub=tile // 3),
        out_shape=[jax.ShapeDtypeStruct((brick, width), out_dtype)] * sets
        + [jax.ShapeDtypeStruct((8, brick), jnp.float32)] * sets,
        in_specs=[pl.BlockSpec(memory_space=pltpu.SMEM)] + [hbm] * (sets + 6),
        out_specs=[vmem] * (2 * sets),
        scratch_shapes=[
            pltpu.VMEM((3, 2, 3 * tile, width), jnp.bfloat16),
            pltpu.VMEM((sets, brick, width), jnp.bfloat16),
            pltpu.VMEM((tile, dim), jnp.float32),
            pltpu.VMEM((tile, dim), jnp.float32),
            pltpu.VMEM((tile, dim), jnp.float32),
            pltpu.SemaphoreType.DMA((sets + 6,)),
        ],
        compiler_params=pltpu.CompilerParams(vmem_limit_bytes=VMEM_LIMIT),
        name=f"attend{sets}",
    )(mask, *queries, *bodies, *edges)
    return outs[:sets], outs[sets:]


def merge_kernel(valid_ref, own, before, after, own_lse, before_lse, after_lse, *outs, heads):
    brick, width = own.shape
    dim = width // heads
    quarter = brick // 4
    lse = [
        own_lse[...],
        jnp.where(valid_ref[0] > 0, before_lse[...], FAR),
        jnp.where(valid_ref[1] > 0, after_lse[...], FAR),
    ]
    top = jnp.maximum(jnp.maximum(lse[0], lse[1]), lse[2])
    shares = [jnp.exp(x - top) for x in lse]
    total = shares[0] + shares[1] + shares[2]
    shares = [x / total for x in shares]
    spare = jnp.zeros((128 - 24, brick), jnp.float32)
    columns = jnp.transpose(jnp.concatenate(shares + [spare], axis=0))
    for k in range(4):
        rows = slice(k * quarter, (k + 1) * quarter)
        for h in range(heads):
            lanes = slice(h * dim, (h + 1) * dim)
            merged = own[rows, lanes].astype(jnp.float32) * columns[rows, h : h + 1]
            merged += before[rows, lanes].astype(jnp.float32) * columns[rows, 8 + h : 9 + h]
            merged += after[rows, lanes].astype(jnp.float32) * columns[rows, 16 + h : 17 + h]
            outs[k][:, lanes] = merged.astype(outs[k].dtype)


def merge(valid, parts, lses, heads):
    brick, width = parts[0].shape
    vmem = pl.BlockSpec(memory_space=pltpu.VMEM)
    return pl.pallas_call(
        functools.partial(merge_kernel, heads=heads),
        out_shape=[jax.ShapeDtypeStruct((brick // 4, width), jnp.bfloat16)] * 4,
        in_specs=[pl.BlockSpec(memory_space=pltpu.SMEM)] + [vmem] * 6,
        out_specs=[vmem] * 4,
        compiler_params=pltpu.CompilerParams(vmem_limit_bytes=VMEM_LIMIT),
        name="merge",
    )(valid, *parts, *lses)


def named(key_tiles, y, xh, z, xl):
    pair = z // TIME_TILES
    time = z % TIME_TILES
    column = 2 * y + xh
    tile_time = key_tiles // 2 % TIME_TILES
    tile_pair = key_tiles // (2 * TIME_TILES) % 2
    tile_column = key_tiles // (4 * TIME_TILES)
    beside = jnp.where(tile_column == column + 1 - 2 * xh, 1, 2)
    column_slot = jnp.where(tile_column == column, 0, beside)
    row_slot = jnp.where(tile_pair == pair, (key_tiles % 2) ^ xl, 2)
    slot = (tile_time - time + 1) * 9 + column_slot * 3 + row_slot
    slot = jnp.where(key_tiles >= 0, slot, -1)
    mask = jnp.any(slot[..., None] == jnp.arange(27, dtype=jnp.int32), axis=2)
    mask = jnp.where(xl == 1, mask[:, ::-1], mask).astype(jnp.int32)
    return mask[..., 0:9], mask[..., 9:18], mask[..., 18:27]


def local(qkv, key_tiles):
    heads = key_tiles.shape[0]
    seq = lax.axis_index("seq")
    head = lax.axis_index("head")
    y, xh, z = seq // 16, seq // 8 % 2, seq % 8
    xl = head // 2
    pair, time = z // TIME_TILES, z % TIME_TILES
    at = head.astype(jnp.int32).reshape(1)

    early, same, late = named(key_tiles, y, xh, z, xl)
    mask_own = send(same, list_pairs(0))
    mask_next = send(early, list_pairs(-1))
    mask_prev = send(late, list_pairs(1))

    pieces = split(at, qkv)
    q_parts = [send(pieces[k], spread_pairs(k)) for k in range(4)]
    kv_parts = [send(pieces[4 + k], spread_pairs(k)) for k in range(4)]
    edge_parts = [send(pieces[4 + k], edge_pairs(k)) for k in range(4)]

    q_own = jnp.concatenate(q_parts, axis=0)
    q_prev = send(q_own, time_pairs(1))
    q_next = send(q_own, time_pairs(-1))

    kv_own = jnp.concatenate(kv_parts, axis=1)
    kv_core = send(kv_own, core_pairs())
    kv_column = send(kv_own, column_pairs())
    low = (pair ^ xh) == 0
    edge_own = jnp.concatenate(
        [jnp.where(low, edge_parts[0], edge_parts[2]), jnp.where(low, edge_parts[1], edge_parts[3])], axis=1
    )
    edge_core = send(edge_own, core_pairs())
    edge_column = send(edge_own, column_pairs())

    bodies = (kv_own, kv_core, kv_column)
    edges = (edge_own, edge_core, edge_column)
    mask_away = jnp.concatenate([mask_prev.reshape(-1), mask_next.reshape(-1)])
    (o_prev, o_next), (l_prev, l_next) = attend(mask_away, (q_prev, q_next), bodies, edges, heads, jnp.bfloat16)
    o_before = send(o_next, time_pairs(1))
    l_before = send(l_next, time_pairs(1))
    o_after = send(o_prev, time_pairs(-1))
    l_after = send(l_prev, time_pairs(-1))
    (o_own,), (l_own,) = attend(mask_own.reshape(-1), (q_own,), bodies, edges, heads, jnp.float32)

    valid = jnp.stack([time > 0, time < TIME_TILES - 1]).astype(jnp.int32)
    chunks = merge(valid, (o_own, o_before, o_after), (l_own, l_before, l_after), heads)
    home = [send(chunks[k], gather_pairs(k)) for k in range(4)]
    return join(at, home)


def solution(mesh):
    placed = (P(None, ("seq", "head"), None), P("head", "seq", None))
    return jax.shard_map(
        local, mesh=mesh, in_specs=placed, out_specs=P(("seq", "head"), None), check_vma=False
    )
```

time: 658 us -> 305 us (0.46)
  the two profiles are of different devices: /device:TPU:8 before, /device:TPU:41 now
where the time goes in v1:
time: 305 us; the launch traced here: 300 us
  Pallas kernels  128 us (42%)
  starting transfers between devices  113 us (37%)
  waiting for transfers between devices  50.3 us (16%)
  local copies, waits for them, and re-layouts  7.02 us (2%)
    ppermute x29, starting transfers between devices, send(): return lax.ppermute(x, AXES, pairs)  113 us
    pallas_call x1, Pallas kernels, split(): pl.pallas_call(split_kernel, out_shape=shapes, in_specs=[pl.BlockSpec(mem...  54.8 us
    pallas_call x2, Pallas kernels, attend(): pl.pallas_call(functools.partial(attend_kernel, sets=sets, heads=heads, t...  51.8 us
    ppermute x29, waiting for transfers between devices, send(): return lax.ppermute(x, AXES, pairs)  50.3 us
    pallas_call x1, Pallas kernels, join(): pl.pallas_call(join_kernel, out_shape=jax.ShapeDtypeStruct((rows, 4 * wid...  19 us
  transfers between devices with their start and end apart: 29, of which 12 were waited for; matrix products, arithmetic and copies ran while one was open for 1% of the time, Pallas kernels for 11%

profile of v1, /device:TPU:41, one launch (start us, length us, event | category | flops | bytes accessed | tf_op | source)
XLA Modules:
  0.0 299.7 jit_solution(15205097838945517509)
XLA Ops:
  0.0 54.8 %split.1 = (bf16[192,384]{1,0:T(8,128)(2,1)}, bf16[192,384]{1,0:T(8,128)(2,1)}, bf16[192,384]{1,0:T(8,128)(2,1)}, bf16[192,384]{1,0:T(8,128)(2,1)}, bf16[2,192,3...) custom-call(s32[1]{0:T(128)} %bitcast.at_ref, ...), custom_call_target="tpu_custom_call" | custom-call | tf_op jit(solution)/shard_map/split/pallas_call | solution.py:107
  54.8 1.4 collective-permute-start.13
  56.2 0.8 collective-permute-start.6
  57.0 11.5 %collective-permute-start.5 = (bf16[2,192,384]{2,1,0:T(8,128)(2,1)}, bf16[2,192,384]{2,1,0:T(8,128)(2,1)S(1)}, u32[]{:S(2)}, u32[]{:S(2)}) collective-permute-start(bf16[2,192,384]{2,1,0:T(8,128)(2,1)} %get-tuple-element.27), channel_id=1, source_target_pairs={{0,0},{1,2},{2,32},{3,34},{4,4},{5,6},{6,36},{7,38},{8,8},{9,10},{... | collective-permute-start | bytes 884744 | tf_op jit(solution)/shard_map/ppermute | solution.py:82
  68.5 3.0 collective-permute-start.1
  72.0 8.0 %collective-permute-done.1 = bf16[192,384]{1,0:T(8,128)(2,1)S(1)} collective-permute-done((bf16[192,384]{1,0:T(8,128)(2,1)}, bf16[192,384]{1,0:T(8,128)(2,1)S(1)}, u32[]{:S(2)}, u32[]{:S(2)}) %collective-permute-start.1) | collective-permute-done | bytes 147488 | tf_op jit(solution)/shard_map/ppermute | solution.py:82
  80.5 0.7 constant_dynamic-update-slice_fusion.3
  81.1 2.7 collective-permute-start.4
  83.8 0.7 constant_dynamic-update-slice_fusion.2
  84.5 1.5 collective-permute-done.3
  86.0 0.7 collective-permute-start.14
  86.6 0.7 constant_dynamic-update-slice_fusion.1
  87.3 1.5 collective-permute-done.4
  88.8 3.2 %collective-permute-start.7 = (bf16[2,192,384]{2,1,0:T(8,128)(2,1)}, bf16[2,192,384]{2,1,0:T(8,128)(2,1)S(1)}, u32[]{:S(2)}, u32[]{:S(2)}) collective-permute-start(bf16[2,192,384]{2,1,0:T(8,128)(2,1)} %get-tuple-element.29), channel_id=1, source_target_pairs={{0,32},{1,34},{2,0},{3,2},{4,36},{5,38},{6,4},{7,6},{8,40},{9,42},... | collective-permute-start | bytes 884744 | tf_op jit(solution)/shard_map/ppermute | solution.py:82
  92.1 0.7 constant_dynamic-update-slice_fusion.refs_0_
  92.7 1.9 collective-permute-start.8
  94.7 1.3 collective-permute-start.11
  96.7 0.7 collective-permute-start.12
  97.4 4.2 %collective-permute-done.8 = bf16[2,192,384]{2,1,0:T(8,128)(2,1)S(1)} collective-permute-done((bf16[2,192,384]{2,1,0:T(8,128)(2,1)}, bf16[2,192,384]{2,1,0:T(8,128)(2,1)S(1)}, u32[]{:S(2)}, u32[]{:S(2)}) %collective-permute-start.8) | collective-permute-done | bytes 294944 | tf_op jit(solution)/shard_map/ppermute | solution.py:82
  101.6 3.3 %collective-permute-start.19 = (bf16[768,384]{1,0:T(8,128)(2,1)}, bf16[768,384]{1,0:T(8,128)(2,1)S(1)}, u32[]{:S(2)}, u32[]{:S(2)}) collective-permute-start(bf16[768,384]{1,0:T(8,128)(2,1)} %constant_dynamic-update-slice_fusion.refs_0_), channel_id=1, source_target_pairs={{0,4},{1,5},{2,6},{3,7},{4,8},{5,9},{6,10},{7,11},{8,12},{9,13},{1... | collective-permute-start | bytes 1769480 | tf_op jit(solution)/shard_map/ppermute | solution.py:82
  104.9 1.9 collective-permute-start.10
  107.6 17.0 %collective-permute-done.11 = bf16[2,192,384]{2,1,0:T(8,128)(2,1)S(1)} collective-permute-done((bf16[2,192,384]{2,1,0:T(8,128)(2,1)S(1)}, bf16[2,192,384]{2,1,0:T(8,128)(2,1)S(1)}, u32[]{:S(2)}, u32[]{:S(2)}) %collective-permute-start.11) | collective-permute-done | bytes 294944 | tf_op jit(solution)/shard_map/ppermute | solution.py:82
  124.6 7.9 %collective-permute-start.17 = (s32[3,2,9]{2,1,0:T(2,128)S(1)}, s32[3,2,9]{2,1,0:T(2,128)S(1)}, u32[]{:S(2)}, u32[]{:S(2)}) collective-permute-start(s32[3,2,9]{2,1,0:T(2,128)S(1)} %get-tuple-element.41), channel_id=1, source_target_pairs={{0,4},{1,6},{2,36},{3,38},{4,8},{5,10},{6,40},{7,42},{8,12},{9,14}... | collective-permute-start | bytes 656 | tf_op jit(solution)/shard_map/ppermute | solution.py:82
  132.4 1.9 collective-permute-start.18
  134.5 1.3 collective-permute-done.17
  135.8 3.3 %collective-permute-start.20 = (bf16[768,384]{1,0:T(8,128)(2,1)}, bf16[768,384]{1,0:T(8,128)(2,1)}, u32[]{:S(2)}, u32[]{:S(2)}) collective-permute-start(bf16[768,384]{1,0:T(8,128)(2,1)} %constant_dynamic-update-slice_fusion.refs_0_), channel_id=1, source_target_pairs={{4,0},{5,1},{6,2},{7,3},{8,4},{9,5},{10,6},{11,7},{12,8},{13,9},{1... | collective-permute-start | bytes 1769480 | tf_op jit(solution)/shard_map/ppermute | solution.py:82
  139.1 2.6 collective-permute-done.18
  141.7 0.8 copy-done
  142.6 3.6 %collective-permute-start.16 = (bf16[2,384,384]{2,1,0:T(8,128)(2,1)S(1)}, bf16[2,384,384]{2,1,0:T(8,128)(2,1)}, u32[]{:S(2)}, u32[]{:S(2)}) collective-permute-start(bf16[2,384,384]{2,1,0:T(8,128)(2,1)S(1)} %pad_maximum_fusion.refs_4_.refs_5_), channel_id=1, source_target_pairs={{1,64},{3,66},{5,68},{7,70},{9,72},{11,74},{13,76},{15,78},{17,80}... | collective-permute-start | bytes 1769480 | tf_op jit(solution)/shard_map/ppermute | solution.py:82
  146.4 4.8 %collective-permute-done.20.refs_1_ = bf16[768,384]{1,0:T(8,128)(2,1)} collective-permute-done((bf16[768,384]{1,0:T(8,128)(2,1)}, bf16[768,384]{1,0:T(8,128)(2,1)}, u32[]{:S(2)}, u32[]{:S(2)}) %collective-permute-start.20) | collective-permute-done | bytes 589856 | tf_op jit(solution)/shard_map/ppermute | solution.py:82
  151.2 2.7 collective-permute-done.16.refs_6_.refs_7_
  154.0 1.1 copy-done.1
  155.0 19.2 %attend2.1 = (bf16[768,384]{1,0:T(8,128)(2,1)}, bf16[768,384]{1,0:T(8,128)(2,1)}, f32[8,768]{1,0:T(8,128)S(1)}, f32[8,768]{1,0:T(8,128)S(1)}) custom-call(s32[108]{0:T(128)S(1)} %pad_add_fusion.mask_ref, bf16[768,384]{1,0:T(8,128)(2,1)S(1)} %copy-done.1, bf16[768,384]{1,0:T(8,128)(2,1)} %collective-permute-done.20.refs_1_, ...), custom_call_target="tpu_custom_call" | custom-call | tf_op jit(solution)/shard_map/attend2/pallas_call | solution.py:225
  175.5 2.2 collective-permute-start.21
  177.7 3.9 %collective-permute-start.22 = (bf16[768,384]{1,0:T(8,128)(2,1)}, bf16[768,384]{1,0:T(8,128)(2,1)}, u32[]{:S(2)}, u32[]{:S(2)}) collective-permute-start(bf16[768,384]{1,0:T(8,128)(2,1)} %get-tuple-element.33), channel_id=1, source_target_pairs={{4,0},{5,1},{6,2},{7,3},{8,4},{9,5},{10,6},{11,7},{12,8},{13,9},{1... | collective-permute-start | bytes 1769480 | tf_op jit(solution)/shard_map/ppermute | solution.py:82
  181.5 27.7 %collective-permute-start = (s32[3,2,9]{2,1,0:T(2,128)S(1)}, s32[3,2,9]{2,1,0:T(2,128)S(1)}, u32[]{:S(2)}, u32[]{:S(2)}) collective-permute-start(s32[3,2,9]{2,1,0:T(2,128)S(1)} %get-tuple-element.43), channel_id=1, source_target_pairs={{0,0},{1,2},{2,32},{3,34},{4,4},{5,6},{6,36},{7,38},{8,8},{9,10},{... | collective-permute-start | bytes 656 | tf_op jit(solution)/shard_map/ppermute | solution.py:82
  209.3 2.6 collective-permute-start.23
  211.9 3.3 %collective-permute-start.24 = (f32[8,768]{1,0:T(8,128)}, f32[8,768]{1,0:T(8,128)}, u32[]{:S(2)}, u32[]{:S(2)}) collective-permute-start(f32[8,768]{1,0:T(8,128)} %copy-done.2), channel_id=1, source_target_pairs={{4,0},{5,1},{6,2},{7,3},{8,4},{9,5},{10,6},{11,7},{12,8},{13,9},{1... | collective-permute-start | bytes 73736 | tf_op jit(solution)/shard_map/ppermute | solution.py:82
  215.3 32.6 %attend1.1 = (f32[768,384]{1,0:T(8,128)S(1)}, f32[8,768]{1,0:T(8,128)S(1)}) custom-call(s32[54]{0:T(128)S(1)} %reshape.14.mask_ref, bf16[768,384]{1,0:T(8,128)(2,1)} %constant_dynamic-update-slice_fusion.refs_0_, bf16[2,768,384]{2,1,0:T(8,128)(2,1)S(1)} %constant_dynamic-update-slice_fusion.4.refs_1_.refs_2_, ...), custom_call_target="tpu_custom_call" | custom-call | tf_op jit(solution)/shard_map/attend1/pallas_call | solution.py:225
  248.0 2.5 merge.1
  250.4 1.9 collective-permute-start.25
  252.4 13.6 %collective-permute-start.26 = (bf16[192,384]{1,0:T(8,128)(2,1)S(1)}, bf16[192,384]{1,0:T(8,128)(2,1)S(1)}, u32[]{:S(2)}, u32[]{:S(2)}) collective-permute-start(bf16[192,384]{1,0:T(8,128)(2,1)S(1)} %get-tuple-element.38), channel_id=1, source_target_pairs={{2,0},{0,1},{34,2},{32,3},{6,4},{4,5},{38,6},{36,7},{10,8},{8,9},{... | collective-permute-start | bytes 442376 | tf_op jit(solution)/shard_map/ppermute | solution.py:82
  266.0 6.1 %collective-permute-start.27 = (bf16[192,384]{1,0:T(8,128)(2,1)S(1)}, bf16[192,384]{1,0:T(8,128)(2,1)S(1)}, u32[]{:S(2)}, u32[]{:S(2)}) collective-permute-start(bf16[192,384]{1,0:T(8,128)(2,1)S(1)} %get-tuple-element.39), channel_id=1, source_target_pairs={{32,0},{34,1},{0,2},{2,3},{36,4},{38,5},{4,6},{6,7},{40,8},{42,9},... | collective-permute-start | bytes 442376 | tf_op jit(solution)/shard_map/ppermute | solution.py:82
  272.0 1.9 collective-permute-start.28
  274.0 3.3 %collective-permute-done.27.rest_2_ = bf16[192,384]{1,0:T(8,128)(2,1)S(1)} collective-permute-done((bf16[192,384]{1,0:T(8,128)(2,1)S(1)}, bf16[192,384]{1,0:T(8,128)(2,1)S(1)}, u32[]{:S(2)}, u32[]{:S(2)}) %collective-permute-start.27) | collective-permute-done | bytes 147488 | tf_op jit(solution)/shard_map/ppermute | solution.py:82
  277.3 2.7 collective-permute-done.28.rest_3_
  280.0 0.6 copy-done.7
  280.7 19.0 %join.1 = bf16[192,1536]{1,0:T(8,128)(2,1)} custom-call(s32[1]{0:T(128)} %bitcast.at_ref, bf16[192,384]{1,0:T(8,128)(2,1)} %copy-done.4, bf16[192,384]{1,0:T(8,128)(2,1)} %copy-done.5, bf16[192,384]{1,0:T(8,128)(2,1)} %copy-done.6, bf16[192,384]{1,0:T(8,128)(2,1)} %copy-done.7), custom_call_target="tpu_custom_call" | custom-call | tf_op jit(solution)/shard_map/join/pallas_call | solution.py:133
  (58 shorter events, 4.1 us)
Async XLA Ops:
  0.0 71.7 %copy-start.8 = (s32[3,2,27]{2,1,0:T(2,128)S(1)}, s32[3,2,27]{2,1,0:T(2,128)}, u32[]{:S(2)}) copy-start(s32[3,2,27]{2,1,0:T(2,128)} %param.3) | copy-start | bytes 1948
  54.8 39.9 %copy-start.10 = (bf16[2,192,384]{2,1,0:T(8,128)(2,1)S(1)}, bf16[2,192,384]{2,1,0:T(8,128)(2,1)}, u32[]{:S(2)}) copy-start(bf16[2,192,384]{2,1,0:T(8,128)(2,1)} %get-tuple-element.27) | copy-start | bytes 884740
  54.8 50.1 %collective-permute-start.13 = (bf16[2,192,384]{2,1,0:T(8,128)(2,1)}, bf16[2,192,384]{2,1,0:T(8,128)(2,1)S(1)}, u32[]{:S(2)}, u32[]{:S(2)}) collective-permute-start(bf16[2,192,384]{2,1,0:T(8,128)(2,1)} %get-tuple-element.28), channel_id=1, source_target_pairs={{2,50},{3,48},{6,54},{7,52},{10,58},{11,56},{14,62},{15,60},{16,2}... | collective-permute-start | bytes 884744 | tf_op jit(solution)/shard_map/ppermute | solution.py:82
  56.2 38.5 %collective-permute-start.6 = (bf16[2,192,384]{2,1,0:T(8,128)(2,1)}, bf16[2,192,384]{2,1,0:T(8,128)(2,1)S(1)}, u32[]{:S(2)}, u32[]{:S(2)}) collective-permute-start(bf16[2,192,384]{2,1,0:T(8,128)(2,1)} %get-tuple-element.28), channel_id=1, source_target_pairs={{0,2},{1,0},{2,34},{3,32},{4,6},{5,4},{6,38},{7,36},{8,10},{9,8},{... | collective-permute-start | bytes 884744 | tf_op jit(solution)/shard_map/ppermute | solution.py:82
  57.0 35.7 %collective-permute-start.5 = (bf16[2,192,384]{2,1,0:T(8,128)(2,1)}, bf16[2,192,384]{2,1,0:T(8,128)(2,1)S(1)}, u32[]{:S(2)}, u32[]{:S(2)}) collective-permute-start(bf16[2,192,384]{2,1,0:T(8,128)(2,1)} %get-tuple-element.27), channel_id=1, source_target_pairs={{0,0},{1,2},{2,32},{3,34},{4,4},{5,6},{6,36},{7,38},{8,8},{9,10},{... | collective-permute-start | bytes 884744 | tf_op jit(solution)/shard_map/ppermute | solution.py:82
  68.5 11.5 %collective-permute-start.1 = (bf16[192,384]{1,0:T(8,128)(2,1)}, bf16[192,384]{1,0:T(8,128)(2,1)S(1)}, u32[]{:S(2)}, u32[]{:S(2)}) collective-permute-start(bf16[192,384]{1,0:T(8,128)(2,1)} %get-tuple-element.23), channel_id=1, source_target_pairs={{0,0},{1,2},{2,32},{3,34},{4,4},{5,6},{6,36},{7,38},{8,8},{9,10},{... | collective-permute-start | bytes 442376 | tf_op jit(solution)/shard_map/ppermute | solution.py:82
  71.5 9.7 %collective-permute-start.2 = (bf16[192,384]{1,0:T(8,128)(2,1)}, bf16[192,384]{1,0:T(8,128)(2,1)S(1)}, u32[]{:S(2)}, u32[]{:S(2)}) collective-permute-start(bf16[192,384]{1,0:T(8,128)(2,1)} %get-tuple-element.24), channel_id=1, source_target_pairs={{0,2},{1,0},{2,34},{3,32},{4,6},{5,4},{6,38},{7,36},{8,10},{9,8},{... | collective-permute-start | bytes 442376 | tf_op jit(solution)/shard_map/ppermute | solution.py:82
  80.0 16.7 %copy-start.9 = (bf16[2,192,384]{2,1,0:T(8,128)(2,1)S(1)}, bf16[2,192,384]{2,1,0:T(8,128)(2,1)}, u32[]{:S(2)}) copy-start(bf16[2,192,384]{2,1,0:T(8,128)(2,1)} %get-tuple-element.29) | copy-start | bytes 884740
  80.0 6.0 %collective-permute-start.3 = (bf16[192,384]{1,0:T(8,128)(2,1)}, bf16[192,384]{1,0:T(8,128)(2,1)S(1)}, u32[]{:S(2)}, u32[]{:S(2)}) collective-permute-start(bf16[192,384]{1,0:T(8,128)(2,1)} %get-tuple-element.25), channel_id=1, source_target_pairs={{0,32},{1,34},{2,0},{3,2},{4,36},{5,38},{6,4},{7,6},{8,40},{9,42},... | collective-permute-start | bytes 442376 | tf_op jit(solution)/shard_map/ppermute | solution.py:82
  81.1 7.7 %collective-permute-start.4 = (bf16[192,384]{1,0:T(8,128)(2,1)}, bf16[192,384]{1,0:T(8,128)(2,1)S(1)}, u32[]{:S(2)}, u32[]{:S(2)}) collective-permute-start(bf16[192,384]{1,0:T(8,128)(2,1)} %get-tuple-element.26), channel_id=1, source_target_pairs={{0,34},{1,32},{2,2},{3,0},{4,38},{5,36},{6,6},{7,4},{8,42},{9,40},... | collective-permute-start | bytes 442376 | tf_op jit(solution)/shard_map/ppermute | solution.py:82
  86.0 20.9 %collective-permute-start.14 = (bf16[2,192,384]{2,1,0:T(8,128)(2,1)}, bf16[2,192,384]{2,1,0:T(8,128)(2,1)S(1)}, u32[]{:S(2)}, u32[]{:S(2)}) collective-permute-start(bf16[2,192,384]{2,1,0:T(8,128)(2,1)} %get-tuple-element.30), channel_id=1, source_target_pairs={{2,18},{3,16},{6,22},{7,20},{10,26},{11,24},{14,30},{15,28},{16,34... | collective-permute-start | bytes 884744 | tf_op jit(solution)/shard_map/ppermute | solution.py:82
  88.8 7.8 %collective-permute-start.7 = (bf16[2,192,384]{2,1,0:T(8,128)(2,1)}, bf16[2,192,384]{2,1,0:T(8,128)(2,1)S(1)}, u32[]{:S(2)}, u32[]{:S(2)}) collective-permute-start(bf16[2,192,384]{2,1,0:T(8,128)(2,1)} %get-tuple-element.29), channel_id=1, source_target_pairs={{0,32},{1,34},{2,0},{3,2},{4,36},{5,38},{6,4},{7,6},{8,40},{9,42},... | collective-permute-start | bytes 884744 | tf_op jit(solution)/shard_map/ppermute | solution.py:82
  92.7 8.9 %collective-permute-start.8 = (bf16[2,192,384]{2,1,0:T(8,128)(2,1)}, bf16[2,192,384]{2,1,0:T(8,128)(2,1)S(1)}, u32[]{:S(2)}, u32[]{:S(2)}) collective-permute-start(bf16[2,192,384]{2,1,0:T(8,128)(2,1)} %get-tuple-element.30), channel_id=1, source_target_pairs={{0,34},{1,32},{2,2},{3,0},{4,38},{5,36},{6,6},{7,4},{8,42},{9,40},... | collective-permute-start | bytes 884744 | tf_op jit(solution)/shard_map/ppermute | solution.py:82
  94.7 29.8 %collective-permute-start.11 = (bf16[2,192,384]{2,1,0:T(8,128)(2,1)S(1)}, bf16[2,192,384]{2,1,0:T(8,128)(2,1)S(1)}, u32[]{:S(2)}, u32[]{:S(2)}) collective-permute-start(bf16[2,192,384]{2,1,0:T(8,128)(2,1)S(1)} %copy-done.10), channel_id=1, source_target_pairs={{2,48},{3,50},{6,52},{7,54},{10,56},{11,58},{14,60},{15,62},{16,0}... | collective-permute-start | bytes 884744 | tf_op jit(solution)/shard_map/ppermute | solution.py:82
  96.7 35.8 %collective-permute-start.12 = (bf16[2,192,384]{2,1,0:T(8,128)(2,1)S(1)}, bf16[2,192,384]{2,1,0:T(8,128)(2,1)S(1)}, u32[]{:S(2)}, u32[]{:S(2)}) collective-permute-start(bf16[2,192,384]{2,1,0:T(8,128)(2,1)S(1)} %copy-done.9), channel_id=1, source_target_pairs={{2,16},{3,18},{6,20},{7,22},{10,24},{11,26},{14,28},{15,30},{16,32... | collective-permute-start | bytes 884744 | tf_op jit(solution)/shard_map/ppermute | solution.py:82
  101.6 40.1 %collective-permute-start.19 = (bf16[768,384]{1,0:T(8,128)(2,1)}, bf16[768,384]{1,0:T(8,128)(2,1)S(1)}, u32[]{:S(2)}, u32[]{:S(2)}) collective-permute-start(bf16[768,384]{1,0:T(8,128)(2,1)} %constant_dynamic-update-slice_fusion.refs_0_), channel_id=1, source_target_pairs={{0,4},{1,5},{2,6},{3,7},{4,8},{5,9},{6,10},{7,11},{8,12},{9,13},{1... | collective-permute-start | bytes 1769480 | tf_op jit(solution)/shard_map/ppermute | solution.py:82
  104.9 49.0 %collective-permute-start.10 = (bf16[2,768,384]{2,1,0:T(8,128)(2,1)S(1)}, bf16[2,768,384]{2,1,0:T(8,128)(2,1)S(1)}, u32[]{:S(2)}, u32[]{:S(2)}) collective-permute-start(bf16[2,768,384]{2,1,0:T(8,128)(2,1)S(1)} %constant_dynamic-update-slice_fusion.4.refs_1_.refs_2_), channel_id=1, source_target_pairs={{1,64},{3,66},{5,68},{7,70},{9,72},{11,74},{13,76},{15,78},{17,80}... | collective-permute-start | bytes 3538952 | tf_op jit(solution)/shard_map/ppermute | solution.py:82
  106.9 47.1 %collective-permute-start.9 = (bf16[2,768,384]{2,1,0:T(8,128)(2,1)S(1)}, bf16[2,768,384]{2,1,0:T(8,128)(2,1)}, u32[]{:S(2)}, u32[]{:S(2)}) collective-permute-start(bf16[2,768,384]{2,1,0:T(8,128)(2,1)S(1)} %constant_dynamic-update-slice_fusion.4.refs_1_.refs_2_), channel_id=1, source_target_pairs={{0,1},{1,0},{2,3},{3,2},{4,5},{5,4},{6,7},{7,6},{8,9},{9,8},{10,11... | collective-permute-start | bytes 3538952 | tf_op jit(solution)/shard_map/ppermute | solution.py:82
  124.6 11.3 %collective-permute-start.17 = (s32[3,2,9]{2,1,0:T(2,128)S(1)}, s32[3,2,9]{2,1,0:T(2,128)S(1)}, u32[]{:S(2)}, u32[]{:S(2)}) collective-permute-start(s32[3,2,9]{2,1,0:T(2,128)S(1)} %get-tuple-element.41), channel_id=1, source_target_pairs={{0,4},{1,6},{2,36},{3,38},{4,8},{5,10},{6,40},{7,42},{8,12},{9,14}... | collective-permute-start | bytes 656 | tf_op jit(solution)/shard_map/ppermute | solution.py:82
  132.4 9.3 %collective-permute-start.18 = (s32[3,2,9]{2,1,0:T(2,128)S(1)}, s32[3,2,9]{2,1,0:T(2,128)S(1)}, u32[]{:S(2)}, u32[]{:S(2)}) collective-permute-start(s32[3,2,9]{2,1,0:T(2,128)S(1)} %get-tuple-element.42), channel_id=1, source_target_pairs={{4,0},{5,2},{6,32},{7,34},{8,4},{9,6},{10,36},{11,38},{12,8},{13,1... | collective-permute-start | bytes 656 | tf_op jit(solution)/shard_map/ppermute | solution.py:82
  135.8 15.4 %collective-permute-start.20 = (bf16[768,384]{1,0:T(8,128)(2,1)}, bf16[768,384]{1,0:T(8,128)(2,1)}, u32[]{:S(2)}, u32[]{:S(2)}) collective-permute-start(bf16[768,384]{1,0:T(8,128)(2,1)} %constant_dynamic-update-slice_fusion.refs_0_), channel_id=1, source_target_pairs={{4,0},{5,1},{6,2},{7,3},{8,4},{9,5},{10,6},{11,7},{12,8},{13,9},{1... | collective-permute-start | bytes 1769480 | tf_op jit(solution)/shard_map/ppermute | solution.py:82
  141.7 9.5 %collective-permute-start.15 = (bf16[2,384,384]{2,1,0:T(8,128)(2,1)S(1)}, bf16[2,384,384]{2,1,0:T(8,128)(2,1)S(1)}, u32[]{:S(2)}, u32[]{:S(2)}) collective-permute-start(bf16[2,384,384]{2,1,0:T(8,128)(2,1)S(1)} %pad_maximum_fusion.refs_4_.refs_5_), channel_id=1, source_target_pairs={{0,1},{1,0},{2,3},{3,2},{4,5},{5,4},{6,7},{7,6},{8,9},{9,8},{10,11... | collective-permute-start | bytes 1769480 | tf_op jit(solution)/shard_map/ppermute | solution.py:82
  141.7 0.8 copy-start
  142.6 11.4 %collective-permute-start.16 = (bf16[2,384,384]{2,1,0:T(8,128)(2,1)S(1)}, bf16[2,384,384]{2,1,0:T(8,128)(2,1)}, u32[]{:S(2)}, u32[]{:S(2)}) collective-permute-start(bf16[2,384,384]{2,1,0:T(8,128)(2,1)S(1)} %pad_maximum_fusion.refs_4_.refs_5_), channel_id=1, source_target_pairs={{1,64},{3,66},{5,68},{7,70},{9,72},{11,74},{13,76},{15,78},{17,80}... | collective-permute-start | bytes 1769480 | tf_op jit(solution)/shard_map/ppermute | solution.py:82
  154.0 1.1 copy-start.1
  174.2 0.6 copy-start.2
  174.9 0.6 copy-start.3
  175.5 72.5 %collective-permute-start.21 = (bf16[768,384]{1,0:T(8,128)(2,1)}, bf16[768,384]{1,0:T(8,128)(2,1)}, u32[]{:S(2)}, u32[]{:S(2)}) collective-permute-start(bf16[768,384]{1,0:T(8,128)(2,1)} %get-tuple-element.32), channel_id=1, source_target_pairs={{0,4},{1,5},{2,6},{3,7},{4,8},{5,9},{6,10},{7,11},{8,12},{9,13},{1... | collective-permute-start | bytes 1769480 | tf_op jit(solution)/shard_map/ppermute | solution.py:82
  177.7 70.3 %collective-permute-start.22 = (bf16[768,384]{1,0:T(8,128)(2,1)}, bf16[768,384]{1,0:T(8,128)(2,1)}, u32[]{:S(2)}, u32[]{:S(2)}) collective-permute-start(bf16[768,384]{1,0:T(8,128)(2,1)} %get-tuple-element.33), channel_id=1, source_target_pairs={{4,0},{5,1},{6,2},{7,3},{8,4},{9,5},{10,6},{11,7},{12,8},{13,9},{1... | collective-permute-start | bytes 1769480 | tf_op jit(solution)/shard_map/ppermute | solution.py:82
  181.5 33.7 %collective-permute-start = (s32[3,2,9]{2,1,0:T(2,128)S(1)}, s32[3,2,9]{2,1,0:T(2,128)S(1)}, u32[]{:S(2)}, u32[]{:S(2)}) collective-permute-start(s32[3,2,9]{2,1,0:T(2,128)S(1)} %get-tuple-element.43), channel_id=1, source_target_pairs={{0,0},{1,2},{2,32},{3,34},{4,4},{5,6},{6,36},{7,38},{8,8},{9,10},{... | collective-permute-start | bytes 656 | tf_op jit(solution)/shard_map/ppermute | solution.py:82
  209.3 38.6 %collective-permute-start.23 = (f32[8,768]{1,0:T(8,128)}, f32[8,768]{1,0:T(8,128)}, u32[]{:S(2)}, u32[]{:S(2)}) collective-permute-start(f32[8,768]{1,0:T(8,128)} %copy-done.3), channel_id=1, source_target_pairs={{0,4},{1,5},{2,6},{3,7},{4,8},{5,9},{6,10},{7,11},{8,12},{9,13},{1... | collective-permute-start | bytes 73736 | tf_op jit(solution)/shard_map/ppermute | solution.py:82
  211.9 36.1 %collective-permute-start.24 = (f32[8,768]{1,0:T(8,128)}, f32[8,768]{1,0:T(8,128)}, u32[]{:S(2)}, u32[]{:S(2)}) collective-permute-start(f32[8,768]{1,0:T(8,128)} %copy-done.2), channel_id=1, source_target_pairs={{4,0},{5,1},{6,2},{7,3},{8,4},{9,5},{10,6},{11,7},{12,8},{13,9},{1... | collective-permute-start | bytes 73736 | tf_op jit(solution)/shard_map/ppermute | solution.py:82
  250.4 23.5 %collective-permute-start.25 = (bf16[192,384]{1,0:T(8,128)(2,1)S(1)}, bf16[192,384]{1,0:T(8,128)(2,1)S(1)}, u32[]{:S(2)}, u32[]{:S(2)}) collective-permute-start(bf16[192,384]{1,0:T(8,128)(2,1)S(1)} %get-tuple-element.37), channel_id=1, source_target_pairs={{0,0},{2,1},{32,2},{34,3},{4,4},{6,5},{36,6},{38,7},{8,8},{10,9},{... | collective-permute-start | bytes 442376 | tf_op jit(solution)/shard_map/ppermute | solution.py:82
  252.4 21.6 %collective-permute-start.26 = (bf16[192,384]{1,0:T(8,128)(2,1)S(1)}, bf16[192,384]{1,0:T(8,128)(2,1)S(1)}, u32[]{:S(2)}, u32[]{:S(2)}) collective-permute-start(bf16[192,384]{1,0:T(8,128)(2,1)S(1)} %get-tuple-element.38), channel_id=1, source_target_pairs={{2,0},{0,1},{34,2},{32,3},{6,4},{4,5},{38,6},{36,7},{10,8},{8,9},{... | collective-permute-start | bytes 442376 | tf_op jit(solution)/shard_map/ppermute | solution.py:82
  266.0 11.3 %collective-permute-start.27 = (bf16[192,384]{1,0:T(8,128)(2,1)S(1)}, bf16[192,384]{1,0:T(8,128)(2,1)S(1)}, u32[]{:S(2)}, u32[]{:S(2)}) collective-permute-start(bf16[192,384]{1,0:T(8,128)(2,1)S(1)} %get-tuple-element.39), channel_id=1, source_target_pairs={{32,0},{34,1},{0,2},{2,3},{36,4},{38,5},{4,6},{6,7},{40,8},{42,9},... | collective-permute-start | bytes 442376 | tf_op jit(solution)/shard_map/ppermute | solution.py:82
  272.0 8.0 %collective-permute-start.28 = (bf16[192,384]{1,0:T(8,128)(2,1)S(1)}, bf16[192,384]{1,0:T(8,128)(2,1)S(1)}, u32[]{:S(2)}, u32[]{:S(2)}) collective-permute-start(bf16[192,384]{1,0:T(8,128)(2,1)S(1)} %get-tuple-element.40), channel_id=1, source_target_pairs={{34,0},{32,1},{2,2},{0,3},{38,4},{36,5},{6,6},{4,7},{42,8},{40,9},... | collective-permute-start | bytes 442376 | tf_op jit(solution)/shard_map/ppermute | solution.py:82
  274.0 6.0 %copy-start.4 = (bf16[192,384]{1,0:T(8,128)(2,1)}, bf16[192,384]{1,0:T(8,128)(2,1)S(1)}, u32[]{:S(2)}) copy-start(bf16[192,384]{1,0:T(8,128)(2,1)S(1)} %collective-permute-done.25.rest_0_) | copy-start | bytes 442372
  274.0 6.0 %copy-start.5 = (bf16[192,384]{1,0:T(8,128)(2,1)}, bf16[192,384]{1,0:T(8,128)(2,1)S(1)}, u32[]{:S(2)}) copy-start(bf16[192,384]{1,0:T(8,128)(2,1)S(1)} %collective-permute-done.26.rest_1_) | copy-start | bytes 442372
  277.3 2.7 copy-start.6
  280.0 0.7 copy-start.7

commit v2 on v1

--- a/solution.py
+++ b/solution.py
@@ -13,6 +13,7 @@
 AXES = ("seq", "head")
 FAR = -1e30
 VMEM_LIMIT = 40 * 2**20
+BATCH = 2
 
 
 def linear(y, xh, z, xl, core):
@@ -82,71 +83,63 @@
     return lax.ppermute(x, AXES, pairs)
 
 
-def split_kernel(at_ref, qkv_ref, *rest):
-    outs, sems = rest[:8], rest[8]
+def split_kernel(at_ref, qkv_ref, *outs):
     width = outs[0].shape[-1]
-    copies = []
     for k in range(4):
-        start = pl.multiple_of((at_ref[0] ^ k) * width, 128)
-        copies.append(pltpu.make_async_copy(qkv_ref.at[0, :, pl.ds(start, width)], outs[k], sems.at[k]))
-        copies.append(
-            pltpu.make_async_copy(qkv_ref.at[pl.ds(1, 2), :, pl.ds(start, width)], outs[4 + k], sems.at[4 + k])
-        )
-    for copy in copies:
-        copy.start()
-    for copy in copies:
-        copy.wait()
+        lanes = pl.ds(pl.multiple_of((at_ref[0] ^ k) * width, 128), width)
+        outs[k][...] = qkv_ref[0, :, lanes]
+        outs[4 + k][...] = qkv_ref[1:3, :, lanes]
 
 
 def split(at, qkv):
     _, rows, columns = qkv.shape
     width = columns // 4
-    hbm = pl.BlockSpec(memory_space=pl.ANY)
+    vmem = pl.BlockSpec(memory_space=pltpu.VMEM)
     shapes = [jax.ShapeDtypeStruct((rows, width), qkv.dtype)] * 4
     shapes += [jax.ShapeDtypeStruct((2, rows, width), qkv.dtype)] * 4
     return pl.pallas_call(
         split_kernel,
         out_shape=shapes,
-        in_specs=[pl.BlockSpec(memory_space=pltpu.SMEM), hbm],
-        out_specs=[hbm] * 8,
-        scratch_shapes=[pltpu.SemaphoreType.DMA((8,))],
+        in_specs=[pl.BlockSpec(memory_space=pltpu.SMEM), vmem],
+        out_specs=[vmem] * 8,
+        compiler_params=pltpu.CompilerParams(vmem_limit_bytes=VMEM_LIMIT),
         name="split",
     )(at, qkv)
 
 
-def join_kernel(at_ref, *rest):
-    parts, out_ref, sems = rest[:4], rest[4], rest[5]
+def join_kernel(at_ref, *refs):
+    parts, out_ref = refs[:4], refs[4]
     width = parts[0].shape[-1]
-    copies = []
     for k in range(4):
-        start = pl.multiple_of((at_ref[0] ^ k) * width, 128)
-        copies.append(pltpu.make_async_copy(parts[k], out_ref.at[:, pl.ds(start, width)], sems.at[k]))
-    for copy in copies:
-        copy.start()
-    for copy in copies:
-        copy.wait()
+        out_ref[:, pl.ds(pl.multiple_of((at_ref[0] ^ k) * width, 128), width)] = parts[k][...]
 
 
 def join(at, parts):
     rows, width = parts[0].shape
-    hbm = pl.BlockSpec(memory_space=pl.ANY)
+    vmem = pl.BlockSpec(memory_space=pltpu.VMEM)
     return pl.pallas_call(
         join_kernel,
         out_shape=jax.ShapeDtypeStruct((rows, 4 * width), parts[0].dtype),
-        in_specs=[pl.BlockSpec(memory_space=pltpu.SMEM)] + [hbm] * 4,
-        out_specs=hbm,
-        scratch_shapes=[pltpu.SemaphoreType.DMA((4,))],
+        in_specs=[pl.BlockSpec(memory_space=pltpu.SMEM)] + [vmem] * 4,
+        out_specs=vmem,
+        compiler_params=pltpu.CompilerParams(vmem_limit_bytes=VMEM_LIMIT),
         name="join",
     )(at, *parts)
 
 
-def attend_kernel(mask_ref, *refs, sets, heads, tile, dim, sub):
+def attend_kernel(mask_ref, *refs, sets, heads, tile, dim):
     queries = refs[:sets]
     bodies = refs[sets : sets + 3]
     edges = refs[sets + 3 : sets + 6]
     outs = refs[sets + 6 : 2 * sets + 6]
     lses = refs[2 * sets + 6 : 3 * sets + 6]
-    pool, held, max_ref, sum_ref, acc_ref, sems = refs[3 * sets + 6 :]
+    pool, held, turned_q, turned_v, max_ref, sum_ref, acc_ref, of_query, of_key = refs[3 * sets + 6 : 3 * sets + 15]
+    rest = refs[3 * sets + 15 :]
+    score_refs = (rest[:BATCH], rest[BATCH : 2 * BATCH])
+    top_refs = (rest[2 * BATCH : 3 * BATCH], rest[3 * BATCH : 4 * BATCH])
+    sems = rest[4 * BATCH]
+    count_q = sets * heads * 2
+
     copies = []
     for n in range(sets):
         copies.append(pltpu.make_async_copy(queries[n], held.at[n], sems.at[n]))
@@ -155,64 +148,84 @@
         copies.append(pltpu.make_async_copy(edges[c], pool.at[c, :, pl.ds(2 * tile, tile)], sems.at[sets + 3 + c]))
     for copy in copies:
         copy.start()
+
+    def list_pairs_of(s, count):
+        for j in range(9):
+            of_query[count] = s
+            of_key[count] = j
+            count = count + mask_ref[s * 9 + j]
+        return count
+
+    count = lax.fori_loop(0, count_q, list_pairs_of, 0)
+    for i in range(4 * BATCH):
+        of_query[count + i] = count_q
+        of_key[count + i] = 0
+    max_ref[...] = jnp.full_like(max_ref, FAR)
+    sum_ref[...] = jnp.zeros_like(sum_ref)
+    acc_ref[...] = jnp.zeros_like(acc_ref)
     for copy in copies:
         copy.wait()
+    for n in range(sets):
+        for h in range(heads):
+            for p in range(2):
+                turned_q[(n * heads + h) * 2 + p] = jnp.transpose(
+                    held[n, p * tile : (p + 1) * tile, h * dim : (h + 1) * dim]
+                )
+    turned_q[count_q] = turned_q[0]
+    for h in range(heads):
+        for j in range(9):
+            c, r = divmod(j, 3)
+            turned_v[h * 9 + j] = jnp.transpose(pool[c, 1, r * tile : (r + 1) * tile, h * dim : (h + 1) * dim])
+
     scale = dim**-0.5
     factor = scale * math.log2(math.e)
+
+    def score(i, out_ref, top_ref):
+        s, j = of_query[i], of_key[i]
+        h = lax.rem(s // 2, heads)
+        c = j // 3
+        rows = pl.ds(pl.multiple_of((j - 3 * c) * tile, 128), tile)
+        keys = pool[c, 0, rows, pl.ds(pl.multiple_of(h * dim, dim), dim)]
+        scores = jnp.dot(keys, turned_q[s], preferred_element_type=jnp.float32)
+        out_ref[...] = scores
+        top_ref[...] = jnp.max(scores.reshape(tile // 8, 8, tile), axis=0)
+
+    def weigh(i, in_ref, top_ref):
+        s, j = of_query[i], of_key[i]
+        h = lax.rem(s // 2, heads)
+        old = max_ref[s, :1, :]
+        new = jnp.maximum(old, jnp.max(top_ref[...], axis=0, keepdims=True))
+        shrink = jnp.exp2((old - new) * factor)
+        max_ref[s, :1, :] = new
+        weights = jnp.exp2((in_ref[...] - new) * factor)
+        sum_ref[s] = sum_ref[s] * shrink + jnp.sum(weights.reshape(tile // 8, 8, tile), axis=0)
+        acc_ref[s] = acc_ref[s] * shrink + jnp.dot(
+            turned_v[h * 9 + j], weights.astype(jnp.bfloat16), preferred_element_type=jnp.float32
+        )
+
+    for u in range(BATCH):
+        score(u, score_refs[0][u], top_refs[0][u])
+
+    def step(t, carry):
+        for half in range(2):
+            base = (2 * t + half) * BATCH
+            for u in range(BATCH):
+                score(base + BATCH + u, score_refs[1 - half][u], top_refs[1 - half][u])
+            for u in range(BATCH):
+                weigh(base + u, score_refs[half][u], top_refs[half][u])
+        return carry
+
+    lax.fori_loop(0, (count + 2 * BATCH - 1) // (2 * BATCH), step, 0)
+
     for n in range(sets):
         lses[n][...] = jnp.zeros_like(lses[n])
-
-        def per_head(h, carry, n=n):
-            lanes = pl.ds(pl.multiple_of(h * dim, dim), dim)
-
-            def per_tile(p, carry):
-                max_ref[...] = jnp.full_like(max_ref, FAR)
-                sum_ref[...] = jnp.zeros_like(sum_ref)
-                acc_ref[...] = jnp.zeros_like(acc_ref)
-
-                def per_key_tile(j, carry):
-                    c = j // 3
-                    start = pl.multiple_of((j - 3 * c) * tile, tile)
-
-                    @pl.when(mask_ref[((n * heads + h) * 2 + p) * 9 + j] > 0)
-                    def _():
-                        keys = pool[c, 0, pl.ds(start, tile), lanes]
-                        values = pool[c, 1, pl.ds(start, tile), lanes]
-                        for b in range(tile // sub):
-                            rows = pl.ds(b * sub, sub)
-                            q = held[n, pl.ds(pl.multiple_of(p * tile + b * sub, sub), sub), lanes]
-                            scores = lax.dot_general(
-                                q, keys, (((1,), (1,)), ((), ())), preferred_element_type=jnp.float32
-                            )
-                            old = max_ref[rows, :]
-                            new = jnp.maximum(old, jnp.max(scores, axis=1, keepdims=True))
-                            shrink = jnp.exp2((old - new) * factor)
-                            weights = jnp.exp2((scores - new[:, :1]) * factor)
-                            total = sum_ref[rows, :] * shrink
-                            for i in range(tile // dim):
-                                total = total + weights[:, i * dim : (i + 1) * dim]
-                            max_ref[rows, :] = new
-                            sum_ref[rows, :] = total
-                            acc_ref[rows, :] = acc_ref[rows, :] * shrink + lax.dot_general(
-                                weights.astype(jnp.bfloat16),
-                                values,
-                                (((1,), (0,)), ((), ())),
-                                preferred_element_type=jnp.float32,
-                            )
-
-                    return carry
-
-                lax.fori_loop(0, 9, per_key_tile, 0)
-                total = jnp.maximum(jnp.sum(sum_ref[...], axis=1, keepdims=True), 1e-30)
-                at = pl.multiple_of(p * tile, tile)
-                outs[n][pl.ds(at, tile), lanes] = (acc_ref[...] / total).astype(outs[n].dtype)
-                lse = max_ref[...] * scale + jnp.log(total)
-                lses[n][pl.ds(h, 1), pl.ds(at, tile)] = jnp.transpose(lse)[:1, :]
-                return carry
-
-            return lax.fori_loop(0, 2, per_tile, carry)
-
-        lax.fori_loop(0, heads, per_head, 0)
+        for h in range(heads):
+            for p in range(2):
+                s = (n * heads + h) * 2 + p
+                at = slice(p * tile, (p + 1) * tile)
+                total = jnp.maximum(jnp.sum(sum_ref[s], axis=0, keepdims=True), 1e-30)
+                outs[n][h * dim : (h + 1) * dim, at] = (acc_ref[s] / total).astype(outs[n].dtype)
+                lses[n][h : h + 1, at] = max_ref[s, :1, :] * scale + jnp.log(total)
 
 
 def attend(mask, queries, bodies, edges, heads, out_dtype):
@@ -220,22 +233,29 @@
     brick, width = queries[0].shape
     tile = brick // 2
     dim = width // heads
+    count_q = sets * heads * 2
     hbm = pl.BlockSpec(memory_space=pl.ANY)
     vmem = pl.BlockSpec(memory_space=pltpu.VMEM)
     outs = pl.pallas_call(
-        functools.partial(attend_kernel, sets=sets, heads=heads, tile=tile, dim=dim, sub=tile // 3),
-        out_shape=[jax.ShapeDtypeStruct((brick, width), out_dtype)] * sets
+        functools.partial(attend_kernel, sets=sets, heads=heads, tile=tile, dim=dim),
+        out_shape=[jax.ShapeDtypeStruct((width, brick), out_dtype)] * sets
         + [jax.ShapeDtypeStruct((8, brick), jnp.float32)] * sets,
         in_specs=[pl.BlockSpec(memory_space=pltpu.SMEM)] + [hbm] * (sets + 6),
         out_specs=[vmem] * (2 * sets),
         scratch_shapes=[
             pltpu.VMEM((3, 2, 3 * tile, width), jnp.bfloat16),
             pltpu.VMEM((sets, brick, width), jnp.bfloat16),
-            pltpu.VMEM((tile, dim), jnp.float32),
-            pltpu.VMEM((tile, dim), jnp.float32),
-            pltpu.VMEM((tile, dim), jnp.float32),
-            pltpu.SemaphoreType.DMA((sets + 6,)),
-        ],
+            pltpu.VMEM((count_q + 1, dim, tile), jnp.bfloat16),
+            pltpu.VMEM((9 * heads, dim, tile), jnp.bfloat16),
+            pltpu.VMEM((count_q + 1, 8, tile), jnp.float32),
+            pltpu.VMEM((count_q + 1, 8, tile), jnp.float32),
+            pltpu.VMEM((count_q + 1, dim, tile), jnp.float32),
+            pltpu.SMEM((count_q * 9 + 8 * BATCH,), jnp.int32),
+            pltpu.SMEM((count_q * 9 + 8 * BATCH,), jnp.int32),
+        ]
+        + [pltpu.VMEM((tile, tile), jnp.float32)] * (2 * BATCH)
+        + [pltpu.VMEM((8, tile), jnp.float32)] * (2 * BATCH)
+        + [pltpu.SemaphoreType.DMA((sets + 6,))],
         compiler_params=pltpu.CompilerParams(vmem_limit_bytes=VMEM_LIMIT),
         name=f"attend{sets}",
     )(mask, *queries, *bodies, *edges)
@@ -243,7 +263,7 @@
 
 
 def merge_kernel(valid_ref, own, before, after, own_lse, before_lse, after_lse, *outs, heads):
-    brick, width = own.shape
+    width, brick = own.shape
     dim = width // heads
     quarter = brick // 4
     lse = [
@@ -255,20 +275,18 @@
     shares = [jnp.exp(x - top) for x in lse]
     total = shares[0] + shares[1] + shares[2]
     shares = [x / total for x in shares]
-    spare = jnp.zeros((128 - 24, brick), jnp.float32)
-    columns = jnp.transpose(jnp.concatenate(shares + [spare], axis=0))
-    for k in range(4):
-        rows = slice(k * quarter, (k + 1) * quarter)
-        for h in range(heads):
-            lanes = slice(h * dim, (h + 1) * dim)
-            merged = own[rows, lanes].astype(jnp.float32) * columns[rows, h : h + 1]
-            merged += before[rows, lanes].astype(jnp.float32) * columns[rows, 8 + h : 9 + h]
-            merged += after[rows, lanes].astype(jnp.float32) * columns[rows, 16 + h : 17 + h]
-            outs[k][:, lanes] = merged.astype(outs[k].dtype)
+    for h in range(heads):
+        lanes = slice(h * dim, (h + 1) * dim)
+        merged = own[lanes, :].astype(jnp.float32) * shares[0][h : h + 1, :]
+        merged += before[lanes, :].astype(jnp.float32) * shares[1][h : h + 1, :]
+        merged += after[lanes, :].astype(jnp.float32) * shares[2][h : h + 1, :]
+        merged = jnp.transpose(merged).astype(jnp.bfloat16)
+        for k in range(4):
+            outs[k][:, lanes] = merged[k * quarter : (k + 1) * quarter, :]
 
 
 def merge(valid, parts, lses, heads):
-    brick, width = parts[0].shape
+    width, brick = parts[0].shape
     vmem = pl.BlockSpec(memory_space=pltpu.VMEM)
     return pl.pallas_call(
         functools.partial(merge_kernel, heads=heads),

time: 305 us -> 169 us (0.55)
  the two profiles are of different devices: /device:TPU:41 before, /device:TPU:177 now
where the time goes in v2:
time: 169 us; the launch traced here: 168 us
  starting transfers between devices  72.5 us (43%)
  waiting for transfers between devices  51.2 us (30%)
  Pallas kernels  33.9 us (20%)
  local copies, waits for them, and re-layouts  9.44 us (6%)
    ppermute x29, starting transfers between devices, send(): return lax.ppermute(x, AXES, pairs)  72.5 us
    ppermute x29, waiting for transfers between devices, send(): return lax.ppermute(x, AXES, pairs)  51.2 us
    pallas_call x2, Pallas kernels, attend(): pl.pallas_call(functools.partial(attend_kernel, sets=sets, heads=heads, t...  31.1 us
    unnamed x18, local copies, waits for them, and re-layouts  7.68 us
  transfers between devices with their start and end apart: 29, of which 11 were waited for; matrix products, arithmetic and copies ran while one was open for 3% of the time, Pallas kernels for 7%

profile of v2, /device:TPU:177, one launch (start us, length us, event | category | flops | bytes accessed | tf_op | source)
XLA Modules:
  0.0 167.9 jit_solution(13602384663771462048)
XLA Ops:
  0.0 1.5 copy-done
  1.6 1.8 %collective-permute-start.13 = (bf16[2,192,384]{2,1,0:T(8,128)(2,1)S(1)}, bf16[2,192,384]{2,1,0:T(8,128)(2,1)S(1)}, u32[]{:S(2)}, u32[]{:S(2)}) collective-permute-start(bf16[2,192,384]{2,1,0:T(8,128)(2,1)S(1)} %get-tuple-element.28), channel_id=1, source_target_pairs={{2,50},{3,48},{6,54},{7,52},{10,58},{11,56},{14,62},{15,60},{16,2}... | collective-permute-start | bytes 884744 | tf_op jit(solution)/shard_map/ppermute | solution.py:83
  3.5 1.4 collective-permute-start.6
  4.9 3.9 %collective-permute-start.5 = (bf16[2,192,384]{2,1,0:T(8,128)(2,1)S(1)}, bf16[2,192,384]{2,1,0:T(8,128)(2,1)}, u32[]{:S(2)}, u32[]{:S(2)}) collective-permute-start(bf16[2,192,384]{2,1,0:T(8,128)(2,1)S(1)} %get-tuple-element.27), channel_id=1, source_target_pairs={{0,0},{1,2},{2,32},{3,34},{4,4},{5,6},{6,36},{7,38},{8,8},{9,10},{... | collective-permute-start | bytes 884744 | tf_op jit(solution)/shard_map/ppermute | solution.py:83
  8.8 1.9 %collective-permute-start.1 = (bf16[192,384]{1,0:T(8,128)(2,1)S(1)}, bf16[192,384]{1,0:T(8,128)(2,1)S(1)}, u32[]{:S(2)}, u32[]{:S(2)}) collective-permute-start(bf16[192,384]{1,0:T(8,128)(2,1)S(1)} %get-tuple-element.23), channel_id=1, source_target_pairs={{0,0},{1,2},{2,32},{3,34},{4,4},{5,6},{6,36},{7,38},{8,8},{9,10},{... | collective-permute-start | bytes 442376 | tf_op jit(solution)/shard_map/ppermute | solution.py:83
  11.2 6.7 %collective-permute-done.1 = bf16[192,384]{1,0:T(8,128)(2,1)S(1)} collective-permute-done((bf16[192,384]{1,0:T(8,128)(2,1)S(1)}, bf16[192,384]{1,0:T(8,128)(2,1)S(1)}, u32[]{:S(2)}, u32[]{:S(2)}) %collective-permute-start.1) | collective-permute-done | bytes 147488 | tf_op jit(solution)/shard_map/ppermute | solution.py:83
  17.9 2.1 %collective-permute-start.3 = (bf16[192,384]{1,0:T(8,128)(2,1)S(1)}, bf16[192,384]{1,0:T(8,128)(2,1)S(1)}, u32[]{:S(2)}, u32[]{:S(2)}) collective-permute-start(bf16[192,384]{1,0:T(8,128)(2,1)S(1)} %get-tuple-element.25), channel_id=1, source_target_pairs={{0,32},{1,34},{2,0},{3,2},{4,36},{5,38},{6,4},{7,6},{8,40},{9,42},... | collective-permute-start | bytes 442376 | tf_op jit(solution)/shard_map/ppermute | solution.py:83
  20.0 0.7 constant_dynamic-update-slice_fusion.3
  20.7 2.3 %collective-permute-start.4 = (bf16[192,384]{1,0:T(8,128)(2,1)S(1)}, bf16[192,384]{1,0:T(8,128)(2,1)S(1)}, u32[]{:S(2)}, u32[]{:S(2)}) collective-permute-start(bf16[192,384]{1,0:T(8,128)(2,1)S(1)} %get-tuple-element.26), channel_id=1, source_target_pairs={{0,34},{1,32},{2,2},{3,0},{4,38},{5,36},{6,6},{7,4},{8,42},{9,40},... | collective-permute-start | bytes 442376 | tf_op jit(solution)/shard_map/ppermute | solution.py:83
  23.0 0.7 constant_dynamic-update-slice_fusion.2
  23.7 12.0 %collective-permute-start.14 = (bf16[2,192,384]{2,1,0:T(8,128)(2,1)S(1)}, bf16[2,192,384]{2,1,0:T(8,128)(2,1)S(1)}, u32[]{:S(2)}, u32[]{:S(2)}) collective-permute-start(bf16[2,192,384]{2,1,0:T(8,128)(2,1)S(1)} %get-tuple-element.30), channel_id=1, source_target_pairs={{2,18},{3,16},{6,22},{7,20},{10,26},{11,24},{14,30},{15,28},{16,34... | collective-permute-start | bytes 884744 | tf_op jit(solution)/shard_map/ppermute | solution.py:83
  35.8 0.7 constant_dynamic-update-slice_fusion.1
  36.4 0.7 constant_dynamic-update-slice_fusion.refs_0_
  37.1 1.9 %collective-permute-start.8 = (bf16[2,192,384]{2,1,0:T(8,128)(2,1)S(1)}, bf16[2,192,384]{2,1,0:T(8,128)(2,1)S(1)}, u32[]{:S(2)}, u32[]{:S(2)}) collective-permute-start(bf16[2,192,384]{2,1,0:T(8,128)(2,1)S(1)} %get-tuple-element.30), channel_id=1, source_target_pairs={{0,34},{1,32},{2,2},{3,0},{4,38},{5,36},{6,6},{7,4},{8,42},{9,40},... | collective-permute-start | bytes 884744 | tf_op jit(solution)/shard_map/ppermute | solution.py:83
  39.1 1.0 constant_dynamic-update-slice_fusion.7
  40.1 1.3 collective-permute-start.11
  41.4 4.2 %collective-permute-done.7 = bf16[2,192,384]{2,1,0:T(8,128)(2,1)S(1)} collective-permute-done((bf16[2,192,384]{2,1,0:T(8,128)(2,1)S(1)}, bf16[2,192,384]{2,1,0:T(8,128)(2,1)S(1)}, u32[]{:S(2)}, u32[]{:S(2)}) %collective-permute-start.7) | collective-permute-done | bytes 294944 | tf_op jit(solution)/shard_map/ppermute | solution.py:83
  45.7 1.9 %collective-permute-start.12 = (bf16[2,192,384]{2,1,0:T(8,128)(2,1)S(1)}, bf16[2,192,384]{2,1,0:T(8,128)(2,1)S(1)}, u32[]{:S(2)}, u32[]{:S(2)}) collective-permute-start(bf16[2,192,384]{2,1,0:T(8,128)(2,1)S(1)} %get-tuple-element.29), channel_id=1, source_target_pairs={{2,16},{3,18},{6,20},{7,22},{10,24},{11,26},{14,28},{15,30},{16,32... | collective-permute-start | bytes 884744 | tf_op jit(solution)/shard_map/ppermute | solution.py:83
  47.7 3.1 %collective-permute-start.19 = (bf16[768,384]{1,0:T(8,128)(2,1)}, bf16[768,384]{1,0:T(8,128)(2,1)S(1)}, u32[]{:S(2)}, u32[]{:S(2)}) collective-permute-start(bf16[768,384]{1,0:T(8,128)(2,1)} %constant_dynamic-update-slice_fusion.refs_0_), channel_id=1, source_target_pairs={{0,4},{1,5},{2,6},{3,7},{4,8},{5,9},{6,10},{7,11},{8,12},{9,13},{1... | collective-permute-start | bytes 1769480 | tf_op jit(solution)/shard_map/ppermute | solution.py:83
  50.9 5.7 %collective-permute-start.10 = (bf16[2,768,384]{2,1,0:T(8,128)(2,1)S(1)}, bf16[2,768,384]{2,1,0:T(8,128)(2,1)S(1)}, u32[]{:S(2)}, u32[]{:S(2)}) collective-permute-start(bf16[2,768,384]{2,1,0:T(8,128)(2,1)S(1)} %constant_dynamic-update-slice_fusion.4.refs_1_.refs_2_), channel_id=1, source_target_pairs={{1,64},{3,66},{5,68},{7,70},{9,72},{11,74},{13,76},{15,78},{17,80}... | collective-permute-start | bytes 3538952 | tf_op jit(solution)/shard_map/ppermute | solution.py:83
  56.6 4.3 %collective-permute-done.14 = bf16[2,192,384]{2,1,0:T(8,128)(2,1)S(1)} collective-permute-done((bf16[2,192,384]{2,1,0:T(8,128)(2,1)S(1)}, bf16[2,192,384]{2,1,0:T(8,128)(2,1)S(1)}, u32[]{:S(2)}, u32[]{:S(2)}) %collective-permute-start.14) | collective-permute-done | bytes 294944 | tf_op jit(solution)/shard_map/ppermute | solution.py:83
  60.8 1.7 %collective-permute-start.9 = (bf16[2,768,384]{2,1,0:T(8,128)(2,1)S(1)}, bf16[2,768,384]{2,1,0:T(8,128)(2,1)}, u32[]{:S(2)}, u32[]{:S(2)}) collective-permute-start(bf16[2,768,384]{2,1,0:T(8,128)(2,1)S(1)} %constant_dynamic-update-slice_fusion.4.refs_1_.refs_2_), channel_id=1, source_target_pairs={{0,1},{1,0},{2,3},{3,2},{4,5},{5,4},{6,7},{7,6},{8,9},{9,8},{10,11... | collective-permute-start | bytes 3538952 | tf_op jit(solution)/shard_map/ppermute | solution.py:83
  62.6 4.5 %collective-permute-done.11 = bf16[2,192,384]{2,1,0:T(8,128)(2,1)S(1)} collective-permute-done((bf16[2,192,384]{2,1,0:T(8,128)(2,1)S(1)}, bf16[2,192,384]{2,1,0:T(8,128)(2,1)S(1)}, u32[]{:S(2)}, u32[]{:S(2)}) %collective-permute-start.11) | collective-permute-done | bytes 294944 | tf_op jit(solution)/shard_map/ppermute | solution.py:83
  67.2 1.9 %collective-permute-start.17 = (s32[3,2,9]{2,1,0:T(2,128)S(1)}, s32[3,2,9]{2,1,0:T(2,128)S(1)}, u32[]{:S(2)}, u32[]{:S(2)}) collective-permute-start(s32[3,2,9]{2,1,0:T(2,128)S(1)} %get-tuple-element.41), channel_id=1, source_target_pairs={{0,4},{1,6},{2,36},{3,38},{4,8},{5,10},{6,40},{7,42},{8,12},{9,14}... | collective-permute-start | bytes 656 | tf_op jit(solution)/shard_map/ppermute | solution.py:83
  69.1 4.4 %collective-permute-done.12 = bf16[2,192,384]{2,1,0:T(8,128)(2,1)S(1)} collective-permute-done((bf16[2,192,384]{2,1,0:T(8,128)(2,1)S(1)}, bf16[2,192,384]{2,1,0:T(8,128)(2,1)S(1)}, u32[]{:S(2)}, u32[]{:S(2)}) %collective-permute-start.12) | collective-permute-done | bytes 294944 | tf_op jit(solution)/shard_map/ppermute | solution.py:83
  73.5 1.9 %collective-permute-start.18 = (s32[3,2,9]{2,1,0:T(2,128)S(1)}, s32[3,2,9]{2,1,0:T(2,128)}, u32[]{:S(2)}, u32[]{:S(2)}) collective-permute-start(s32[3,2,9]{2,1,0:T(2,128)S(1)} %get-tuple-element.42), channel_id=1, source_target_pairs={{4,0},{5,2},{6,32},{7,34},{8,4},{9,6},{10,36},{11,38},{12,8},{13,1... | collective-permute-start | bytes 656 | tf_op jit(solution)/shard_map/ppermute | solution.py:83
  75.5 1.9 %collective-permute-start.20 = (bf16[768,384]{1,0:T(8,128)(2,1)}, bf16[768,384]{1,0:T(8,128)(2,1)}, u32[]{:S(2)}, u32[]{:S(2)}) collective-permute-start(bf16[768,384]{1,0:T(8,128)(2,1)} %constant_dynamic-update-slice_fusion.refs_0_), channel_id=1, source_target_pairs={{4,0},{5,1},{6,2},{7,3},{8,4},{9,5},{10,6},{11,7},{12,8},{13,9},{1... | collective-permute-start | bytes 1769480 | tf_op jit(solution)/shard_map/ppermute | solution.py:83
  77.5 3.4 %collective-permute-done.18 = s32[3,2,9]{2,1,0:T(2,128)} collective-permute-done((s32[3,2,9]{2,1,0:T(2,128)S(1)}, s32[3,2,9]{2,1,0:T(2,128)}, u32[]{:S(2)}, u32[]{:S(2)}) %collective-permute-start.18) | collective-permute-done | bytes 248 | tf_op jit(solution)/shard_map/ppermute | solution.py:83
  80.9 0.8 copy-done.1
  81.7 3.3 %collective-permute-start.16 = (bf16[2,384,384]{2,1,0:T(8,128)(2,1)S(1)}, bf16[2,384,384]{2,1,0:T(8,128)(2,1)}, u32[]{:S(2)}, u32[]{:S(2)}) collective-permute-start(bf16[2,384,384]{2,1,0:T(8,128)(2,1)S(1)} %pad_maximum_fusion.refs_4_.refs_5_), channel_id=1, source_target_pairs={{1,64},{3,66},{5,68},{7,70},{9,72},{11,74},{13,76},{15,78},{17,80}... | collective-permute-start | bytes 1769480 | tf_op jit(solution)/shard_map/ppermute | solution.py:83
  85.1 0.8 reshape.16
  85.9 17.4 %collective-permute-done.20.refs_1_ = bf16[768,384]{1,0:T(8,128)(2,1)} collective-permute-done((bf16[768,384]{1,0:T(8,128)(2,1)}, bf16[768,384]{1,0:T(8,128)(2,1)}, u32[]{:S(2)}, u32[]{:S(2)}) %collective-permute-start.20) | collective-permute-done | bytes 589856 | tf_op jit(solution)/shard_map/ppermute | solution.py:83
  103.3 1.1 copy-done.2
  104.4 19.0 %attend2.1 = (bf16[384,768]{1,0:T(8,128)(2,1)}, bf16[384,768]{1,0:T(8,128)(2,1)}, f32[8,768]{1,0:T(8,128)S(1)}, f32[8,768]{1,0:T(8,128)S(1)}) custom-call(s32[108]{0:T(128)S(1)} %pad_add_fusion.mask_ref, bf16[768,384]{1,0:T(8,128)(2,1)S(1)} %copy-done.2, bf16[768,384]{1,0:T(8,128)(2,1)} %collective-permute-done.20.refs_1_, ...), custom_call_target="tpu_custom_call" | custom-call | tf_op jit(solution)/shard_map/attend2/pallas_call | solution.py:239
  124.6 3.0 %collective-permute-start.21 = (bf16[384,768]{1,0:T(8,128)(2,1)}, bf16[384,768]{1,0:T(8,128)(2,1)}, u32[]{:S(2)}, u32[]{:S(2)}) collective-permute-start(bf16[384,768]{1,0:T(8,128)(2,1)} %get-tuple-element.32), channel_id=1, source_target_pairs={{0,4},{1,5},{2,6},{3,7},{4,8},{5,9},{6,10},{7,11},{8,12},{9,13},{1... | collective-permute-start | bytes 1769480 | tf_op jit(solution)/shard_map/ppermute | solution.py:83
  127.6 3.1 %collective-permute-start.22 = (bf16[384,768]{1,0:T(8,128)(2,1)}, bf16[384,768]{1,0:T(8,128)(2,1)}, u32[]{:S(2)}, u32[]{:S(2)}) collective-permute-start(bf16[384,768]{1,0:T(8,128)(2,1)} %get-tuple-element.33), channel_id=1, source_target_pairs={{4,0},{5,1},{6,2},{7,3},{8,4},{9,5},{10,6},{11,7},{12,8},{13,9},{1... | collective-permute-start | bytes 1769480 | tf_op jit(solution)/shard_map/ppermute | solution.py:83
  130.7 1.9 %collective-permute-start = (s32[3,2,9]{2,1,0:T(2,128)S(1)}, s32[3,2,9]{2,1,0:T(2,128)S(1)}, u32[]{:S(2)}, u32[]{:S(2)}) collective-permute-start(s32[3,2,9]{2,1,0:T(2,128)S(1)} %get-tuple-element.43), channel_id=1, source_target_pairs={{0,0},{1,2},{2,32},{3,34},{4,4},{5,6},{6,36},{7,38},{8,8},{9,10},{... | collective-permute-start | bytes 656 | tf_op jit(solution)/shard_map/ppermute | solution.py:83
  132.6 2.2 %collective-permute-start.23 = (f32[8,768]{1,0:T(8,128)}, f32[8,768]{1,0:T(8,128)}, u32[]{:S(2)}, u32[]{:S(2)}) collective-permute-start(f32[8,768]{1,0:T(8,128)} %copy-done.4), channel_id=1, source_target_pairs={{0,4},{1,5},{2,6},{3,7},{4,8},{5,9},{6,10},{7,11},{8,12},{9,13},{1... | collective-permute-start | bytes 73736 | tf_op jit(solution)/shard_map/ppermute | solution.py:83
  134.9 3.6 %collective-permute-start.24 = (f32[8,768]{1,0:T(8,128)}, f32[8,768]{1,0:T(8,128)}, u32[]{:S(2)}, u32[]{:S(2)}) collective-permute-start(f32[8,768]{1,0:T(8,128)} %copy-done.3), channel_id=1, source_target_pairs={{4,0},{5,1},{6,2},{7,3},{8,4},{9,5},{10,6},{11,7},{12,8},{13,9},{1... | collective-permute-start | bytes 73736 | tf_op jit(solution)/shard_map/ppermute | solution.py:83
  138.7 12.1 %attend1.1 = (f32[384,768]{1,0:T(8,128)S(1)}, f32[8,768]{1,0:T(8,128)S(1)}) custom-call(s32[54]{0:T(128)S(1)} %reshape.14.mask_ref, bf16[768,384]{1,0:T(8,128)(2,1)} %constant_dynamic-update-slice_fusion.refs_0_, bf16[2,768,384]{2,1,0:T(8,128)(2,1)S(1)} %constant_dynamic-update-slice_fusion.4.refs_1_.refs_2_, ...), custom_call_target="tpu_custom_call" | custom-call | tf_op jit(solution)/shard_map/attend1/pallas_call | solution.py:239
  150.9 1.7 %merge.1 = (bf16[192,384]{1,0:T(8,128)(2,1)S(1)}, bf16[192,384]{1,0:T(8,128)(2,1)S(1)}, bf16[192,384]{1,0:T(8,128)(2,1)S(1)}, bf16[192,384]{1,0:T(8,128)(2,1)S(1)}) custom-call(s32[2]{0:T(128)S(1)} %add_convert_fusion.valid_ref, f32[384,768]{1,0:T(8,128)S(1)} %get-tuple-element.31.own, bf16[384,768]{1,0:T(8,128)(2,1)} %collective-permute-done.21.before, ...), custom_call_target="tpu_custom_call" | custom-call | tf_op jit(solution)/shard_map/merge/pallas_call | solution.py:291
  152.6 3.8 %collective-permute-start.25 = (bf16[192,384]{1,0:T(8,128)(2,1)S(1)}, bf16[192,384]{1,0:T(8,128)(2,1)S(1)}, u32[]{:S(2)}, u32[]{:S(2)}) collective-permute-start(bf16[192,384]{1,0:T(8,128)(2,1)S(1)} %get-tuple-element.37), channel_id=1, source_target_pairs={{0,0},{2,1},{32,2},{34,3},{4,4},{6,5},{36,6},{38,7},{8,8},{10,9},{... | collective-permute-start | bytes 442376 | tf_op jit(solution)/shard_map/ppermute | solution.py:83
  156.5 2.5 %collective-permute-start.27 = (bf16[192,384]{1,0:T(8,128)(2,1)S(1)}, bf16[192,384]{1,0:T(8,128)(2,1)S(1)}, u32[]{:S(2)}, u32[]{:S(2)}) collective-permute-start(bf16[192,384]{1,0:T(8,128)(2,1)S(1)} %get-tuple-element.39), channel_id=1, source_target_pairs={{32,0},{34,1},{0,2},{2,3},{36,4},{38,5},{4,6},{6,7},{40,8},{42,9},... | collective-permute-start | bytes 442376 | tf_op jit(solution)/shard_map/ppermute | solution.py:83
  159.0 1.9 %collective-permute-start.28 = (bf16[192,384]{1,0:T(8,128)(2,1)S(1)}, bf16[192,384]{1,0:T(8,128)(2,1)S(1)}, u32[]{:S(2)}, u32[]{:S(2)}) collective-permute-start(bf16[192,384]{1,0:T(8,128)(2,1)S(1)} %get-tuple-element.40), channel_id=1, source_target_pairs={{34,0},{32,1},{2,2},{0,3},{38,4},{36,5},{6,6},{4,7},{42,8},{40,9},... | collective-permute-start | bytes 442376 | tf_op jit(solution)/shard_map/ppermute | solution.py:83
  160.9 1.5 collective-permute-done.26.refs_1_
  162.4 1.5 collective-permute-done.27.refs_2_
  163.9 3.1 %collective-permute-done.28.refs_3_ = bf16[192,384]{1,0:T(8,128)(2,1)S(1)} collective-permute-done((bf16[192,384]{1,0:T(8,128)(2,1)S(1)}, bf16[192,384]{1,0:T(8,128)(2,1)S(1)}, u32[]{:S(2)}, u32[]{:S(2)}) %collective-permute-start.28) | collective-permute-done | bytes 147488 | tf_op jit(solution)/shard_map/ppermute | solution.py:83
  167.1 0.9 join.1
  (48 shorter events, 2.5 us)
Async XLA Ops:
  0.0 11.0 %copy-start.5 = (s32[3,2,27]{2,1,0:T(2,128)S(1)}, s32[3,2,27]{2,1,0:T(2,128)}, u32[]{:S(2)}) copy-start(s32[3,2,27]{2,1,0:T(2,128)} %param.3) | copy-start | bytes 1948
  0.0 1.5 copy-start
  1.6 49.2 %collective-permute-start.13 = (bf16[2,192,384]{2,1,0:T(8,128)(2,1)S(1)}, bf16[2,192,384]{2,1,0:T(8,128)(2,1)S(1)}, u32[]{:S(2)}, u32[]{:S(2)}) collective-permute-start(bf16[2,192,384]{2,1,0:T(8,128)(2,1)S(1)} %get-tuple-element.28), channel_id=1, source_target_pairs={{2,50},{3,48},{6,54},{7,52},{10,58},{11,56},{14,62},{15,60},{16,2}... | collective-permute-start | bytes 884744 | tf_op jit(solution)/shard_map/ppermute | solution.py:83
  3.5 36.5 %collective-permute-start.6 = (bf16[2,192,384]{2,1,0:T(8,128)(2,1)S(1)}, bf16[2,192,384]{2,1,0:T(8,128)(2,1)S(1)}, u32[]{:S(2)}, u32[]{:S(2)}) collective-permute-start(bf16[2,192,384]{2,1,0:T(8,128)(2,1)S(1)} %get-tuple-element.28), channel_id=1, source_target_pairs={{0,2},{1,0},{2,34},{3,32},{4,6},{5,4},{6,38},{7,36},{8,10},{9,8},{... | collective-permute-start | bytes 884744 | tf_op jit(solution)/shard_map/ppermute | solution.py:83
  4.9 32.2 %collective-permute-start.5 = (bf16[2,192,384]{2,1,0:T(8,128)(2,1)S(1)}, bf16[2,192,384]{2,1,0:T(8,128)(2,1)}, u32[]{:S(2)}, u32[]{:S(2)}) collective-permute-start(bf16[2,192,384]{2,1,0:T(8,128)(2,1)S(1)} %get-tuple-element.27), channel_id=1, source_target_pairs={{0,0},{1,2},{2,32},{3,34},{4,4},{5,6},{6,36},{7,38},{8,8},{9,10},{... | collective-permute-start | bytes 884744 | tf_op jit(solution)/shard_map/ppermute | solution.py:83
  8.8 9.1 %collective-permute-start.1 = (bf16[192,384]{1,0:T(8,128)(2,1)S(1)}, bf16[192,384]{1,0:T(8,128)(2,1)S(1)}, u32[]{:S(2)}, u32[]{:S(2)}) collective-permute-start(bf16[192,384]{1,0:T(8,128)(2,1)S(1)} %get-tuple-element.23), channel_id=1, source_target_pairs={{0,0},{1,2},{2,32},{3,34},{4,4},{5,6},{6,36},{7,38},{8,8},{9,10},{... | collective-permute-start | bytes 442376 | tf_op jit(solution)/shard_map/ppermute | solution.py:83
  10.8 10.0 %collective-permute-start.2 = (bf16[192,384]{1,0:T(8,128)(2,1)S(1)}, bf16[192,384]{1,0:T(8,128)(2,1)S(1)}, u32[]{:S(2)}, u32[]{:S(2)}) collective-permute-start(bf16[192,384]{1,0:T(8,128)(2,1)S(1)} %get-tuple-element.24), channel_id=1, source_target_pairs={{0,2},{1,0},{2,34},{3,32},{4,6},{5,4},{6,38},{7,36},{8,10},{9,8},{... | collective-permute-start | bytes 442376 | tf_op jit(solution)/shard_map/ppermute | solution.py:83
  17.9 5.8 %collective-permute-start.3 = (bf16[192,384]{1,0:T(8,128)(2,1)S(1)}, bf16[192,384]{1,0:T(8,128)(2,1)S(1)}, u32[]{:S(2)}, u32[]{:S(2)}) collective-permute-start(bf16[192,384]{1,0:T(8,128)(2,1)S(1)} %get-tuple-element.25), channel_id=1, source_target_pairs={{0,32},{1,34},{2,0},{3,2},{4,36},{5,38},{6,4},{7,6},{8,40},{9,42},... | collective-permute-start | bytes 442376 | tf_op jit(solution)/shard_map/ppermute | solution.py:83
  20.7 15.7 %collective-permute-start.4 = (bf16[192,384]{1,0:T(8,128)(2,1)S(1)}, bf16[192,384]{1,0:T(8,128)(2,1)S(1)}, u32[]{:S(2)}, u32[]{:S(2)}) collective-permute-start(bf16[192,384]{1,0:T(8,128)(2,1)S(1)} %get-tuple-element.26), channel_id=1, source_target_pairs={{0,34},{1,32},{2,2},{3,0},{4,38},{5,36},{6,6},{7,4},{8,42},{9,40},... | collective-permute-start | bytes 442376 | tf_op jit(solution)/shard_map/ppermute | solution.py:83
  23.7 37.1 %collective-permute-start.14 = (bf16[2,192,384]{2,1,0:T(8,128)(2,1)S(1)}, bf16[2,192,384]{2,1,0:T(8,128)(2,1)S(1)}, u32[]{:S(2)}, u32[]{:S(2)}) collective-permute-start(bf16[2,192,384]{2,1,0:T(8,128)(2,1)S(1)} %get-tuple-element.30), channel_id=1, source_target_pairs={{2,18},{3,16},{6,22},{7,20},{10,26},{11,24},{14,30},{15,28},{16,34... | collective-permute-start | bytes 884744 | tf_op jit(solution)/shard_map/ppermute | solution.py:83
  36.4 9.2 %collective-permute-start.7 = (bf16[2,192,384]{2,1,0:T(8,128)(2,1)S(1)}, bf16[2,192,384]{2,1,0:T(8,128)(2,1)S(1)}, u32[]{:S(2)}, u32[]{:S(2)}) collective-permute-start(bf16[2,192,384]{2,1,0:T(8,128)(2,1)S(1)} %get-tuple-element.29), channel_id=1, source_target_pairs={{0,32},{1,34},{2,0},{3,2},{4,36},{5,38},{6,4},{7,6},{8,40},{9,42},... | collective-permute-start | bytes 884744 | tf_op jit(solution)/shard_map/ppermute | solution.py:83
  37.1 10.6 %collective-permute-start.8 = (bf16[2,192,384]{2,1,0:T(8,128)(2,1)S(1)}, bf16[2,192,384]{2,1,0:T(8,128)(2,1)S(1)}, u32[]{:S(2)}, u32[]{:S(2)}) collective-permute-start(bf16[2,192,384]{2,1,0:T(8,128)(2,1)S(1)} %get-tuple-element.30), channel_id=1, source_target_pairs={{0,34},{1,32},{2,2},{3,0},{4,38},{5,36},{6,6},{7,4},{8,42},{9,40},... | collective-permute-start | bytes 884744 | tf_op jit(solution)/shard_map/ppermute | solution.py:83
  40.1 27.1 %collective-permute-start.11 = (bf16[2,192,384]{2,1,0:T(8,128)(2,1)S(1)}, bf16[2,192,384]{2,1,0:T(8,128)(2,1)S(1)}, u32[]{:S(2)}, u32[]{:S(2)}) collective-permute-start(bf16[2,192,384]{2,1,0:T(8,128)(2,1)S(1)} %get-tuple-element.27), channel_id=1, source_target_pairs={{2,48},{3,50},{6,52},{7,54},{10,56},{11,58},{14,60},{15,62},{16,0}... | collective-permute-start | bytes 884744 | tf_op jit(solution)/shard_map/ppermute | solution.py:83
  45.7 27.8 %collective-permute-start.12 = (bf16[2,192,384]{2,1,0:T(8,128)(2,1)S(1)}, bf16[2,192,384]{2,1,0:T(8,128)(2,1)S(1)}, u32[]{:S(2)}, u32[]{:S(2)}) collective-permute-start(bf16[2,192,384]{2,1,0:T(8,128)(2,1)S(1)} %get-tuple-element.29), channel_id=1, source_target_pairs={{2,16},{3,18},{6,20},{7,22},{10,24},{11,26},{14,28},{15,30},{16,32... | collective-permute-start | bytes 884744 | tf_op jit(solution)/shard_map/ppermute | solution.py:83
  47.7 33.2 %collective-permute-start.19 = (bf16[768,384]{1,0:T(8,128)(2,1)}, bf16[768,384]{1,0:T(8,128)(2,1)S(1)}, u32[]{:S(2)}, u32[]{:S(2)}) collective-permute-start(bf16[768,384]{1,0:T(8,128)(2,1)} %constant_dynamic-update-slice_fusion.refs_0_), channel_id=1, source_target_pairs={{0,4},{1,5},{2,6},{3,7},{4,8},{5,9},{6,10},{7,11},{8,12},{9,13},{1... | collective-permute-start | bytes 1769480 | tf_op jit(solution)/shard_map/ppermute | solution.py:83
  50.9 52.5 %collective-permute-start.10 = (bf16[2,768,384]{2,1,0:T(8,128)(2,1)S(1)}, bf16[2,768,384]{2,1,0:T(8,128)(2,1)S(1)}, u32[]{:S(2)}, u32[]{:S(2)}) collective-permute-start(bf16[2,768,384]{2,1,0:T(8,128)(2,1)S(1)} %constant_dynamic-update-slice_fusion.4.refs_1_.refs_2_), channel_id=1, source_target_pairs={{1,64},{3,66},{5,68},{7,70},{9,72},{11,74},{13,76},{15,78},{17,80}... | collective-permute-start | bytes 3538952 | tf_op jit(solution)/shard_map/ppermute | solution.py:83
  60.8 42.5 %collective-permute-start.9 = (bf16[2,768,384]{2,1,0:T(8,128)(2,1)S(1)}, bf16[2,768,384]{2,1,0:T(8,128)(2,1)}, u32[]{:S(2)}, u32[]{:S(2)}) collective-permute-start(bf16[2,768,384]{2,1,0:T(8,128)(2,1)S(1)} %constant_dynamic-update-slice_fusion.4.refs_1_.refs_2_), channel_id=1, source_target_pairs={{0,1},{1,0},{2,3},{3,2},{4,5},{5,4},{6,7},{7,6},{8,9},{9,8},{10,11... | collective-permute-start | bytes 3538952 | tf_op jit(solution)/shard_map/ppermute | solution.py:83
  67.2 8.4 %collective-permute-start.17 = (s32[3,2,9]{2,1,0:T(2,128)S(1)}, s32[3,2,9]{2,1,0:T(2,128)S(1)}, u32[]{:S(2)}, u32[]{:S(2)}) collective-permute-start(s32[3,2,9]{2,1,0:T(2,128)S(1)} %get-tuple-element.41), channel_id=1, source_target_pairs={{0,4},{1,6},{2,36},{3,38},{4,8},{5,10},{6,40},{7,42},{8,12},{9,14}... | collective-permute-start | bytes 656 | tf_op jit(solution)/shard_map/ppermute | solution.py:83
  73.5 7.4 %collective-permute-start.18 = (s32[3,2,9]{2,1,0:T(2,128)S(1)}, s32[3,2,9]{2,1,0:T(2,128)}, u32[]{:S(2)}, u32[]{:S(2)}) collective-permute-start(s32[3,2,9]{2,1,0:T(2,128)S(1)} %get-tuple-element.42), channel_id=1, source_target_pairs={{4,0},{5,2},{6,32},{7,34},{8,4},{9,6},{10,36},{11,38},{12,8},{13,1... | collective-permute-start | bytes 656 | tf_op jit(solution)/shard_map/ppermute | solution.py:83
  75.5 27.8 %collective-permute-start.20 = (bf16[768,384]{1,0:T(8,128)(2,1)}, bf16[768,384]{1,0:T(8,128)(2,1)}, u32[]{:S(2)}, u32[]{:S(2)}) collective-permute-start(bf16[768,384]{1,0:T(8,128)(2,1)} %constant_dynamic-update-slice_fusion.refs_0_), channel_id=1, source_target_pairs={{4,0},{5,1},{6,2},{7,3},{8,4},{9,5},{10,6},{11,7},{12,8},{13,9},{1... | collective-permute-start | bytes 1769480 | tf_op jit(solution)/shard_map/ppermute | solution.py:83
  80.9 22.4 %collective-permute-start.15 = (bf16[2,384,384]{2,1,0:T(8,128)(2,1)S(1)}, bf16[2,384,384]{2,1,0:T(8,128)(2,1)S(1)}, u32[]{:S(2)}, u32[]{:S(2)}) collective-permute-start(bf16[2,384,384]{2,1,0:T(8,128)(2,1)S(1)} %pad_maximum_fusion.refs_4_.refs_5_), channel_id=1, source_target_pairs={{0,1},{1,0},{2,3},{3,2},{4,5},{5,4},{6,7},{7,6},{8,9},{9,8},{10,11... | collective-permute-start | bytes 1769480 | tf_op jit(solution)/shard_map/ppermute | solution.py:83
  80.9 0.8 copy-start.1
  81.7 21.6 %collective-permute-start.16 = (bf16[2,384,384]{2,1,0:T(8,128)(2,1)S(1)}, bf16[2,384,384]{2,1,0:T(8,128)(2,1)}, u32[]{:S(2)}, u32[]{:S(2)}) collective-permute-start(bf16[2,384,384]{2,1,0:T(8,128)(2,1)S(1)} %pad_maximum_fusion.refs_4_.refs_5_), channel_id=1, source_target_pairs={{1,64},{3,66},{5,68},{7,70},{9,72},{11,74},{13,76},{15,78},{17,80}... | collective-permute-start | bytes 1769480 | tf_op jit(solution)/shard_map/ppermute | solution.py:83
  103.3 1.1 copy-start.2
  123.4 0.6 copy-start.3
  124.0 0.6 copy-start.4
  124.6 26.2 %collective-permute-start.21 = (bf16[384,768]{1,0:T(8,128)(2,1)}, bf16[384,768]{1,0:T(8,128)(2,1)}, u32[]{:S(2)}, u32[]{:S(2)}) collective-permute-start(bf16[384,768]{1,0:T(8,128)(2,1)} %get-tuple-element.32), channel_id=1, source_target_pairs={{0,4},{1,5},{2,6},{3,7},{4,8},{5,9},{6,10},{7,11},{8,12},{9,13},{1... | collective-permute-start | bytes 1769480 | tf_op jit(solution)/shard_map/ppermute | solution.py:83
  127.6 23.2 %collective-permute-start.22 = (bf16[384,768]{1,0:T(8,128)(2,1)}, bf16[384,768]{1,0:T(8,128)(2,1)}, u32[]{:S(2)}, u32[]{:S(2)}) collective-permute-start(bf16[384,768]{1,0:T(8,128)(2,1)} %get-tuple-element.33), channel_id=1, source_target_pairs={{4,0},{5,1},{6,2},{7,3},{8,4},{9,5},{10,6},{11,7},{12,8},{13,9},{1... | collective-permute-start | bytes 1769480 | tf_op jit(solution)/shard_map/ppermute | solution.py:83
  130.7 7.9 %collective-permute-start = (s32[3,2,9]{2,1,0:T(2,128)S(1)}, s32[3,2,9]{2,1,0:T(2,128)S(1)}, u32[]{:S(2)}, u32[]{:S(2)}) collective-permute-start(s32[3,2,9]{2,1,0:T(2,128)S(1)} %get-tuple-element.43), channel_id=1, source_target_pairs={{0,0},{1,2},{2,32},{3,34},{4,4},{5,6},{6,36},{7,38},{8,8},{9,10},{... | collective-permute-start | bytes 656 | tf_op jit(solution)/shard_map/ppermute | solution.py:83
  132.6 18.2 %collective-permute-start.23 = (f32[8,768]{1,0:T(8,128)}, f32[8,768]{1,0:T(8,128)}, u32[]{:S(2)}, u32[]{:S(2)}) collective-permute-start(f32[8,768]{1,0:T(8,128)} %copy-done.4), channel_id=1, source_target_pairs={{0,4},{1,5},{2,6},{3,7},{4,8},{5,9},{6,10},{7,11},{8,12},{9,13},{1... | collective-permute-start | bytes 73736 | tf_op jit(solution)/shard_map/ppermute | solution.py:83
  134.9 16.0 %collective-permute-start.24 = (f32[8,768]{1,0:T(8,128)}, f32[8,768]{1,0:T(8,128)}, u32[]{:S(2)}, u32[]{:S(2)}) collective-permute-start(f32[8,768]{1,0:T(8,128)} %copy-done.3), channel_id=1, source_target_pairs={{4,0},{5,1},{6,2},{7,3},{8,4},{9,5},{10,6},{11,7},{12,8},{13,9},{1... | collective-permute-start | bytes 73736 | tf_op jit(solution)/shard_map/ppermute | solution.py:83
  152.6 8.3 %collective-permute-start.25 = (bf16[192,384]{1,0:T(8,128)(2,1)S(1)}, bf16[192,384]{1,0:T(8,128)(2,1)S(1)}, u32[]{:S(2)}, u32[]{:S(2)}) collective-permute-start(bf16[192,384]{1,0:T(8,128)(2,1)S(1)} %get-tuple-element.37), channel_id=1, source_target_pairs={{0,0},{2,1},{32,2},{34,3},{4,4},{6,5},{36,6},{38,7},{8,8},{10,9},{... | collective-permute-start | bytes 442376 | tf_op jit(solution)/shard_map/ppermute | solution.py:83
  156.4 6.0 %collective-permute-start.26 = (bf16[192,384]{1,0:T(8,128)(2,1)S(1)}, bf16[192,384]{1,0:T(8,128)(2,1)S(1)}, u32[]{:S(2)}, u32[]{:S(2)}) collective-permute-start(bf16[192,384]{1,0:T(8,128)(2,1)S(1)} %get-tuple-element.38), channel_id=1, source_target_pairs={{2,0},{0,1},{34,2},{32,3},{6,4},{4,5},{38,6},{36,7},{10,8},{8,9},{... | collective-permute-start | bytes 442376 | tf_op jit(solution)/shard_map/ppermute | solution.py:83
  156.5 7.4 %collective-permute-start.27 = (bf16[192,384]{1,0:T(8,128)(2,1)S(1)}, bf16[192,384]{1,0:T(8,128)(2,1)S(1)}, u32[]{:S(2)}, u32[]{:S(2)}) collective-permute-start(bf16[192,384]{1,0:T(8,128)(2,1)S(1)} %get-tuple-element.39), channel_id=1, source_target_pairs={{32,0},{34,1},{0,2},{2,3},{36,4},{38,5},{4,6},{6,7},{40,8},{42,9},... | collective-permute-start | bytes 442376 | tf_op jit(solution)/shard_map/ppermute | solution.py:83
  159.0 8.1 %collective-permute-start.28 = (bf16[192,384]{1,0:T(8,128)(2,1)S(1)}, bf16[192,384]{1,0:T(8,128)(2,1)S(1)}, u32[]{:S(2)}, u32[]{:S(2)}) collective-permute-start(bf16[192,384]{1,0:T(8,128)(2,1)S(1)} %get-tuple-element.40), channel_id=1, source_target_pairs={{34,0},{32,1},{2,2},{0,3},{38,4},{36,5},{6,6},{4,7},{42,8},{40,9},... | collective-permute-start | bytes 442376 | tf_op jit(solution)/shard_map/ppermute | solution.py:83

commit v3 on v2

--- a/solution.py
+++ b/solution.py
@@ -9,11 +9,11 @@
 from jax.sharding import PartitionSpec as P
 
 TIME_TILES = 4
-ROWS_PER_BRICK = 2
 AXES = ("seq", "head")
 FAR = -1e30
 VMEM_LIMIT = 40 * 2**20
 BATCH = 2
+EXTRA = 16
 
 
 def linear(y, xh, z, xl, core):
@@ -87,7 +87,7 @@
     width = outs[0].shape[-1]
     for k in range(4):
         lanes = pl.ds(pl.multiple_of((at_ref[0] ^ k) * width, 128), width)
-        outs[k][...] = qkv_ref[0, :, lanes]
+        outs[k][...] = qkv_ref[:, :, lanes]
         outs[4 + k][...] = qkv_ref[1:3, :, lanes]
 
 
@@ -95,7 +95,7 @@
     _, rows, columns = qkv.shape
     width = columns // 4
     vmem = pl.BlockSpec(memory_space=pltpu.VMEM)
-    shapes = [jax.ShapeDtypeStruct((rows, width), qkv.dtype)] * 4
+    shapes = [jax.ShapeDtypeStruct((3, rows, width), qkv.dtype)] * 4
     shapes += [jax.ShapeDtypeStruct((2, rows, width), qkv.dtype)] * 4
     return pl.pallas_call(
         split_kernel,
@@ -105,6 +105,68 @@
         compiler_params=pltpu.CompilerParams(vmem_limit_bytes=VMEM_LIMIT),
         name="split",
     )(at, qkv)
+
+
+def stack_kernel(*refs):
+    parts, q_ref, kv_ref, sems = refs[:4], refs[4], refs[5], refs[6]
+    rows = parts[0].shape[1]
+    copies = []
+    for k in range(4):
+        at = pl.ds(k * rows, rows)
+        copies.append(pltpu.make_async_copy(parts[k].at[0], q_ref.at[at], sems.at[k]))
+        copies.append(pltpu.make_async_copy(parts[k].at[pl.ds(1, 2)], kv_ref.at[:, at], sems.at[4 + k]))
+    for copy in copies:
+        copy.start()
+    for copy in copies:
+        copy.wait()
+
+
+def stack(parts):
+    _, rows, width = parts[0].shape
+    vmem = pl.BlockSpec(memory_space=pltpu.VMEM)
+    return pl.pallas_call(
+        stack_kernel,
+        out_shape=[
+            jax.ShapeDtypeStruct((4 * rows, width), parts[0].dtype),
+            jax.ShapeDtypeStruct((2, 4 * rows, width), parts[0].dtype),
+        ],
+        in_specs=[pl.BlockSpec(memory_space=pl.ANY)] * 4,
+        out_specs=[vmem] * 2,
+        scratch_shapes=[pltpu.SemaphoreType.DMA((8,))],
+        compiler_params=pltpu.CompilerParams(vmem_limit_bytes=VMEM_LIMIT),
+        name="stack",
+    )(*parts)
+
+
+def choose_kernel(high_ref, *refs):
+    parts, out_ref, sems = refs[:4], refs[4], refs[5]
+    rows = parts[0].shape[1]
+    for half in range(2):
+
+        @pl.when(high_ref[0] == half)
+        def _():
+            copies = []
+            for b in range(2):
+                into = out_ref.at[:, pl.ds(b * rows, rows)]
+                copies.append(pltpu.make_async_copy(parts[2 * half + b], into, sems.at[2 * half + b]))
+            for copy in copies:
+                copy.start()
+            for copy in copies:
+                copy.wait()
+
+
+def choose(high, parts):
+    _, rows, width = parts[0].shape
+    vmem = pl.BlockSpec(memory_space=pltpu.VMEM)
+    return pl.pallas_call(
+        choose_kernel,
+        out_shape=jax.ShapeDtypeStruct((2, 2 * rows, width), parts[0].dtype),
+        in_specs=[pl.BlockSpec(memory_space=pltpu.SMEM)] + [pl.BlockSpec(memory_space=pl.ANY)] * 4,
+        out_specs=vmem,
+        scratch_shapes=[pltpu.SemaphoreType.DMA((4,))],
+        compiler_params=pltpu.CompilerParams(vmem_limit_bytes=VMEM_LIMIT),
+        name="choose",
+    )(high, *parts)
 
 
 def join_kernel(at_ref, *refs):
@@ -132,9 +194,8 @@
     bodies = refs[sets : sets + 3]
     edges = refs[sets + 3 : sets + 6]
     outs = refs[sets + 6 : 2 * sets + 6]
-    lses = refs[2 * sets + 6 : 3 * sets + 6]
-    pool, held, turned_q, turned_v, max_ref, sum_ref, acc_ref, of_query, of_key = refs[3 * sets + 6 : 3 * sets + 15]
-    rest = refs[3 * sets + 15 :]
+    pool, held, turned_q, turned_v, max_ref, sum_ref, acc_ref, of_query, of_key = refs[2 * sets + 6 : 2 * sets + 15]
+    rest = refs[2 * sets + 15 :]
     score_refs = (rest[:BATCH], rest[BATCH : 2 * BATCH])
     top_refs = (rest[2 * BATCH : 3 * BATCH], rest[3 * BATCH : 4 * BATCH])
     sems = rest[4 * BATCH]
@@ -217,15 +278,20 @@
 
     lax.fori_loop(0, (count + 2 * BATCH - 1) // (2 * BATCH), step, 0)
 
+    width = heads * dim
     for n in range(sets):
-        lses[n][...] = jnp.zeros_like(lses[n])
+        outs[n][width : width + EXTRA, :] = jnp.zeros((EXTRA, 2 * tile), outs[n].dtype)
         for h in range(heads):
             for p in range(2):
                 s = (n * heads + h) * 2 + p
                 at = slice(p * tile, (p + 1) * tile)
                 total = jnp.maximum(jnp.sum(sum_ref[s], axis=0, keepdims=True), 1e-30)
                 outs[n][h * dim : (h + 1) * dim, at] = (acc_ref[s] / total).astype(outs[n].dtype)
-                lses[n][h : h + 1, at] = max_ref[s, :1, :] * scale + jnp.log(total)
+                left = max_ref[s, :1, :] * scale + jnp.log(total)
+                for i in range(3):
+                    part = left.astype(outs[n].dtype)
+                    outs[n][width + 3 * h + i : width + 3 * h + i + 1, at] = part
+                    left = left - part.astype(jnp.float32)
 
 
 def attend(mask, queries, bodies, edges, heads, out_dtype):
@@ -236,12 +302,11 @@
     count_q = sets * heads * 2
     hbm = pl.BlockSpec(memory_space=pl.ANY)
     vmem = pl.BlockSpec(memory_space=pltpu.VMEM)
-    outs = pl.pallas_call(
+    return pl.pallas_call(
         functools.partial(attend_kernel, sets=sets, heads=heads, tile=tile, dim=dim),
-        out_shape=[jax.ShapeDtypeStruct((width, brick), out_dtype)] * sets
-        + [jax.ShapeDtypeStruct((8, brick), jnp.float32)] * sets,
+        out_shape=[jax.ShapeDtypeStruct((width + EXTRA, brick), out_dtype)] * sets,
         in_specs=[pl.BlockSpec(memory_space=pltpu.SMEM)] + [hbm] * (sets + 6),
-        out_specs=[vmem] * (2 * sets),
+        out_specs=[vmem] * sets,
         scratch_shapes=[
             pltpu.VMEM((3, 2, 3 * tile, width), jnp.bfloat16),
             pltpu.VMEM((sets, brick, width), jnp.bfloat16),
@@ -259,60 +324,55 @@
         compiler_params=pltpu.CompilerParams(vmem_limit_bytes=VMEM_LIMIT),
         name=f"attend{sets}",
     )(mask, *queries, *bodies, *edges)
-    return outs[:sets], outs[sets:]
-
-
-def merge_kernel(valid_ref, own, before, after, own_lse, before_lse, after_lse, *outs, heads):
-    width, brick = own.shape
+
+
+def merge_kernel(valid_ref, *refs, heads):
+    parts, outs = refs[:3], refs[3:]
+    width, brick = parts[0].shape[0] - EXTRA, parts[0].shape[1]
     dim = width // heads
     quarter = brick // 4
-    lse = [
-        own_lse[...],
-        jnp.where(valid_ref[0] > 0, before_lse[...], FAR),
-        jnp.where(valid_ref[1] > 0, after_lse[...], FAR),
-    ]
-    top = jnp.maximum(jnp.maximum(lse[0], lse[1]), lse[2])
-    shares = [jnp.exp(x - top) for x in lse]
-    total = shares[0] + shares[1] + shares[2]
-    shares = [x / total for x in shares]
     for h in range(heads):
+        lse = []
+        for i in range(3):
+            rows = parts[i][width : width + EXTRA, :].astype(jnp.float32)
+            lse.append(rows[3 * h : 3 * h + 1] + rows[3 * h + 1 : 3 * h + 2] + rows[3 * h + 2 : 3 * h + 3])
+        lse[1] = jnp.where(valid_ref[0] > 0, lse[1], FAR)
+        lse[2] = jnp.where(valid_ref[1] > 0, lse[2], FAR)
+        top = jnp.maximum(jnp.maximum(lse[0], lse[1]), lse[2])
+        shares = [jnp.exp(x - top) for x in lse]
+        total = shares[0] + shares[1] + shares[2]
         lanes = slice(h * dim, (h + 1) * dim)
-        merged = own[lanes, :].astype(jnp.float32) * shares[0][h : h + 1, :]
-        merged += before[lanes, :].astype(jnp.float32) * shares[1][h : h + 1, :]
-        merged += after[lanes, :].astype(jnp.float32) * shares[2][h : h + 1, :]
+        merged = parts[0][lanes, :].astype(jnp.float32) * (shares[0] / total)
+        merged += parts[1][lanes, :].astype(jnp.float32) * (shares[1] / total)
+        merged += parts[2][lanes, :].astype(jnp.float32) * (shares[2] / total)
         merged = jnp.transpose(merged).astype(jnp.bfloat16)
         for k in range(4):
             outs[k][:, lanes] = merged[k * quarter : (k + 1) * quarter, :]
 
 
-def merge(valid, parts, lses, heads):
-    width, brick = parts[0].shape
+def merge(valid, parts, heads):
+    width, brick = parts[0].shape[0] - EXTRA, parts[0].shape[1]
     vmem = pl.BlockSpec(memory_space=pltpu.VMEM)
     return pl.pallas_call(
         functools.partial(merge_kernel, heads=heads),
         out_shape=[jax.ShapeDtypeStruct((brick // 4, width), jnp.bfloat16)] * 4,
-        in_specs=[pl.BlockSpec(memory_space=pltpu.SMEM)] + [vmem] * 6,
+        in_specs=[pl.BlockSpec(memory_space=pltpu.SMEM)] + [vmem] * 3,
         out_specs=[vmem] * 4,
         compiler_params=pltpu.CompilerParams(vmem_limit_bytes=VMEM_LIMIT),
         name="merge",
-    )(valid, *parts, *lses)
-
-
-def named(key_tiles, y, xh, z, xl):
-    pair = z // TIME_TILES
-    time = z % TIME_TILES
-    column = 2 * y + xh
-    tile_time = key_tiles // 2 % TIME_TILES
-    tile_pair = key_tiles // (2 * TIME_TILES) % 2
-    tile_column = key_tiles // (4 * TIME_TILES)
-    beside = jnp.where(tile_column == column + 1 - 2 * xh, 1, 2)
+    )(valid, *parts)
+
+
+def named(lists, column, pair, time, xh):
+    tile_time = lists // 2 % TIME_TILES
+    tile_pair = lists // (2 * TIME_TILES) % 2
+    tile_column = lists // (4 * TIME_TILES)
+    beside = jnp.where(tile_column == column + 1 - 2 * (column % 2), 1, 2)
     column_slot = jnp.where(tile_column == column, 0, beside)
-    row_slot = jnp.where(tile_pair == pair, (key_tiles % 2) ^ xl, 2)
-    slot = (tile_time - time + 1) * 9 + column_slot * 3 + row_slot
-    slot = jnp.where(key_tiles >= 0, slot, -1)
-    mask = jnp.any(slot[..., None] == jnp.arange(27, dtype=jnp.int32), axis=2)
-    mask = jnp.where(xl == 1, mask[:, ::-1], mask).astype(jnp.int32)
-    return mask[..., 0:9], mask[..., 9:18], mask[..., 18:27]
+    row_slot = jnp.where(tile_pair == pair, (lists % 2) ^ xh, 2)
+    slot = jnp.where((lists >= 0) & (tile_time == time), column_slot * 3 + row_slot, -1)
+    mask = jnp.any(slot[..., None] == jnp.arange(9, dtype=jnp.int32), axis=-2)
+    return jnp.where(xh == 1, mask[..., ::-1, :], mask)
 
 
 def local(qkv, key_tiles):
@@ -320,46 +380,41 @@
     seq = lax.axis_index("seq")
     head = lax.axis_index("head")
     y, xh, z = seq // 16, seq // 8 % 2, seq % 8
-    xl = head // 2
+    core = head % 2
     pair, time = z // TIME_TILES, z % TIME_TILES
     at = head.astype(jnp.int32).reshape(1)
-
-    early, same, late = named(key_tiles, y, xh, z, xl)
-    mask_own = send(same, list_pairs(0))
-    mask_next = send(early, list_pairs(-1))
-    mask_prev = send(late, list_pairs(1))
+    high = (pair ^ xh).astype(jnp.int32).reshape(1)
+    valid = jnp.stack([time > 0, time < TIME_TILES - 1])
+
+    lists = [send(key_tiles, list_pairs(by)) for by in (0, 1, -1)]
+    lists, qkv = lax.optimization_barrier((lists, qkv))
+    lists = jnp.stack(lists)
+    mask = named(lists, 2 * y + core, pair, time, xh)
+    here = jnp.concatenate([jnp.ones((1,), bool), valid])
+    mask = (mask & here[:, None, None, None]).astype(jnp.int32)
+    mask_own, mask_away = mask[0].reshape(-1), mask[1:].reshape(-1)
 
     pieces = split(at, qkv)
-    q_parts = [send(pieces[k], spread_pairs(k)) for k in range(4)]
-    kv_parts = [send(pieces[4 + k], spread_pairs(k)) for k in range(4)]
+    parts = [send(pieces[k], spread_pairs(k)) for k in range(4)]
     edge_parts = [send(pieces[4 + k], edge_pairs(k)) for k in range(4)]
 
-    q_own = jnp.concatenate(q_parts, axis=0)
+    q_own, kv_own = stack(parts)
     q_prev = send(q_own, time_pairs(1))
     q_next = send(q_own, time_pairs(-1))
-
-    kv_own = jnp.concatenate(kv_parts, axis=1)
     kv_core = send(kv_own, core_pairs())
     kv_column = send(kv_own, column_pairs())
-    low = (pair ^ xh) == 0
-    edge_own = jnp.concatenate(
-        [jnp.where(low, edge_parts[0], edge_parts[2]), jnp.where(low, edge_parts[1], edge_parts[3])], axis=1
-    )
+    edge_own = choose(high, edge_parts)
     edge_core = send(edge_own, core_pairs())
     edge_column = send(edge_own, column_pairs())
 
     bodies = (kv_own, kv_core, kv_column)
     edges = (edge_own, edge_core, edge_column)
-    mask_away = jnp.concatenate([mask_prev.reshape(-1), mask_next.reshape(-1)])
-    (o_prev, o_next), (l_prev, l_next) = attend(mask_away, (q_prev, q_next), bodies, edges, heads, jnp.bfloat16)
+    o_prev, o_next = attend(mask_away, (q_prev, q_next), bodies, edges, heads, jnp.bfloat16)
     o_before = send(o_next, time_pairs(1))
-    l_before = send(l_next, time_pairs(1))
     o_after = send(o_prev, time_pairs(-1))
-    l_after = send(l_prev, time_pairs(-1))
-    (o_own,), (l_own,) = attend(mask_own.reshape(-1), (q_own,), bodies, edges, heads, jnp.float32)
-
-    valid = jnp.stack([time > 0, time < TIME_TILES - 1]).astype(jnp.int32)
-    chunks = merge(valid, (o_own, o_before, o_after), (l_own, l_before, l_after), heads)
+    (o_own,) = attend(mask_own, (q_own,), bodies, edges, heads, jnp.float32)
+
+    chunks = merge(valid.astype(jnp.int32), (o_own, o_before, o_after), heads)
     home = [send(chunks[k], gather_pairs(k)) for k in range(4)]
     return join(at, home)
 

time: 169 us -> 170 us (level)
  the two profiles are of different devices: /device:TPU:177 before, /device:TPU:8 now
where the time goes in v3:
time: 170 us
  starting transfers between devices  94.7 us (56%)
  waiting for transfers between devices  45.2 us (27%)
  Pallas kernels  18.8 us (11%)
  local copies, waits for them, and re-layouts  9.42 us (6%)
    ppermute x23, starting transfers between devices, send(): return lax.ppermute(x, AXES, pairs)  94.7 us
    ppermute x23, waiting for transfers between devices, send(): return lax.ppermute(x, AXES, pairs)  45.2 us
    pallas_call x2, Pallas kernels, attend(): pl.pallas_call(functools.partial(attend_kernel, sets=sets, heads=heads, t...  12.9 us
    unnamed x12, local copies, waits for them, and re-layouts  5.65 us
    slice x4, local copies, waits for them, and re-layouts, local(): mask_own, mask_away = (mask[0].reshape(-1), mask[1:].reshape(-1))  3.59 us
  transfers between devices with their start and end apart: 23, of which 9 were waited for; matrix products, arithmetic and copies ran while one was open for 3% of the time, Pallas kernels for 5%

profile of v3, /device:TPU:8, one launch (start us, length us, event | category | flops | bytes accessed | tf_op | source)
XLA Modules:
  0.0 169.8 jit_solution(7702515872396868768)
XLA Ops:
  0.0 1.3 collective-permute-start
  1.3 1.3 collective-permute-start.2
  2.6 4.5 %collective-permute-start.1 = (s32[3,2,27]{2,1,0:T(2,128)}, s32[3,2,27]{2,1,0:T(2,128)S(1)}, u32[]{:S(2)}, u32[]{:S(2)}) collective-permute-start(s32[3,2,27]{2,1,0:T(2,128)} %param.3), channel_id=1, source_target_pairs={{0,4},{1,6},{2,36},{3,38},{4,8},{5,10},{6,40},{7,42},{8,12},{9,14}... | collective-permute-start | bytes 1952 | tf_op jit(solution)/shard_map/ppermute | solution.py:83
  7.2 1.5 collective-permute-done.1
  8.7 1.5 copy-done
  10.2 1.4 split.1
  11.5 1.3 collective-permute-start.9
  12.8 1.3 collective-permute-start.10
  14.1 0.7 collective-permute-start.11
  14.8 1.7 collective-permute-start.3
  16.5 21.9 %collective-permute-start.4 = (bf16[3,192,384]{2,1,0:T(8,128)(2,1)}, bf16[3,192,384]{2,1,0:T(8,128)(2,1)S(1)}, u32[]{:S(2)}, u32[]{:S(2)}) collective-permute-start(bf16[3,192,384]{2,1,0:T(8,128)(2,1)} %get-tuple-element.30), channel_id=1, source_target_pairs={{0,2},{1,0},{2,34},{3,32},{4,6},{5,4},{6,38},{7,36},{8,10},{9,8},{... | collective-permute-start | bytes 1327112 | tf_op jit(solution)/shard_map/ppermute | solution.py:83
  38.4 4.9 %collective-permute-start.6 = (bf16[3,192,384]{2,1,0:T(8,128)(2,1)}, bf16[3,192,384]{2,1,0:T(8,128)(2,1)S(1)}, u32[]{:S(2)}, u32[]{:S(2)}) collective-permute-start(bf16[3,192,384]{2,1,0:T(8,128)(2,1)} %get-tuple-element.32), channel_id=1, source_target_pairs={{0,34},{1,32},{2,2},{3,0},{4,38},{5,36},{6,6},{7,4},{8,42},{9,40},... | collective-permute-start | bytes 1327112 | tf_op jit(solution)/shard_map/ppermute | solution.py:83
  43.4 0.7 collective-permute-start.12
  44.1 0.1 choose.1.refs_4_.refs_5_
  44.3 2.4 %collective-permute-start.14 = (bf16[2,384,384]{2,1,0:T(8,128)(2,1)S(1)}, bf16[2,384,384]{2,1,0:T(8,128)(2,1)S(1)}, u32[]{:S(2)}, u32[]{:S(2)}) collective-permute-start(bf16[2,384,384]{2,1,0:T(8,128)(2,1)S(1)} %choose.1.refs_4_.refs_5_), channel_id=1, source_target_pairs={{1,64},{3,66},{5,68},{7,70},{9,72},{11,74},{13,76},{15,78},{17,80}... | collective-permute-start | bytes 1769480 | tf_op jit(solution)/shard_map/ppermute | solution.py:83
  46.7 5.9 %collective-permute-done.4.refs_1_ = bf16[3,192,384]{2,1,0:T(8,128)(2,1)S(1)} collective-permute-done((bf16[3,192,384]{2,1,0:T(8,128)(2,1)}, bf16[3,192,384]{2,1,0:T(8,128)(2,1)S(1)}, u32[]{:S(2)}, u32[]{:S(2)}) %collective-permute-start.4) | collective-permute-done | bytes 442400 | tf_op jit(solution)/shard_map/ppermute | solution.py:83
  52.6 12.3 %collective-permute-done.5.refs_2_ = bf16[3,192,384]{2,1,0:T(8,128)(2,1)S(1)} collective-permute-done((bf16[3,192,384]{2,1,0:T(8,128)(2,1)}, bf16[3,192,384]{2,1,0:T(8,128)(2,1)S(1)}, u32[]{:S(2)}, u32[]{:S(2)}) %collective-permute-start.5) | collective-permute-done | bytes 442400 | tf_op jit(solution)/shard_map/ppermute | solution.py:83
  64.9 0.8 copy-done.1
  65.6 0.8 copy-done.3
  66.4 1.0 copy-done.2
  67.4 1.0 copy-done.4
  68.4 1.8 %stack.29 = (bf16[768,384]{1,0:T(8,128)(2,1)}, bf16[2,768,384]{2,1,0:T(8,128)(2,1)S(1)}) custom-call(bf16[3,192,384]{2,1,0:T(8,128)(2,1)S(1)} %collective-permute-done.3.refs_0_, bf16[3,192,384]{2,1,0:T(8,128)(2,1)S(1)} %collective-permute-done.4.refs_1_, bf16[3,192,384]{2,1,0:T(8,128)(2,1)S(1)} %copy-done.2, bf16[3,192,384]{2,1,0:T(8,128)(2,1)S(1)} %copy-done.4), custom_call_target="tpu_custom_call" | custom-call | tf_op jit(solution)/shard_map/stack/pallas_call | solution.py:127
  70.2 1.9 %collective-permute-start.8 = (bf16[2,768,384]{2,1,0:T(8,128)(2,1)S(1)}, bf16[2,768,384]{2,1,0:T(8,128)(2,1)S(1)}, u32[]{:S(2)}, u32[]{:S(2)}) collective-permute-start(bf16[2,768,384]{2,1,0:T(8,128)(2,1)S(1)} %get-tuple-element.34.refs_1_.refs_2_), channel_id=1, source_target_pairs={{1,64},{3,66},{5,68},{7,70},{9,72},{11,74},{13,76},{15,78},{17,80}... | collective-permute-start | bytes 3538952 | tf_op jit(solution)/shard_map/ppermute | solution.py:83
  72.1 1.8 %collective-permute-start.7 = (bf16[2,768,384]{2,1,0:T(8,128)(2,1)S(1)}, bf16[2,768,384]{2,1,0:T(8,128)(2,1)}, u32[]{:S(2)}, u32[]{:S(2)}) collective-permute-start(bf16[2,768,384]{2,1,0:T(8,128)(2,1)S(1)} %get-tuple-element.34.refs_1_.refs_2_), channel_id=1, source_target_pairs={{0,1},{1,0},{2,3},{3,2},{4,5},{5,4},{6,7},{7,6},{8,9},{9,8},{10,11... | collective-permute-start | bytes 3538952 | tf_op jit(solution)/shard_map/ppermute | solution.py:83
  74.0 1.3 collective-permute-start.16
  75.3 13.3 %collective-permute-start.15 = (bf16[768,384]{1,0:T(8,128)(2,1)}, bf16[768,384]{1,0:T(8,128)(2,1)}, u32[]{:S(2)}, u32[]{:S(2)}) collective-permute-start(bf16[768,384]{1,0:T(8,128)(2,1)} %get-tuple-element.33.refs_0_), channel_id=1, source_target_pairs={{0,4},{1,5},{2,6},{3,7},{4,8},{5,9},{6,10},{7,11},{8,12},{9,13},{1... | collective-permute-start | bytes 1769480 | tf_op jit(solution)/shard_map/ppermute | solution.py:83
  88.6 0.1 and_select_fusion.4
  88.8 1.0 fusion
  89.8 0.6 copy-done.5
  90.5 0.6 slice.9
  91.1 0.9 copy.5
  92.0 8.0 %collective-permute-done.16.refs_1_ = bf16[768,384]{1,0:T(8,128)(2,1)} collective-permute-done((bf16[768,384]{1,0:T(8,128)(2,1)}, bf16[768,384]{1,0:T(8,128)(2,1)}, u32[]{:S(2)}, u32[]{:S(2)}) %collective-permute-start.16) | collective-permute-done | bytes 589856 | tf_op jit(solution)/shard_map/ppermute | solution.py:83
  100.0 1.2 collective-permute-done.15.refs_0_
  101.2 6.7 %attend2.1 = (bf16[400,768]{1,0:T(8,128)(2,1)}, bf16[400,768]{1,0:T(8,128)(2,1)}) custom-call(s32[108]{0:T(128)S(1)} %reshape.243.mask_ref, bf16[768,384]{1,0:T(8,128)(2,1)} %collective-permute-done.15.refs_0_, bf16[768,384]{1,0:T(8,128)(2,1)} %collective-permute-done.16.refs_1_, bf16[2,768,384]{2,1,0:T(8,128)(2,1)S(1)} %get-tuple-element.34.refs_1_.refs_2_, ...), custom_call_target="tpu_custom_call" | custom-call | tf_op jit(solution)/shard_map/attend2/pallas_call | solution.py:305
  107.9 6.2 %collective-permute-start.17 = (bf16[400,768]{1,0:T(8,128)(2,1)}, bf16[400,768]{1,0:T(8,128)(2,1)}, u32[]{:S(2)}, u32[]{:S(2)}) collective-permute-start(bf16[400,768]{1,0:T(8,128)(2,1)} %get-tuple-element.39), channel_id=1, source_target_pairs={{0,4},{1,5},{2,6},{3,7},{4,8},{5,9},{6,10},{7,11},{8,12},{9,13},{1... | collective-permute-start | bytes 1843208 | tf_op jit(solution)/shard_map/ppermute | solution.py:83
  114.1 1.3 collective-permute-start.18
  115.5 1.3 slice.8
  116.8 0.8 copy.4
  117.7 6.2 %attend1.1.refs_0_ = f32[400,768]{1,0:T(8,128)S(1)} custom-call(s32[54]{0:T(128)S(1)} %reshape_squeeze.3.mask_ref, bf16[768,384]{1,0:T(8,128)(2,1)} %get-tuple-element.33.refs_0_, bf16[2,768,384]{2,1,0:T(8,128)(2,1)S(1)} %get-tuple-element.34.refs_1_.refs_2_, bf16[2,768,384]{2,1,0:T(8,128)(2,1)} %collective-permute-done.7.refs_2_.refs_3_, ...), custom_call_target="tpu_custom_call" | custom-call | tf_op jit(solution)/shard_map/attend1/pallas_call | solution.py:305
  123.9 2.6 %collective-permute-done.17.refs_1_ = bf16[400,768]{1,0:T(8,128)(2,1)} collective-permute-done((bf16[400,768]{1,0:T(8,128)(2,1)}, bf16[400,768]{1,0:T(8,128)(2,1)}, u32[]{:S(2)}, u32[]{:S(2)}) %collective-permute-start.17) | collective-permute-done | bytes 614432 | tf_op jit(solution)/shard_map/ppermute | solution.py:83
  126.5 4.9 %collective-permute-done.18.refs_2_ = bf16[400,768]{1,0:T(8,128)(2,1)} collective-permute-done((bf16[400,768]{1,0:T(8,128)(2,1)}, bf16[400,768]{1,0:T(8,128)(2,1)}, u32[]{:S(2)}, u32[]{:S(2)}) %collective-permute-start.18) | collective-permute-done | bytes 614432 | tf_op jit(solution)/shard_map/ppermute | solution.py:83
  131.4 1.8 %merge.1 = (bf16[192,384]{1,0:T(8,128)(2,1)S(1)}, bf16[192,384]{1,0:T(8,128)(2,1)S(1)}, bf16[192,384]{1,0:T(8,128)(2,1)S(1)}, bf16[192,384]{1,0:T(8,128)(2,1)S(1)}) custom-call(s32[2]{0:T(128)S(1)} %add_convert_fusion.valid_ref, f32[400,768]{1,0:T(8,128)S(1)} %attend1.1.refs_0_, bf16[400,768]{1,0:T(8,128)(2,1)} %collective-permute-done.17.refs_1_, ...), custom_call_target="tpu_custom_call" | custom-call | tf_op jit(solution)/shard_map/merge/pallas_call | solution.py:356
  133.2 0.7 collective-permute-start.19
  133.8 24.3 %collective-permute-start.20 = (bf16[192,384]{1,0:T(8,128)(2,1)S(1)}, bf16[192,384]{1,0:T(8,128)(2,1)S(1)}, u32[]{:S(2)}, u32[]{:S(2)}) collective-permute-start(bf16[192,384]{1,0:T(8,128)(2,1)S(1)} %get-tuple-element.42), channel_id=1, source_target_pairs={{2,0},{0,1},{34,2},{32,3},{6,4},{4,5},{38,6},{36,7},{10,8},{8,9},{... | collective-permute-start | bytes 442376 | tf_op jit(solution)/shard_map/ppermute | solution.py:83
  158.2 1.9 %collective-permute-start.22 = (bf16[192,384]{1,0:T(8,128)(2,1)S(1)}, bf16[192,384]{1,0:T(8,128)(2,1)S(1)}, u32[]{:S(2)}, u32[]{:S(2)}) collective-permute-start(bf16[192,384]{1,0:T(8,128)(2,1)S(1)} %get-tuple-element.44), channel_id=1, source_target_pairs={{34,0},{32,1},{2,2},{0,3},{38,4},{36,5},{6,6},{4,7},{42,8},{40,9},... | collective-permute-start | bytes 442376 | tf_op jit(solution)/shard_map/ppermute | solution.py:83
  160.1 4.8 %collective-permute-done.21.refs_2_ = bf16[192,384]{1,0:T(8,128)(2,1)S(1)} collective-permute-done((bf16[192,384]{1,0:T(8,128)(2,1)S(1)}, bf16[192,384]{1,0:T(8,128)(2,1)S(1)}, u32[]{:S(2)}, u32[]{:S(2)}) %collective-permute-start.21) | collective-permute-done | bytes 147488 | tf_op jit(solution)/shard_map/ppermute | solution.py:83
  164.9 4.0 %collective-permute-done.22.refs_3_ = bf16[192,384]{1,0:T(8,128)(2,1)S(1)} collective-permute-done((bf16[192,384]{1,0:T(8,128)(2,1)S(1)}, bf16[192,384]{1,0:T(8,128)(2,1)S(1)}, u32[]{:S(2)}, u32[]{:S(2)}) %collective-permute-start.22) | collective-permute-done | bytes 147488 | tf_op jit(solution)/shard_map/ppermute | solution.py:83
  169.0 0.9 join.1
  (29 shorter events, 0.6 us)
Async XLA Ops:
  0.0 7.2 %collective-permute-start = (s32[3,2,27]{2,1,0:T(2,128)}, s32[3,2,27]{2,1,0:T(2,128)S(1)}, u32[]{:S(2)}, u32[]{:S(2)}) collective-permute-start(s32[3,2,27]{2,1,0:T(2,128)} %param.3), channel_id=1, source_target_pairs={{0,0},{1,2},{2,32},{3,34},{4,4},{5,6},{6,36},{7,38},{8,8},{9,10},{... | collective-permute-start | bytes 1952 | tf_op jit(solution)/shard_map/ppermute | solution.py:83
  1.3 5.9 %collective-permute-start.2 = (s32[3,2,27]{2,1,0:T(2,128)}, s32[3,2,27]{2,1,0:T(2,128)S(1)}, u32[]{:S(2)}, u32[]{:S(2)}) collective-permute-start(s32[3,2,27]{2,1,0:T(2,128)} %param.3), channel_id=1, source_target_pairs={{4,0},{5,2},{6,32},{7,34},{8,4},{9,6},{10,36},{11,38},{12,8},{13,1... | collective-permute-start | bytes 1952 | tf_op jit(solution)/shard_map/ppermute | solution.py:83
  2.6 6.1 %collective-permute-start.1 = (s32[3,2,27]{2,1,0:T(2,128)}, s32[3,2,27]{2,1,0:T(2,128)S(1)}, u32[]{:S(2)}, u32[]{:S(2)}) collective-permute-start(s32[3,2,27]{2,1,0:T(2,128)} %param.3), channel_id=1, source_target_pairs={{0,4},{1,6},{2,36},{3,38},{4,8},{5,10},{6,40},{7,42},{8,12},{9,14}... | collective-permute-start | bytes 1952 | tf_op jit(solution)/shard_map/ppermute | solution.py:83
  8.7 1.5 copy-start
  11.5 26.9 %collective-permute-start.9 = (bf16[2,192,384]{2,1,0:T(8,128)(2,1)S(1)}, bf16[2,192,384]{2,1,0:T(8,128)(2,1)S(1)}, u32[]{:S(2)}, u32[]{:S(2)}) collective-permute-start(bf16[2,192,384]{2,1,0:T(8,128)(2,1)S(1)} %get-tuple-element.35), channel_id=1, source_target_pairs={{2,48},{3,50},{6,52},{7,54},{10,56},{11,58},{14,60},{15,62},{16,0}... | collective-permute-start | bytes 884744 | tf_op jit(solution)/shard_map/ppermute | solution.py:83
  12.8 25.6 %collective-permute-start.10 = (bf16[2,192,384]{2,1,0:T(8,128)(2,1)S(1)}, bf16[2,192,384]{2,1,0:T(8,128)(2,1)S(1)}, u32[]{:S(2)}, u32[]{:S(2)}) collective-permute-start(bf16[2,192,384]{2,1,0:T(8,128)(2,1)S(1)} %get-tuple-element.36), channel_id=1, source_target_pairs={{2,50},{3,48},{6,54},{7,52},{10,58},{11,56},{14,62},{15,60},{16,2}... | collective-permute-start | bytes 884744 | tf_op jit(solution)/shard_map/ppermute | solution.py:83
  14.1 29.3 %collective-permute-start.11 = (bf16[2,192,384]{2,1,0:T(8,128)(2,1)S(1)}, bf16[2,192,384]{2,1,0:T(8,128)(2,1)S(1)}, u32[]{:S(2)}, u32[]{:S(2)}) collective-permute-start(bf16[2,192,384]{2,1,0:T(8,128)(2,1)S(1)} %get-tuple-element.37), channel_id=1, source_target_pairs={{2,16},{3,18},{6,20},{7,22},{10,24},{11,26},{14,28},{15,30},{16,32... | collective-permute-start | bytes 884744 | tf_op jit(solution)/shard_map/ppermute | solution.py:83
  14.8 31.9 %collective-permute-start.3 = (bf16[3,192,384]{2,1,0:T(8,128)(2,1)}, bf16[3,192,384]{2,1,0:T(8,128)(2,1)S(1)}, u32[]{:S(2)}, u32[]{:S(2)}) collective-permute-start(bf16[3,192,384]{2,1,0:T(8,128)(2,1)} %get-tuple-element.29), channel_id=1, source_target_pairs={{0,0},{1,2},{2,32},{3,34},{4,4},{5,6},{6,36},{7,38},{8,8},{9,10},{... | collective-permute-start | bytes 1327112 | tf_op jit(solution)/shard_map/ppermute | solution.py:83
  16.5 36.1 %collective-permute-start.4 = (bf16[3,192,384]{2,1,0:T(8,128)(2,1)}, bf16[3,192,384]{2,1,0:T(8,128)(2,1)S(1)}, u32[]{:S(2)}, u32[]{:S(2)}) collective-permute-start(bf16[3,192,384]{2,1,0:T(8,128)(2,1)} %get-tuple-element.30), channel_id=1, source_target_pairs={{0,2},{1,0},{2,34},{3,32},{4,6},{5,4},{6,38},{7,36},{8,10},{9,8},{... | collective-permute-start | bytes 1327112 | tf_op jit(solution)/shard_map/ppermute | solution.py:83
  38.4 26.4 %collective-permute-start.5 = (bf16[3,192,384]{2,1,0:T(8,128)(2,1)}, bf16[3,192,384]{2,1,0:T(8,128)(2,1)S(1)}, u32[]{:S(2)}, u32[]{:S(2)}) collective-permute-start(bf16[3,192,384]{2,1,0:T(8,128)(2,1)} %get-tuple-element.31), channel_id=1, source_target_pairs={{0,32},{1,34},{2,0},{3,2},{4,36},{5,38},{6,4},{7,6},{8,40},{9,42},... | collective-permute-start | bytes 1327112 | tf_op jit(solution)/shard_map/ppermute | solution.py:83
  38.4 27.2 %collective-permute-start.6 = (bf16[3,192,384]{2,1,0:T(8,128)(2,1)}, bf16[3,192,384]{2,1,0:T(8,128)(2,1)S(1)}, u32[]{:S(2)}, u32[]{:S(2)}) collective-permute-start(bf16[3,192,384]{2,1,0:T(8,128)(2,1)} %get-tuple-element.32), channel_id=1, source_target_pairs={{0,34},{1,32},{2,2},{3,0},{4,38},{5,36},{6,6},{7,4},{8,42},{9,40},... | collective-permute-start | bytes 1327112 | tf_op jit(solution)/shard_map/ppermute | solution.py:83
  43.4 0.8 collective-permute-start.12
  44.3 31.0 %collective-permute-start.14 = (bf16[2,384,384]{2,1,0:T(8,128)(2,1)S(1)}, bf16[2,384,384]{2,1,0:T(8,128)(2,1)S(1)}, u32[]{:S(2)}, u32[]{:S(2)}) collective-permute-start(bf16[2,384,384]{2,1,0:T(8,128)(2,1)S(1)} %choose.1.refs_4_.refs_5_), channel_id=1, source_target_pairs={{1,64},{3,66},{5,68},{7,70},{9,72},{11,74},{13,76},{15,78},{17,80}... | collective-permute-start | bytes 1769480 | tf_op jit(solution)/shard_map/ppermute | solution.py:83
  64.9 0.8 copy-start.1
  65.6 0.8 copy-start.3
  66.4 1.0 copy-start.2
  67.4 1.0 copy-start.4
  70.2 31.0 %collective-permute-start.8 = (bf16[2,768,384]{2,1,0:T(8,128)(2,1)S(1)}, bf16[2,768,384]{2,1,0:T(8,128)(2,1)S(1)}, u32[]{:S(2)}, u32[]{:S(2)}) collective-permute-start(bf16[2,768,384]{2,1,0:T(8,128)(2,1)S(1)} %get-tuple-element.34.refs_1_.refs_2_), channel_id=1, source_target_pairs={{1,64},{3,66},{5,68},{7,70},{9,72},{11,74},{13,76},{15,78},{17,80}... | collective-permute-start | bytes 3538952 | tf_op jit(solution)/shard_map/ppermute | solution.py:83
  72.1 29.1 %collective-permute-start.7 = (bf16[2,768,384]{2,1,0:T(8,128)(2,1)S(1)}, bf16[2,768,384]{2,1,0:T(8,128)(2,1)}, u32[]{:S(2)}, u32[]{:S(2)}) collective-permute-start(bf16[2,768,384]{2,1,0:T(8,128)(2,1)S(1)} %get-tuple-element.34.refs_1_.refs_2_), channel_id=1, source_target_pairs={{0,1},{1,0},{2,3},{3,2},{4,5},{5,4},{6,7},{7,6},{8,9},{9,8},{10,11... | collective-permute-start | bytes 3538952 | tf_op jit(solution)/shard_map/ppermute | solution.py:83
  73.9 18.1 %collective-permute-start.13 = (bf16[2,384,384]{2,1,0:T(8,128)(2,1)S(1)}, bf16[2,384,384]{2,1,0:T(8,128)(2,1)}, u32[]{:S(2)}, u32[]{:S(2)}) collective-permute-start(bf16[2,384,384]{2,1,0:T(8,128)(2,1)S(1)} %choose.1.refs_4_.refs_5_), channel_id=1, source_target_pairs={{0,1},{1,0},{2,3},{3,2},{4,5},{5,4},{6,7},{7,6},{8,9},{9,8},{10,11... | collective-permute-start | bytes 1769480 | tf_op jit(solution)/shard_map/ppermute | solution.py:83
  74.0 26.0 %collective-permute-start.16 = (bf16[768,384]{1,0:T(8,128)(2,1)}, bf16[768,384]{1,0:T(8,128)(2,1)}, u32[]{:S(2)}, u32[]{:S(2)}) collective-permute-start(bf16[768,384]{1,0:T(8,128)(2,1)} %get-tuple-element.33.refs_0_), channel_id=1, source_target_pairs={{4,0},{5,1},{6,2},{7,3},{8,4},{9,5},{10,6},{11,7},{12,8},{13,9},{1... | collective-permute-start | bytes 1769480 | tf_op jit(solution)/shard_map/ppermute | solution.py:83
  75.3 25.9 %collective-permute-start.15 = (bf16[768,384]{1,0:T(8,128)(2,1)}, bf16[768,384]{1,0:T(8,128)(2,1)}, u32[]{:S(2)}, u32[]{:S(2)}) collective-permute-start(bf16[768,384]{1,0:T(8,128)(2,1)} %get-tuple-element.33.refs_0_), channel_id=1, source_target_pairs={{0,4},{1,5},{2,6},{3,7},{4,8},{5,9},{6,10},{7,11},{8,12},{9,13},{1... | collective-permute-start | bytes 1769480 | tf_op jit(solution)/shard_map/ppermute | solution.py:83
  89.8 0.6 copy-start.5
  107.9 18.6 %collective-permute-start.17 = (bf16[400,768]{1,0:T(8,128)(2,1)}, bf16[400,768]{1,0:T(8,128)(2,1)}, u32[]{:S(2)}, u32[]{:S(2)}) collective-permute-start(bf16[400,768]{1,0:T(8,128)(2,1)} %get-tuple-element.39), channel_id=1, source_target_pairs={{0,4},{1,5},{2,6},{3,7},{4,8},{5,9},{6,10},{7,11},{8,12},{9,13},{1... | collective-permute-start | bytes 1843208 | tf_op jit(solution)/shard_map/ppermute | solution.py:83
  114.1 17.3 %collective-permute-start.18 = (bf16[400,768]{1,0:T(8,128)(2,1)}, bf16[400,768]{1,0:T(8,128)(2,1)}, u32[]{:S(2)}, u32[]{:S(2)}) collective-permute-start(bf16[400,768]{1,0:T(8,128)(2,1)} %get-tuple-element.40), channel_id=1, source_target_pairs={{4,0},{5,1},{6,2},{7,3},{8,4},{9,5},{10,6},{11,7},{12,8},{13,9},{1... | collective-permute-start | bytes 1843208 | tf_op jit(solution)/shard_map/ppermute | solution.py:83
  133.2 26.9 %collective-permute-start.19 = (bf16[192,384]{1,0:T(8,128)(2,1)S(1)}, bf16[192,384]{1,0:T(8,128)(2,1)S(1)}, u32[]{:S(2)}, u32[]{:S(2)}) collective-permute-start(bf16[192,384]{1,0:T(8,128)(2,1)S(1)} %get-tuple-element.41), channel_id=1, source_target_pairs={{0,0},{2,1},{32,2},{34,3},{4,4},{6,5},{36,6},{38,7},{8,8},{10,9},{... | collective-permute-start | bytes 442376 | tf_op jit(solution)/shard_map/ppermute | solution.py:83
  133.8 26.3 %collective-permute-start.20 = (bf16[192,384]{1,0:T(8,128)(2,1)S(1)}, bf16[192,384]{1,0:T(8,128)(2,1)S(1)}, u32[]{:S(2)}, u32[]{:S(2)}) collective-permute-start(bf16[192,384]{1,0:T(8,128)(2,1)S(1)} %get-tuple-element.42), channel_id=1, source_target_pairs={{2,0},{0,1},{34,2},{32,3},{6,4},{4,5},{38,6},{36,7},{10,8},{8,9},{... | collective-permute-start | bytes 442376 | tf_op jit(solution)/shard_map/ppermute | solution.py:83
  158.2 6.8 %collective-permute-start.21 = (bf16[192,384]{1,0:T(8,128)(2,1)S(1)}, bf16[192,384]{1,0:T(8,128)(2,1)S(1)}, u32[]{:S(2)}, u32[]{:S(2)}) collective-permute-start(bf16[192,384]{1,0:T(8,128)(2,1)S(1)} %get-tuple-element.43), channel_id=1, source_target_pairs={{32,0},{34,1},{0,2},{2,3},{36,4},{38,5},{4,6},{6,7},{40,8},{42,9},... | collective-permute-start | bytes 442376 | tf_op jit(solution)/shard_map/ppermute | solution.py:83
  158.2 10.8 %collective-permute-start.22 = (bf16[192,384]{1,0:T(8,128)(2,1)S(1)}, bf16[192,384]{1,0:T(8,128)(2,1)S(1)}, u32[]{:S(2)}, u32[]{:S(2)}) collective-permute-start(bf16[192,384]{1,0:T(8,128)(2,1)S(1)} %get-tuple-element.44), channel_id=1, source_target_pairs={{34,0},{32,1},{2,2},{0,3},{38,4},{36,5},{6,6},{4,7},{42,8},{40,9},... | collective-permute-start | bytes 442376 | tf_op jit(solution)/shard_map/ppermute | solution.py:83

commit v4 on v3

v4 whole, which is shorter than its diff:
```python
import functools
import math

import jax
import jax.numpy as jnp
from jax import lax
from jax.experimental import pallas as pl
from jax.experimental.pallas import tpu as pltpu
from jax.sharding import PartitionSpec as P

TIME_TILES = 4
AXES = ("seq", "head")
FAR = -1e30
VMEM_LIMIT = 40 * 2**20
BATCH = 2
EXTRA = 16
POOL = 9


def linear(y, xh, z, xl, core):
    return ((y * 2 + xh) * 8 + z) * 4 + xl * 2 + core


def devices():
    for y in range(4):
        for xh in range(2):
            for z in range(8):
                for xl in range(2):
                    for core in range(2):
                        yield y, xh, z, xl, core


def spread_pairs(k):
    pairs = []
    for y, xh, z, xl, core in devices():
        group = (2 * xl + core) ^ k
        pairs.append((linear(y, xh, z, xl, core), linear(y, group >> 1, z, group & 1, xh)))
    return pairs


def gather_pairs(k):
    return [(b, a) for a, b in spread_pairs(k)]


def edge_pairs():
    return [(linear(y, xh, z, xl, c), linear(y, xh, z ^ 4, xl, c)) for y, xh, z, xl, c in devices()]


def core_pairs():
    return [(linear(y, xh, z, xl, c), linear(y, xh, z, xl, 1 - c)) for y, xh, z, xl, c in devices()]


def column_pairs():
    pairs = []
    for y, xh, z, xl, core in devices():
        to = y + (1 if core == 1 else -1)
        if 0 <= to < 4:
            pairs.append((linear(y, xh, z, xl, core), linear(to, xh, z, xl, 1 - core)))
    return pairs


def time_pairs(by):
    pairs = []
    for y, xh, z, xl, core in devices():
        if 0 <= z % TIME_TILES + by < TIME_TILES:
            pairs.append((linear(y, xh, z, xl, core), linear(y, xh, z + by, xl, core)))
    return pairs


def list_pairs(by):
    pairs = []
    for y, xh, z, xl, core in devices():
        if 0 <= z % TIME_TILES + by < TIME_TILES:
            pairs.append((linear(y, xh, z, xl, core), linear(y, xl, z + by, core, xh)))
    return pairs


def send(x, pairs):
    return lax.ppermute(x, AXES, pairs)


def split_kernel(at_ref, qkv_ref, *refs):
    outs, sems = refs[:8], refs[8]
    width = outs[0].shape[-1]
    copies = []
    for k in range(4):
        lanes = pl.ds(pl.multiple_of((at_ref[0] ^ k) * width, 128), width)
        copies.append(pltpu.make_async_copy(qkv_ref.at[0, :, lanes], outs[k], sems.at[k]))
    for copy in copies:
        copy.start()
    for k in range(4):
        lanes = pl.ds(pl.multiple_of((at_ref[0] ^ k) * width, 128), width)
        outs[4 + k][...] = qkv_ref[1:3, :, lanes]
    for copy in copies:
        copy.wait()


def split(at, qkv):
    _, rows, columns = qkv.shape
    width = columns // 4
    vmem = pl.BlockSpec(memory_space=pltpu.VMEM)
    shapes = [jax.ShapeDtypeStruct((rows, width), qkv.dtype)] * 4
    shapes += [jax.ShapeDtypeStruct((2, rows, width), qkv.dtype)] * 4
    return pl.pallas_call(
        split_kernel,
        out_shape=shapes,
        in_specs=[pl.BlockSpec(memory_space=pltpu.SMEM), vmem],
        out_specs=[pl.BlockSpec(memory_space=pl.ANY)] * 4 + [vmem] * 4,
        scratch_shapes=[pltpu.SemaphoreType.DMA((4,))],
        compiler_params=pltpu.CompilerParams(vmem_limit_bytes=VMEM_LIMIT),
        name="split",
    )(at, qkv)


def stack_kernel(place_ref, *refs):
    parts, kv_ref, edge_ref, sems = refs[:4], refs[4], refs[5], refs[6]
    rows = parts[0].shape[1]
    copies = []
    for k in range(4):
        copies.append(pltpu.make_async_copy(parts[k], kv_ref.at[:, pl.ds(k * rows, rows)], sems.at[k]))
    for copy in copies:
        copy.start()
    for copy in copies:
        copy.wait()
    edge_ref[...] = kv_ref[:, pl.ds(pl.multiple_of(place_ref[0] * (2 * rows), 128), 2 * rows), :]


def stack(place, parts):
    _, rows, width = parts[0].shape
    vmem = pl.BlockSpec(memory_space=pltpu.VMEM)
    return pl.pallas_call(
        stack_kernel,
        out_shape=[
            jax.ShapeDtypeStruct((2, 4 * rows, width), parts[0].dtype),
            jax.ShapeDtypeStruct((2, 2 * rows, width), parts[0].dtype),
        ],
        in_specs=[pl.BlockSpec(memory_space=pltpu.SMEM)] + [pl.BlockSpec(memory_space=pl.ANY)] * 4,
        out_specs=[vmem] * 2,
        scratch_shapes=[pltpu.SemaphoreType.DMA((4,))],
        compiler_params=pltpu.CompilerParams(vmem_limit_bytes=VMEM_LIMIT),
        name="stack",
    )(place, *parts)


def stack_queries_kernel(*refs):
    parts, q_ref, sems = refs[:4], refs[4], refs[5]
    rows = parts[0].shape[0]
    copies = []
    for k in range(4):
        copies.append(pltpu.make_async_copy(parts[k], q_ref.at[pl.ds(k * rows, rows)], sems.at[k]))
    for copy in copies:
        copy.start()
    for copy in copies:
        copy.wait()


def stack_queries(parts):
    rows, width = parts[0].shape
    return pl.pallas_call(
        stack_queries_kernel,
        out_shape=jax.ShapeDtypeStruct((4 * rows, width), parts[0].dtype),
        in_specs=[pl.BlockSpec(memory_space=pl.ANY)] * 4,
        out_specs=pl.BlockSpec(memory_space=pltpu.VMEM),
        scratch_shapes=[pltpu.SemaphoreType.DMA((4,))],
        compiler_params=pltpu.CompilerParams(vmem_limit_bytes=VMEM_LIMIT),
        name="stack_queries",
    )(*parts)


def join_kernel(at_ref, *refs):
    parts, out_ref = refs[:4], refs[4]
    width = parts[0].shape[-1]
    for k in range(4):
        out_ref[:, pl.ds(pl.multiple_of((at_ref[0] ^ k) * width, 128), width)] = parts[k][...]


def join(at, parts):
    rows, width = parts[0].shape
    vmem = pl.BlockSpec(memory_space=pltpu.VMEM)
    return pl.pallas_call(
        join_kernel,
        out_shape=jax.ShapeDtypeStruct((rows, 4 * width), parts[0].dtype),
        in_specs=[pl.BlockSpec(memory_space=pltpu.SMEM)] + [vmem] * 4,
        out_specs=vmem,
        compiler_params=pltpu.CompilerParams(vmem_limit_bytes=VMEM_LIMIT),
        name="join",
    )(at, *parts)


def attend_kernel(mask_ref, *refs, sets, tiles, first_set, first_tile, heads, tile, dim):
    pieces = 3 if tiles != POOL else 6
    queries = refs[:sets]
    sources = refs[sets : sets + pieces]
    refs = refs[sets + pieces :]
    outs = refs[:sets]
    pool, held, turned_q, turned_v, max_ref, sum_ref, acc_ref, of_query, of_key = refs[sets : sets + 9]
    rest = refs[sets + 9 :]
    score_refs = (rest[:BATCH], rest[BATCH : 2 * BATCH])
    top_refs = (rest[2 * BATCH : 3 * BATCH], rest[3 * BATCH : 4 * BATCH])
    sems = rest[4 * BATCH]
    count_q = sets * heads * 2

    copies = []
    for n in range(sets):
        copies.append(pltpu.make_async_copy(queries[n], held.at[n], sems.at[n]))
    at = 0
    for source in sources:
        for r in range(source.shape[1] // tile):
            copies.append(
                pltpu.make_async_copy(source.at[:, pl.ds(r * tile, tile)], pool.at[at], sems.at[sets + at])
            )
            at += 1
    for copy in copies:
        copy.start()

    def list_pairs_of(s, count):
        for j in range(tiles):
            of_query[count] = s
            of_key[count] = j
            count = count + mask_ref[(first_set * heads * 2 + s) * POOL + first_tile + j]
        return count

    count = lax.fori_loop(0, count_q, list_pairs_of, 0)
    for i in range(4 * BATCH):
        of_query[count + i] = count_q
        of_key[count + i] = 0
    max_ref[...] = jnp.full_like(max_ref, FAR)
    sum_ref[...] = jnp.zeros_like(sum_ref)
    acc_ref[...] = jnp.zeros_like(acc_ref)
    for copy in copies:
        copy.wait()
    for n in range(sets):
        for h in range(heads):
            for p in range(2):
                turned_q[(n * heads + h) * 2 + p] = jnp.transpose(
                    held[n, p * tile : (p + 1) * tile, h * dim : (h + 1) * dim]
                )
    turned_q[count_q] = turned_q[0]
    for h in range(heads):
        for j in range(tiles):
            turned_v[h * tiles + j] = jnp.transpose(pool[j, 1, :, h * dim : (h + 1) * dim])

    scale = dim**-0.5
    factor = scale * math.log2(math.e)

    def score(i, out_ref, top_ref):
        s, j = of_query[i], of_key[i]
        h = lax.rem(s // 2, heads)
        keys = pool[j, 0, :, pl.ds(pl.multiple_of(h * dim, dim), dim)]
        scores = jnp.dot(keys, turned_q[s], preferred_element_type=jnp.float32)
        out_ref[...] = scores
        top_ref[...] = jnp.max(scores.reshape(tile // 8, 8, tile), axis=0)

    def weigh(i, in_ref, top_ref):
        s, j = of_query[i], of_key[i]
        h = lax.rem(s // 2, heads)
        old = max_ref[s, :1, :]
        new = jnp.maximum(old, jnp.max(top_ref[...], axis=0, keepdims=True))
        shrink = jnp.exp2((old - new) * factor)
        max_ref[s, :1, :] = new
        weights = jnp.exp2((in_ref[...] - new) * factor)
        sum_ref[s] = sum_ref[s] * shrink + jnp.sum(weights.reshape(tile // 8, 8, tile), axis=0)
        acc_ref[s] = acc_ref[s] * shrink + jnp.dot(
            turned_v[h * tiles + j], weights.astype(jnp.bfloat16), preferred_element_type=jnp.float32
        )

    for u in range(BATCH):
        score(u, score_refs[0][u], top_refs[0][u])

    def step(t, carry):
        for half in range(2):
            base = (2 * t + half) * BATCH
            for u in range(BATCH):
                score(base + BATCH + u, score_refs[1 - half][u], top_refs[1 - half][u])
            for u in range(BATCH):
                weigh(base + u, score_refs[half][u], top_refs[half][u])
        return carry

    lax.fori_loop(0, (count + 2 * BATCH - 1) // (2 * BATCH), step, 0)

    width = heads * dim
    for n in range(sets):
        outs[n][width : width + EXTRA, :] = jnp.zeros((EXTRA, 2 * tile), outs[n].dtype)
        for h in range(heads):
            for p in range(2):
                s = (n * heads + h) * 2 + p
                at = slice(p * tile, (p + 1) * tile)
                total = jnp.maximum(jnp.sum(sum_ref[s], axis=0, keepdims=True), 1e-30)
                outs[n][h * dim : (h + 1) * dim, at] = (acc_ref[s] / total).astype(outs[n].dtype)
                left = max_ref[s, :1, :] * scale + jnp.log(total)
                for i in range(3):
                    part = left.astype(outs[n].dtype)
                    outs[n][width + 3 * h + i : width + 3 * h + i + 1, at] = part
                    left = left - part.astype(jnp.float32)


def attend(mask, queries, sources, heads, first_set, first_tile, out_dtype):
    sets = len(queries)
    brick, width = queries[0].shape
    tile = brick // 2
    dim = width // heads
    tiles = sum(source.shape[1] for source in sources) // tile
    count_q = sets * heads * 2
    hbm = pl.BlockSpec(memory_space=pl.ANY)
    vmem = pl.BlockSpec(memory_space=pltpu.VMEM)
    return pl.pallas_call(
        functools.partial(
            attend_kernel,
            sets=sets,
            tiles=tiles,
            first_set=first_set,
            first_tile=first_tile,
            heads=heads,
            tile=tile,
            dim=dim,
        ),
        out_shape=[jax.ShapeDtypeStruct((width + EXTRA, brick), out_dtype)] * sets,
        in_specs=[pl.BlockSpec(memory_space=pltpu.SMEM)] + [hbm] * (sets + len(sources)),
        out_specs=[vmem] * sets,
        scratch_shapes=[
            pltpu.VMEM((tiles, 2, tile, width), jnp.bfloat16),
            pltpu.VMEM((sets, brick, width), jnp.bfloat16),
            pltpu.VMEM((count_q + 1, dim, tile), jnp.bfloat16),
            pltpu.VMEM((tiles * heads, dim, tile), jnp.bfloat16),
            pltpu.VMEM((count_q + 1, 8, tile), jnp.float32),
            pltpu.VMEM((count_q + 1, 8, tile), jnp.float32),
            pltpu.VMEM((count_q + 1, dim, tile), jnp.float32),
            pltpu.SMEM((count_q * tiles + 8 * BATCH,), jnp.int32),
            pltpu.SMEM((count_q * tiles + 8 * BATCH,), jnp.int32),
        ]
        + [pltpu.VMEM((tile, tile), jnp.float32)] * (2 * BATCH)
        + [pltpu.VMEM((8, tile), jnp.float32)] * (2 * BATCH)
        + [pltpu.SemaphoreType.DMA((sets + tiles,))],
        compiler_params=pltpu.CompilerParams(vmem_limit_bytes=VMEM_LIMIT),
        name=f"attend_{sets}_{tiles}",
    )(mask, *queries, *sources)


def merge_kernel(valid_ref, *refs, heads):
    parts, outs = refs[:4], refs[4:]
    width, brick = parts[0].shape[0] - EXTRA, parts[0].shape[1]
    dim = width // heads
    quarter = brick // 4
    for h in range(heads):
        lse = []
        for i in range(4):
            rows = parts[i][width : width + EXTRA, :].astype(jnp.float32)
            lse.append(rows[3 * h : 3 * h + 1] + rows[3 * h + 1 : 3 * h + 2] + rows[3 * h + 2 : 3 * h + 3])
        lse[2] = jnp.where(valid_ref[0] > 0, lse[2], FAR)
        lse[3] = jnp.where(valid_ref[1] > 0, lse[3], FAR)
        top = jnp.maximum(jnp.maximum(lse[0], lse[1]), jnp.maximum(lse[2], lse[3]))
        shares = [jnp.exp(x - top) for x in lse]
        total = shares[0] + shares[1] + shares[2] + shares[3]
        lanes = slice(h * dim, (h + 1) * dim)
        merged = parts[0][lanes, :].astype(jnp.float32) * (shares[0] / total)
        merged += parts[1][lanes, :].astype(jnp.float32) * (shares[1] / total)
        merged += parts[2][lanes, :].astype(jnp.float32) * (shares[2] / total)
        merged += parts[3][lanes, :].astype(jnp.float32) * (shares[3] / total)
        merged = jnp.transpose(merged).astype(jnp.bfloat16)
        for k in range(4):
            outs[k][:, lanes] = merged[k * quarter : (k + 1) * quarter, :]


def merge(valid, parts, heads):
    width, brick = parts[0].shape[0] - EXTRA, parts[0].shape[1]
    vmem = pl.BlockSpec(memory_space=pltpu.VMEM)
    return pl.pallas_call(
        functools.partial(merge_kernel, heads=heads),
        out_shape=[jax.ShapeDtypeStruct((brick // 4, width), jnp.bfloat16)] * 4,
        in_specs=[pl.BlockSpec(memory_space=pltpu.SMEM)] + [vmem] * 4,
        out_specs=[vmem] * 4,
        compiler_params=pltpu.CompilerParams(vmem_limit_bytes=VMEM_LIMIT),
        name="merge",
    )(valid, *parts)


def named(lists, column, pair, time, xh):
    tile_time = lists // 2 % TIME_TILES
    tile_pair = lists // (2 * TIME_TILES) % 2
    tile_column = lists // (4 * TIME_TILES)
    beside = jnp.where(tile_column == column + 1 - 2 * (column % 2), 1, 2)
    column_slot = jnp.where(tile_column == column, 0, beside)
    slot = jnp.where(tile_pair == pair, column_slot * 2 + ((lists % 2) ^ xh), 6 + column_slot)
    slot = jnp.where((lists >= 0) & (tile_time == time), slot, -1)
    mask = jnp.any(slot[..., None] == jnp.arange(POOL, dtype=jnp.int32), axis=-2)
    return jnp.where(xh == 1, mask[..., ::-1, :], mask)


def local(qkv, key_tiles):
    heads = key_tiles.shape[0]
    seq = lax.axis_index("seq")
    head = lax.axis_index("head")
    y, xh, z = seq // 16, seq // 8 % 2, seq % 8
    core = head % 2
    pair, time = z // TIME_TILES, z % TIME_TILES
    at = head.astype(jnp.int32).reshape(1)
    place = ((1 - pair) ^ xh).astype(jnp.int32).reshape(1)
    valid = jnp.stack([time > 0, time < TIME_TILES - 1])

    lists = [send(key_tiles, list_pairs(by)) for by in (0, 1, -1)]
    lists, qkv = lax.optimization_barrier((lists, qkv))
    lists = jnp.stack(lists)
    mask = named(lists, 2 * y + core, pair, time, xh)
    here = jnp.concatenate([jnp.ones((1,), bool), valid])
    mask = (mask & here[:, None, None, None]).astype(jnp.int32).reshape(-1)

    pieces = split(at, qkv)
    kv_parts = [send(pieces[4 + k], spread_pairs(k)) for k in range(4)]
    kv_parts[0], q_pieces = lax.optimization_barrier((kv_parts[0], pieces[:4]))
    q_parts = [send(q_pieces[k], spread_pairs(k)) for k in range(4)]
    kv_own, edge = stack(place, kv_parts)
    kv_core = send(kv_own, core_pairs())
    kv_column = send(kv_own, column_pairs())
    edge_own = send(edge, edge_pairs())
    q_own = stack_queries(q_parts)
    q_prev = send(q_own, time_pairs(1))
    q_next = send(q_own, time_pairs(-1))

    bodies = (kv_own, kv_core, kv_column)
    (o_body,) = attend(mask, (q_own,), bodies, heads, 0, 0, jnp.float32)
    o_body, edge_own = lax.optimization_barrier((o_body, edge_own))
    edges = (edge_own, send(edge_own, core_pairs()), send(edge_own, column_pairs()))
    o_prev, o_next = attend(mask, (q_prev, q_next), bodies + edges, heads, 1, 0, jnp.bfloat16)
    o_before = send(o_next, time_pairs(1))
    o_after = send(o_prev, time_pairs(-1))
    (o_edge,) = attend(mask, (q_own,), edges, heads, 0, 6, jnp.float32)

    chunks = merge(valid.astype(jnp.int32), (o_body, o_edge, o_before, o_after), heads)
    home = [send(chunks[k], gather_pairs(k)) for k in range(4)]
    return join(at, home)


def solution(mesh):
    placed = (P(None, ("seq", "head"), None), P("head", "seq", None))
    return jax.shard_map(
        local, mesh=mesh, in_specs=placed, out_specs=P(("seq", "head"), None), check_vma=False
    )
```

time: 170 us -> 147 us (0.86); the launches traced: 170 us -> 150 us
  starting transfers between devices: 94.7 us -> 80.4 us
  local copies, waits for them, and re-layouts: 9.42 us -> 4.33 us
    ppermute x23 -> x24, starting transfers between devices: 94.7 us -> 80.4 us  [send(): return lax.ppermute(x, AXES, pairs)]
    slice x4 -> x0, local copies, waits for them, and re-layouts: 3.59 us -> none  [local(): mask_own, mask_away = (mask[0].reshape(-1), mask[1:].reshape(-1))]
    unnamed x12 -> x10, local copies, waits for them, and re-layouts: 5.65 us -> 4.09 us
    ppermute x23 -> x24, waiting for transfers between devices: 45.2 us -> 44 us  [send(): return lax.ppermute(x, AXES, pairs)]
    pallas_call x4 -> x5, Pallas kernels: 14.8 us -> 15.6 us  [the longest x3 13.4 us: attend(): pl.pallas_call(functools.partial(attend_kernel, sets=sets, tiles=tiles, f...]
  transfers between devices with their start and end apart: 23 -> 24, of which waited for: 9 -> 9; matrix products, arithmetic and copies ran while one was open for 3% -> 2% of each run, Pallas kernels for 5% -> 6%
where the time goes in v4:
time: 147 us; the launch traced here: 150 us
  starting transfers between devices  80.4 us (55%)
  waiting for transfers between devices  44 us (30%)
  Pallas kernels  17.8 us (12%)
  local copies, waits for them, and re-layouts  4.33 us (3%)
  other arithmetic  2.58 us (2%)
    ppermute x24, starting transfers between devices, send(): return lax.ppermute(x, AXES, pairs)  80.4 us
    ppermute x24, waiting for transfers between devices, send(): return lax.ppermute(x, AXES, pairs)  44 us
    pallas_call x3, Pallas kernels, attend(): pl.pallas_call(functools.partial(attend_kernel, sets=sets, tiles=tiles, f...  13.4 us
    unnamed x10, local copies, waits for them, and re-layouts  4.09 us
  transfers between devices with their start and end apart: 24, of which 9 were waited for; matrix products, arithmetic and copies ran while one was open for 2% of the time, Pallas kernels for 6%

profile of v4, /device:TPU:8, one launch (start us, length us, event | category | flops | bytes accessed | tf_op | source)
XLA Modules:
  0.0 149.5 jit_solution(6175196679858659488)
XLA Ops:
  0.0 1.3 collective-permute-start
  1.3 1.3 collective-permute-start.2
  2.6 4.5 %collective-permute-start.1 = (s32[3,2,27]{2,1,0:T(2,128)}, s32[3,2,27]{2,1,0:T(2,128)S(1)}, u32[]{:S(2)}, u32[]{:S(2)}) collective-permute-start(s32[3,2,27]{2,1,0:T(2,128)} %param.3), channel_id=1, source_target_pairs={{0,4},{1,6},{2,36},{3,38},{4,8},{5,10},{6,40},{7,42},{8,12},{9,14}... | collective-permute-start | bytes 1952 | tf_op jit(solution)/shard_map/ppermute | solution.py:79
  7.2 1.5 collective-permute-done.1
  8.7 1.5 copy-done
  10.2 0.2 split.1
  10.4 0.6 copy-done.1
  11.0 0.6 copy-done.2
  11.7 0.7 copy-done.3
  12.4 0.7 copy-done.4
  13.0 0.7 collective-permute-start.3
  13.7 7.0 %collective-permute-start.8 = (bf16[2,192,384]{2,1,0:T(8,128)(2,1)S(1)}, bf16[2,192,384]{2,1,0:T(8,128)(2,1)S(1)}, u32[]{:S(2)}, u32[]{:S(2)}) collective-permute-start(bf16[2,192,384]{2,1,0:T(8,128)(2,1)S(1)} %get-tuple-element.46), channel_id=1, source_target_pairs={{0,2},{1,0},{2,34},{3,32},{4,6},{5,4},{6,38},{7,36},{8,10},{9,8},{... | collective-permute-start | bytes 884744 | tf_op jit(solution)/shard_map/ppermute | solution.py:79
  20.6 2.1 %collective-permute-start.9 = (bf16[2,192,384]{2,1,0:T(8,128)(2,1)S(1)}, bf16[2,192,384]{2,1,0:T(8,128)(2,1)S(1)}, u32[]{:S(2)}, u32[]{:S(2)}) collective-permute-start(bf16[2,192,384]{2,1,0:T(8,128)(2,1)S(1)} %get-tuple-element.47), channel_id=1, source_target_pairs={{0,32},{1,34},{2,0},{3,2},{4,36},{5,38},{6,4},{7,6},{8,40},{9,42},... | collective-permute-start | bytes 884744 | tf_op jit(solution)/shard_map/ppermute | solution.py:79
  22.8 1.9 %collective-permute-start.10 = (bf16[2,192,384]{2,1,0:T(8,128)(2,1)S(1)}, bf16[2,192,384]{2,1,0:T(8,128)(2,1)S(1)}, u32[]{:S(2)}, u32[]{:S(2)}) collective-permute-start(bf16[2,192,384]{2,1,0:T(8,128)(2,1)S(1)} %get-tuple-element.48), channel_id=1, source_target_pairs={{0,34},{1,32},{2,2},{3,0},{4,38},{5,36},{6,6},{7,4},{8,42},{9,40},... | collective-permute-start | bytes 884744 | tf_op jit(solution)/shard_map/ppermute | solution.py:79
  24.8 1.7 %collective-permute-done.8.refs_1_ = bf16[2,192,384]{2,1,0:T(8,128)(2,1)S(1)} collective-permute-done((bf16[2,192,384]{2,1,0:T(8,128)(2,1)S(1)}, bf16[2,192,384]{2,1,0:T(8,128)(2,1)S(1)}, u32[]{:S(2)}, u32[]{:S(2)}) %collective-permute-start.8) | collective-permute-done | bytes 294944 | tf_op jit(solution)/shard_map/ppermute | solution.py:79
  26.5 8.0 %collective-permute-done.9.refs_2_ = bf16[2,192,384]{2,1,0:T(8,128)(2,1)S(1)} collective-permute-done((bf16[2,192,384]{2,1,0:T(8,128)(2,1)S(1)}, bf16[2,192,384]{2,1,0:T(8,128)(2,1)S(1)}, u32[]{:S(2)}, u32[]{:S(2)}) %collective-permute-start.9) | collective-permute-done | bytes 294944 | tf_op jit(solution)/shard_map/ppermute | solution.py:79
  34.5 1.1 stack.29
  35.6 2.0 %collective-permute-start.12 = (bf16[2,768,384]{2,1,0:T(8,128)(2,1)S(1)}, bf16[2,768,384]{2,1,0:T(8,128)(2,1)S(1)}, u32[]{:S(2)}, u32[]{:S(2)}) collective-permute-start(bf16[2,768,384]{2,1,0:T(8,128)(2,1)S(1)} %get-tuple-element.49.refs_1_.refs_2_), channel_id=1, source_target_pairs={{1,64},{3,66},{5,68},{7,70},{9,72},{11,74},{13,76},{15,78},{17,80}... | collective-permute-start | bytes 3538952 | tf_op jit(solution)/shard_map/ppermute | solution.py:79
  37.6 1.7 %collective-permute-start.11 = (bf16[2,768,384]{2,1,0:T(8,128)(2,1)S(1)}, bf16[2,768,384]{2,1,0:T(8,128)(2,1)S(1)}, u32[]{:S(2)}, u32[]{:S(2)}) collective-permute-start(bf16[2,768,384]{2,1,0:T(8,128)(2,1)S(1)} %get-tuple-element.49.refs_1_.refs_2_), channel_id=1, source_target_pairs={{0,1},{1,0},{2,3},{3,2},{4,5},{5,4},{6,7},{7,6},{8,9},{9,8},{10,11... | collective-permute-start | bytes 3538952 | tf_op jit(solution)/shard_map/ppermute | solution.py:79
  39.3 7.2 %collective-permute-start.13 = (bf16[2,384,384]{2,1,0:T(8,128)(2,1)}, bf16[2,384,384]{2,1,0:T(8,128)(2,1)}, u32[]{:S(2)}, u32[]{:S(2)}) collective-permute-start(bf16[2,384,384]{2,1,0:T(8,128)(2,1)} %get-tuple-element.50), channel_id=1, source_target_pairs={{0,16},{1,17},{2,18},{3,19},{4,20},{5,21},{6,22},{7,23},{8,24},{9,... | collective-permute-start | bytes 1769480 | tf_op jit(solution)/shard_map/ppermute | solution.py:79
  46.5 0.7 pad_add_fusion.1
  47.2 2.8 %collective-permute-start.4 = (bf16[192,384]{1,0:T(8,128)(2,1)}, bf16[192,384]{1,0:T(8,128)(2,1)}, u32[]{:S(2)}, u32[]{:S(2)}) collective-permute-start(bf16[192,384]{1,0:T(8,128)(2,1)} %copy-done.4), channel_id=1, source_target_pairs={{0,0},{1,2},{2,32},{3,34},{4,4},{5,6},{6,36},{7,38},{8,8},{9,10},{... | collective-permute-start | bytes 442376 | tf_op jit(solution)/shard_map/ppermute | solution.py:79
  50.0 1.3 collective-permute-start.5
  51.4 1.0 fusion
  52.5 4.9 %collective-permute-start.6 = (bf16[192,384]{1,0:T(8,128)(2,1)}, bf16[192,384]{1,0:T(8,128)(2,1)}, u32[]{:S(2)}, u32[]{:S(2)}) collective-permute-start(bf16[192,384]{1,0:T(8,128)(2,1)} %copy-done.2), channel_id=1, source_target_pairs={{0,32},{1,34},{2,0},{3,2},{4,36},{5,38},{6,4},{7,6},{8,40},{9,42},... | collective-permute-start | bytes 442376 | tf_op jit(solution)/shard_map/ppermute | solution.py:79
  57.4 4.0 %collective-permute-start.7 = (bf16[192,384]{1,0:T(8,128)(2,1)}, bf16[192,384]{1,0:T(8,128)(2,1)}, u32[]{:S(2)}, u32[]{:S(2)}) collective-permute-start(bf16[192,384]{1,0:T(8,128)(2,1)} %copy-done.1), channel_id=1, source_target_pairs={{0,34},{1,32},{2,2},{3,0},{4,38},{5,36},{6,6},{7,4},{8,42},{9,40},... | collective-permute-start | bytes 442376 | tf_op jit(solution)/shard_map/ppermute | solution.py:79
  61.5 0.7 fusion.2
  62.3 2.1 %collective-permute-done.7.refs_3_ = bf16[192,384]{1,0:T(8,128)(2,1)} collective-permute-done((bf16[192,384]{1,0:T(8,128)(2,1)}, bf16[192,384]{1,0:T(8,128)(2,1)}, u32[]{:S(2)}, u32[]{:S(2)}) %collective-permute-start.7) | collective-permute-done | bytes 147488 | tf_op jit(solution)/shard_map/ppermute | solution.py:79
  64.4 1.2 stack_queries.1.refs_0_
  65.6 1.3 collective-permute-start.17
  66.9 5.6 %collective-permute-start.16 = (bf16[768,384]{1,0:T(8,128)(2,1)S(1)}, bf16[768,384]{1,0:T(8,128)(2,1)S(1)}, u32[]{:S(2)}, u32[]{:S(2)}) collective-permute-start(bf16[768,384]{1,0:T(8,128)(2,1)S(1)} %stack_queries.1.refs_0_), channel_id=1, source_target_pairs={{0,4},{1,5},{2,6},{3,7},{4,8},{5,9},{6,10},{7,11},{8,12},{9,13},{1... | collective-permute-start | bytes 1769480 | tf_op jit(solution)/shard_map/ppermute | solution.py:79
  72.5 4.1 %attend_1_6.1.refs_0_ = f32[400,768]{1,0:T(8,128)S(1)} custom-call(s32[162]{0:T(256)S(1)} %reshape.249.mask_ref, bf16[768,384]{1,0:T(8,128)(2,1)S(1)} %stack_queries.1.refs_0_, bf16[2,768,384]{2,1,0:T(8,128)(2,1)S(1)} %get-tuple-element.49.refs_1_.refs_2_, bf16[2,768,384]{2,1,0:T(8,128)(2,1)S(1)} %collective-permute-done.11.refs_2_.refs_3_, ...), custom_call_target="tpu_custom_call" | custom-call | tf_op jit(solution)/shard_map/attend_1_6/pallas_call | solution.py:306
  76.6 3.3 %collective-permute-start.15 = (bf16[2,384,384]{2,1,0:T(8,128)(2,1)}, bf16[2,384,384]{2,1,0:T(8,128)(2,1)S(1)}, u32[]{:S(2)}, u32[]{:S(2)}) collective-permute-start(bf16[2,384,384]{2,1,0:T(8,128)(2,1)} %collective-permute-done.13.refs_1_.refs_5_), channel_id=1, source_target_pairs={{1,64},{3,66},{5,68},{7,70},{9,72},{11,74},{13,76},{15,78},{17,80}... | collective-permute-start | bytes 1769480 | tf_op jit(solution)/shard_map/ppermute | solution.py:79
  79.9 0.4 collective-permute-start.14
  80.3 8.0 %collective-permute-done.17.refs_1_ = bf16[768,384]{1,0:T(8,128)(2,1)S(1)} collective-permute-done((bf16[768,384]{1,0:T(8,128)(2,1)S(1)}, bf16[768,384]{1,0:T(8,128)(2,1)S(1)}, u32[]{:S(2)}, u32[]{:S(2)}) %collective-permute-start.17) | collective-permute-done | bytes 589856 | tf_op jit(solution)/shard_map/ppermute | solution.py:79
  88.3 5.9 %attend_2_9.1 = (bf16[400,768]{1,0:T(8,128)(2,1)S(1)}, bf16[400,768]{1,0:T(8,128)(2,1)S(1)}) custom-call(s32[162]{0:T(256)S(1)} %reshape.249.mask_ref, bf16[768,384]{1,0:T(8,128)(2,1)S(1)} %collective-permute-done.16.refs_0_, bf16[768,384]{1,0:T(8,128)(2,1)S(1)} %collective-permute-done.17.refs_1_, ...), custom_call_target="tpu_custom_call" | custom-call | tf_op jit(solution)/shard_map/attend_2_9/pallas_call | solution.py:306
  94.3 5.5 %collective-permute-start.18 = (bf16[400,768]{1,0:T(8,128)(2,1)S(1)}, bf16[400,768]{1,0:T(8,128)(2,1)S(1)}, u32[]{:S(2)}, u32[]{:S(2)}) collective-permute-start(bf16[400,768]{1,0:T(8,128)(2,1)S(1)} %get-tuple-element.53), channel_id=1, source_target_pairs={{0,4},{1,5},{2,6},{3,7},{4,8},{5,9},{6,10},{7,11},{8,12},{9,13},{1... | collective-permute-start | bytes 1843208 | tf_op jit(solution)/shard_map/ppermute | solution.py:79
  99.8 1.3 collective-permute-start.19
  101.2 3.4 %attend_1_3.1.refs_1_ = f32[400,768]{1,0:T(8,128)S(1)} custom-call(s32[162]{0:T(256)S(1)} %reshape.249.mask_ref, bf16[768,384]{1,0:T(8,128)(2,1)S(1)} %stack_queries.1.refs_0_, bf16[2,384,384]{2,1,0:T(8,128)(2,1)} %collective-permute-done.13.refs_1_.refs_5_, bf16[2,384,384]{2,1,0:T(8,128)(2,1)S(1)} %collective-permute-done.14.refs_2_.refs_6_, ...), custom_call_target="tpu_custom_call" | custom-call | tf_op jit(solution)/shard_map/attend_1_3/pallas_call | solution.py:306
  104.5 9.3 %collective-permute-done.18.refs_2_ = bf16[400,768]{1,0:T(8,128)(2,1)S(1)} collective-permute-done((bf16[400,768]{1,0:T(8,128)(2,1)S(1)}, bf16[400,768]{1,0:T(8,128)(2,1)S(1)}, u32[]{:S(2)}, u32[]{:S(2)}) %collective-permute-start.18) | collective-permute-done | bytes 614432 | tf_op jit(solution)/shard_map/ppermute | solution.py:79
  113.9 4.4 %collective-permute-done.19.refs_3_ = bf16[400,768]{1,0:T(8,128)(2,1)S(1)} collective-permute-done((bf16[400,768]{1,0:T(8,128)(2,1)S(1)}, bf16[400,768]{1,0:T(8,128)(2,1)S(1)}, u32[]{:S(2)}, u32[]{:S(2)}) %collective-permute-start.19) | collective-permute-done | bytes 614432 | tf_op jit(solution)/shard_map/ppermute | solution.py:79
  118.2 1.2 merge.1
  119.4 0.7 collective-permute-start.20
  120.1 17.8 %collective-permute-start.21 = (bf16[192,384]{1,0:T(8,128)(2,1)S(1)}, bf16[192,384]{1,0:T(8,128)(2,1)S(1)}, u32[]{:S(2)}, u32[]{:S(2)}) collective-permute-start(bf16[192,384]{1,0:T(8,128)(2,1)S(1)} %get-tuple-element.56), channel_id=1, source_target_pairs={{2,0},{0,1},{34,2},{32,3},{6,4},{4,5},{38,6},{36,7},{10,8},{8,9},{... | collective-permute-start | bytes 442376 | tf_op jit(solution)/shard_map/ppermute | solution.py:79
  137.8 1.9 %collective-permute-start.23 = (bf16[192,384]{1,0:T(8,128)(2,1)S(1)}, bf16[192,384]{1,0:T(8,128)(2,1)S(1)}, u32[]{:S(2)}, u32[]{:S(2)}) collective-permute-start(bf16[192,384]{1,0:T(8,128)(2,1)S(1)} %get-tuple-element.58), channel_id=1, source_target_pairs={{34,0},{32,1},{2,2},{0,3},{38,4},{36,5},{6,6},{4,7},{42,8},{40,9},... | collective-permute-start | bytes 442376 | tf_op jit(solution)/shard_map/ppermute | solution.py:79
  139.8 4.8 %collective-permute-done.22.refs_2_ = bf16[192,384]{1,0:T(8,128)(2,1)S(1)} collective-permute-done((bf16[192,384]{1,0:T(8,128)(2,1)S(1)}, bf16[192,384]{1,0:T(8,128)(2,1)S(1)}, u32[]{:S(2)}, u32[]{:S(2)}) %collective-permute-start.22) | collective-permute-done | bytes 147488 | tf_op jit(solution)/shard_map/ppermute | solution.py:79
  144.6 4.0 %collective-permute-done.23.refs_3_ = bf16[192,384]{1,0:T(8,128)(2,1)S(1)} collective-permute-done((bf16[192,384]{1,0:T(8,128)(2,1)S(1)}, bf16[192,384]{1,0:T(8,128)(2,1)S(1)}, u32[]{:S(2)}, u32[]{:S(2)}) %collective-permute-start.23) | collective-permute-done | bytes 147488 | tf_op jit(solution)/shard_map/ppermute | solution.py:79
  148.6 0.9 join.1
  (27 shorter events, 0.5 us)
Async XLA Ops:
  0.0 7.2 %collective-permute-start = (s32[3,2,27]{2,1,0:T(2,128)}, s32[3,2,27]{2,1,0:T(2,128)S(1)}, u32[]{:S(2)}, u32[]{:S(2)}) collective-permute-start(s32[3,2,27]{2,1,0:T(2,128)} %param.3), channel_id=1, source_target_pairs={{0,0},{1,2},{2,32},{3,34},{4,4},{5,6},{6,36},{7,38},{8,8},{9,10},{... | collective-permute-start | bytes 1952 | tf_op jit(solution)/shard_map/ppermute | solution.py:79
  1.3 5.9 %collective-permute-start.2 = (s32[3,2,27]{2,1,0:T(2,128)}, s32[3,2,27]{2,1,0:T(2,128)S(1)}, u32[]{:S(2)}, u32[]{:S(2)}) collective-permute-start(s32[3,2,27]{2,1,0:T(2,128)} %param.3), channel_id=1, source_target_pairs={{4,0},{5,2},{6,32},{7,34},{8,4},{9,6},{10,36},{11,38},{12,8},{13,1... | collective-permute-start | bytes 1952 | tf_op jit(solution)/shard_map/ppermute | solution.py:79
  2.6 6.1 %collective-permute-start.1 = (s32[3,2,27]{2,1,0:T(2,128)}, s32[3,2,27]{2,1,0:T(2,128)S(1)}, u32[]{:S(2)}, u32[]{:S(2)}) collective-permute-start(s32[3,2,27]{2,1,0:T(2,128)} %param.3), channel_id=1, source_target_pairs={{0,4},{1,6},{2,36},{3,38},{4,8},{5,10},{6,40},{7,42},{8,12},{9,14}... | collective-permute-start | bytes 1952 | tf_op jit(solution)/shard_map/ppermute | solution.py:79
  8.7 1.5 copy-start
  10.4 0.7 copy-start.1
  11.0 0.7 copy-start.2
  11.7 0.7 copy-start.3
  12.4 0.7 copy-start.4
  13.0 11.8 %collective-permute-start.3 = (bf16[2,192,384]{2,1,0:T(8,128)(2,1)S(1)}, bf16[2,192,384]{2,1,0:T(8,128)(2,1)S(1)}, u32[]{:S(2)}, u32[]{:S(2)}) collective-permute-start(bf16[2,192,384]{2,1,0:T(8,128)(2,1)S(1)} %get-tuple-element.36), channel_id=1, source_target_pairs={{0,0},{1,2},{2,32},{3,34},{4,4},{5,6},{6,36},{7,38},{8,8},{9,10},{... | collective-permute-start | bytes 884744 | tf_op jit(solution)/shard_map/ppermute | solution.py:79
  13.7 12.8 %collective-permute-start.8 = (bf16[2,192,384]{2,1,0:T(8,128)(2,1)S(1)}, bf16[2,192,384]{2,1,0:T(8,128)(2,1)S(1)}, u32[]{:S(2)}, u32[]{:S(2)}) collective-permute-start(bf16[2,192,384]{2,1,0:T(8,128)(2,1)S(1)} %get-tuple-element.46), channel_id=1, source_target_pairs={{0,2},{1,0},{2,34},{3,32},{4,6},{5,4},{6,38},{7,36},{8,10},{9,8},{... | collective-permute-start | bytes 884744 | tf_op jit(solution)/shard_map/ppermute | solution.py:79
  20.6 13.9 %collective-permute-start.9 = (bf16[2,192,384]{2,1,0:T(8,128)(2,1)S(1)}, bf16[2,192,384]{2,1,0:T(8,128)(2,1)S(1)}, u32[]{:S(2)}, u32[]{:S(2)}) collective-permute-start(bf16[2,192,384]{2,1,0:T(8,128)(2,1)S(1)} %get-tuple-element.47), channel_id=1, source_target_pairs={{0,32},{1,34},{2,0},{3,2},{4,36},{5,38},{6,4},{7,6},{8,40},{9,42},... | collective-permute-start | bytes 884744 | tf_op jit(solution)/shard_map/ppermute | solution.py:79
  22.8 11.8 %collective-permute-start.10 = (bf16[2,192,384]{2,1,0:T(8,128)(2,1)S(1)}, bf16[2,192,384]{2,1,0:T(8,128)(2,1)S(1)}, u32[]{:S(2)}, u32[]{:S(2)}) collective-permute-start(bf16[2,192,384]{2,1,0:T(8,128)(2,1)S(1)} %get-tuple-element.48), channel_id=1, source_target_pairs={{0,34},{1,32},{2,2},{3,0},{4,38},{5,36},{6,6},{7,4},{8,42},{9,40},... | collective-permute-start | bytes 884744 | tf_op jit(solution)/shard_map/ppermute | solution.py:79
  35.6 36.8 %collective-permute-start.12 = (bf16[2,768,384]{2,1,0:T(8,128)(2,1)S(1)}, bf16[2,768,384]{2,1,0:T(8,128)(2,1)S(1)}, u32[]{:S(2)}, u32[]{:S(2)}) collective-permute-start(bf16[2,768,384]{2,1,0:T(8,128)(2,1)S(1)} %get-tuple-element.49.refs_1_.refs_2_), channel_id=1, source_target_pairs={{1,64},{3,66},{5,68},{7,70},{9,72},{11,74},{13,76},{15,78},{17,80}... | collective-permute-start | bytes 3538952 | tf_op jit(solution)/shard_map/ppermute | solution.py:79
  37.6 34.8 %collective-permute-start.11 = (bf16[2,768,384]{2,1,0:T(8,128)(2,1)S(1)}, bf16[2,768,384]{2,1,0:T(8,128)(2,1)S(1)}, u32[]{:S(2)}, u32[]{:S(2)}) collective-permute-start(bf16[2,768,384]{2,1,0:T(8,128)(2,1)S(1)} %get-tuple-element.49.refs_1_.refs_2_), channel_id=1, source_target_pairs={{0,1},{1,0},{2,3},{3,2},{4,5},{5,4},{6,7},{7,6},{8,9},{9,8},{10,11... | collective-permute-start | bytes 3538952 | tf_op jit(solution)/shard_map/ppermute | solution.py:79
  39.3 37.3 %collective-permute-start.13 = (bf16[2,384,384]{2,1,0:T(8,128)(2,1)}, bf16[2,384,384]{2,1,0:T(8,128)(2,1)}, u32[]{:S(2)}, u32[]{:S(2)}) collective-permute-start(bf16[2,384,384]{2,1,0:T(8,128)(2,1)} %get-tuple-element.50), channel_id=1, source_target_pairs={{0,16},{1,17},{2,18},{3,19},{4,20},{5,21},{6,22},{7,23},{8,24},{9,... | collective-permute-start | bytes 1769480 | tf_op jit(solution)/shard_map/ppermute | solution.py:79
  47.2 5.4 %collective-permute-start.4 = (bf16[192,384]{1,0:T(8,128)(2,1)}, bf16[192,384]{1,0:T(8,128)(2,1)}, u32[]{:S(2)}, u32[]{:S(2)}) collective-permute-start(bf16[192,384]{1,0:T(8,128)(2,1)} %copy-done.4), channel_id=1, source_target_pairs={{0,0},{1,2},{2,32},{3,34},{4,4},{5,6},{6,36},{7,38},{8,8},{9,10},{... | collective-permute-start | bytes 442376 | tf_op jit(solution)/shard_map/ppermute | solution.py:79
  50.0 7.4 %collective-permute-start.5 = (bf16[192,384]{1,0:T(8,128)(2,1)}, bf16[192,384]{1,0:T(8,128)(2,1)}, u32[]{:S(2)}, u32[]{:S(2)}) collective-permute-start(bf16[192,384]{1,0:T(8,128)(2,1)} %copy-done.3), channel_id=1, source_target_pairs={{0,2},{1,0},{2,34},{3,32},{4,6},{5,4},{6,38},{7,36},{8,10},{9,8},{... | collective-permute-start | bytes 442376 | tf_op jit(solution)/shard_map/ppermute | solution.py:79
  52.5 9.8 %collective-permute-start.6 = (bf16[192,384]{1,0:T(8,128)(2,1)}, bf16[192,384]{1,0:T(8,128)(2,1)}, u32[]{:S(2)}, u32[]{:S(2)}) collective-permute-start(bf16[192,384]{1,0:T(8,128)(2,1)} %copy-done.2), channel_id=1, source_target_pairs={{0,32},{1,34},{2,0},{3,2},{4,36},{5,38},{6,4},{7,6},{8,40},{9,42},... | collective-permute-start | bytes 442376 | tf_op jit(solution)/shard_map/ppermute | solution.py:79
  57.4 7.0 %collective-permute-start.7 = (bf16[192,384]{1,0:T(8,128)(2,1)}, bf16[192,384]{1,0:T(8,128)(2,1)}, u32[]{:S(2)}, u32[]{:S(2)}) collective-permute-start(bf16[192,384]{1,0:T(8,128)(2,1)} %copy-done.1), channel_id=1, source_target_pairs={{0,34},{1,32},{2,2},{3,0},{4,38},{5,36},{6,6},{7,4},{8,42},{9,40},... | collective-permute-start | bytes 442376 | tf_op jit(solution)/shard_map/ppermute | solution.py:79
  65.6 22.7 %collective-permute-start.17 = (bf16[768,384]{1,0:T(8,128)(2,1)S(1)}, bf16[768,384]{1,0:T(8,128)(2,1)S(1)}, u32[]{:S(2)}, u32[]{:S(2)}) collective-permute-start(bf16[768,384]{1,0:T(8,128)(2,1)S(1)} %stack_queries.1.refs_0_), channel_id=1, source_target_pairs={{4,0},{5,1},{6,2},{7,3},{8,4},{9,5},{10,6},{11,7},{12,8},{13,9},{1... | collective-permute-start | bytes 1769480 | tf_op jit(solution)/shard_map/ppermute | solution.py:79
  66.9 21.5 %collective-permute-start.16 = (bf16[768,384]{1,0:T(8,128)(2,1)S(1)}, bf16[768,384]{1,0:T(8,128)(2,1)S(1)}, u32[]{:S(2)}, u32[]{:S(2)}) collective-permute-start(bf16[768,384]{1,0:T(8,128)(2,1)S(1)} %stack_queries.1.refs_0_), channel_id=1, source_target_pairs={{0,4},{1,5},{2,6},{3,7},{4,8},{5,9},{6,10},{7,11},{8,12},{9,13},{1... | collective-permute-start | bytes 1769480 | tf_op jit(solution)/shard_map/ppermute | solution.py:79
  76.6 11.7 %collective-permute-start.15 = (bf16[2,384,384]{2,1,0:T(8,128)(2,1)}, bf16[2,384,384]{2,1,0:T(8,128)(2,1)S(1)}, u32[]{:S(2)}, u32[]{:S(2)}) collective-permute-start(bf16[2,384,384]{2,1,0:T(8,128)(2,1)} %collective-permute-done.13.refs_1_.refs_5_), channel_id=1, source_target_pairs={{1,64},{3,66},{5,68},{7,70},{9,72},{11,74},{13,76},{15,78},{17,80}... | collective-permute-start | bytes 1769480 | tf_op jit(solution)/shard_map/ppermute | solution.py:79
  79.9 8.4 %collective-permute-start.14 = (bf16[2,384,384]{2,1,0:T(8,128)(2,1)}, bf16[2,384,384]{2,1,0:T(8,128)(2,1)S(1)}, u32[]{:S(2)}, u32[]{:S(2)}) collective-permute-start(bf16[2,384,384]{2,1,0:T(8,128)(2,1)} %collective-permute-done.13.refs_1_.refs_5_), channel_id=1, source_target_pairs={{0,1},{1,0},{2,3},{3,2},{4,5},{5,4},{6,7},{7,6},{8,9},{9,8},{10,11... | collective-permute-start | bytes 1769480 | tf_op jit(solution)/shard_map/ppermute | solution.py:79
  94.3 19.6 %collective-permute-start.18 = (bf16[400,768]{1,0:T(8,128)(2,1)S(1)}, bf16[400,768]{1,0:T(8,128)(2,1)S(1)}, u32[]{:S(2)}, u32[]{:S(2)}) collective-permute-start(bf16[400,768]{1,0:T(8,128)(2,1)S(1)} %get-tuple-element.53), channel_id=1, source_target_pairs={{0,4},{1,5},{2,6},{3,7},{4,8},{5,9},{6,10},{7,11},{8,12},{9,13},{1... | collective-permute-start | bytes 1843208 | tf_op jit(solution)/shard_map/ppermute | solution.py:79
  99.8 18.4 %collective-permute-start.19 = (bf16[400,768]{1,0:T(8,128)(2,1)S(1)}, bf16[400,768]{1,0:T(8,128)(2,1)S(1)}, u32[]{:S(2)}, u32[]{:S(2)}) collective-permute-start(bf16[400,768]{1,0:T(8,128)(2,1)S(1)} %get-tuple-element.54), channel_id=1, source_target_pairs={{4,0},{5,1},{6,2},{7,3},{8,4},{9,5},{10,6},{11,7},{12,8},{13,9},{1... | collective-permute-start | bytes 1843208 | tf_op jit(solution)/shard_map/ppermute | solution.py:79
  119.4 20.4 %collective-permute-start.20 = (bf16[192,384]{1,0:T(8,128)(2,1)S(1)}, bf16[192,384]{1,0:T(8,128)(2,1)S(1)}, u32[]{:S(2)}, u32[]{:S(2)}) collective-permute-start(bf16[192,384]{1,0:T(8,128)(2,1)S(1)} %get-tuple-element.55), channel_id=1, source_target_pairs={{0,0},{2,1},{32,2},{34,3},{4,4},{6,5},{36,6},{38,7},{8,8},{10,9},{... | collective-permute-start | bytes 442376 | tf_op jit(solution)/shard_map/ppermute | solution.py:79
  120.1 19.7 %collective-permute-start.21 = (bf16[192,384]{1,0:T(8,128)(2,1)S(1)}, bf16[192,384]{1,0:T(8,128)(2,1)S(1)}, u32[]{:S(2)}, u32[]{:S(2)}) collective-permute-start(bf16[192,384]{1,0:T(8,128)(2,1)S(1)} %get-tuple-element.56), channel_id=1, source_target_pairs={{2,0},{0,1},{34,2},{32,3},{6,4},{4,5},{38,6},{36,7},{10,8},{8,9},{... | collective-permute-start | bytes 442376 | tf_op jit(solution)/shard_map/ppermute | solution.py:79
  137.8 6.8 %collective-permute-start.22 = (bf16[192,384]{1,0:T(8,128)(2,1)S(1)}, bf16[192,384]{1,0:T(8,128)(2,1)S(1)}, u32[]{:S(2)}, u32[]{:S(2)}) collective-permute-start(bf16[192,384]{1,0:T(8,128)(2,1)S(1)} %get-tuple-element.57), channel_id=1, source_target_pairs={{32,0},{34,1},{0,2},{2,3},{36,4},{38,5},{4,6},{6,7},{40,8},{42,9},... | collective-permute-start | bytes 442376 | tf_op jit(solution)/shard_map/ppermute | solution.py:79
  137.8 10.8 %collective-permute-start.23 = (bf16[192,384]{1,0:T(8,128)(2,1)S(1)}, bf16[192,384]{1,0:T(8,128)(2,1)S(1)}, u32[]{:S(2)}, u32[]{:S(2)}) collective-permute-start(bf16[192,384]{1,0:T(8,128)(2,1)S(1)} %get-tuple-element.58), channel_id=1, source_target_pairs={{34,0},{32,1},{2,2},{0,3},{38,4},{36,5},{6,6},{4,7},{42,8},{40,9},... | collective-permute-start | bytes 442376 | tf_op jit(solution)/shard_map/ppermute | solution.py:79

commit v5 on v4

--- a/solution.py
+++ b/solution.py
@@ -11,7 +11,8 @@
 TIME_TILES = 4
 AXES = ("seq", "head")
 FAR = -1e30
-VMEM_LIMIT = 40 * 2**20
+VMEM_LIMIT = 28 * 2**20
+VMEM_SMALL = 12 * 2**20
 BATCH = 2
 EXTRA = 16
 POOL = 9
@@ -79,45 +80,33 @@
     return lax.ppermute(x, AXES, pairs)
 
 
-def split_kernel(at_ref, qkv_ref, *refs):
-    outs, sems = refs[:8], refs[8]
+def split_kernel(at_ref, qkv_ref, *outs):
     width = outs[0].shape[-1]
-    copies = []
     for k in range(4):
-        lanes = pl.ds(pl.multiple_of((at_ref[0] ^ k) * width, 128), width)
-        copies.append(pltpu.make_async_copy(qkv_ref.at[0, :, lanes], outs[k], sems.at[k]))
-    for copy in copies:
-        copy.start()
-    for k in range(4):
-        lanes = pl.ds(pl.multiple_of((at_ref[0] ^ k) * width, 128), width)
-        outs[4 + k][...] = qkv_ref[1:3, :, lanes]
-    for copy in copies:
-        copy.wait()
+        outs[k][...] = qkv_ref[:, :, pl.ds(pl.multiple_of((at_ref[0] ^ k) * width, 128), width)]
 
 
 def split(at, qkv):
-    _, rows, columns = qkv.shape
-    width = columns // 4
-    vmem = pl.BlockSpec(memory_space=pltpu.VMEM)
-    shapes = [jax.ShapeDtypeStruct((rows, width), qkv.dtype)] * 4
-    shapes += [jax.ShapeDtypeStruct((2, rows, width), qkv.dtype)] * 4
+    count, rows, columns = qkv.shape
+    vmem = pl.BlockSpec(memory_space=pltpu.VMEM)
     return pl.pallas_call(
         split_kernel,
-        out_shape=shapes,
+        out_shape=[jax.ShapeDtypeStruct((count, rows, columns // 4), qkv.dtype)] * 4,
         in_specs=[pl.BlockSpec(memory_space=pltpu.SMEM), vmem],
-        out_specs=[pl.BlockSpec(memory_space=pl.ANY)] * 4 + [vmem] * 4,
-        scratch_shapes=[pltpu.SemaphoreType.DMA((4,))],
-        compiler_params=pltpu.CompilerParams(vmem_limit_bytes=VMEM_LIMIT),
+        out_specs=[vmem] * 4,
+        compiler_params=pltpu.CompilerParams(vmem_limit_bytes=VMEM_SMALL),
         name="split",
     )(at, qkv)
 
 
 def stack_kernel(place_ref, *refs):
-    parts, kv_ref, edge_ref, sems = refs[:4], refs[4], refs[5], refs[6]
+    parts, (q_ref, kv_ref, edge_ref), sems = refs[:4], refs[4:7], refs[7]
     rows = parts[0].shape[1]
     copies = []
     for k in range(4):
-        copies.append(pltpu.make_async_copy(parts[k], kv_ref.at[:, pl.ds(k * rows, rows)], sems.at[k]))
+        at = pl.ds(k * rows, rows)
+        copies.append(pltpu.make_async_copy(parts[k].at[pl.ds(1, 2)], kv_ref.at[:, at], sems.at[k]))
+        copies.append(pltpu.make_async_copy(parts[k].at[0], q_ref.at[at], sems.at[4 + k]))
     for copy in copies:
         copy.start()
     for copy in copies:
@@ -131,40 +120,16 @@
     return pl.pallas_call(
         stack_kernel,
         out_shape=[
+            jax.ShapeDtypeStruct((4 * rows, width), parts[0].dtype),
             jax.ShapeDtypeStruct((2, 4 * rows, width), parts[0].dtype),
             jax.ShapeDtypeStruct((2, 2 * rows, width), parts[0].dtype),
         ],
         in_specs=[pl.BlockSpec(memory_space=pltpu.SMEM)] + [pl.BlockSpec(memory_space=pl.ANY)] * 4,
-        out_specs=[vmem] * 2,
-        scratch_shapes=[pltpu.SemaphoreType.DMA((4,))],
-        compiler_params=pltpu.CompilerParams(vmem_limit_bytes=VMEM_LIMIT),
+        out_specs=[vmem] * 3,
+        scratch_shapes=[pltpu.SemaphoreType.DMA((8,))],
+        compiler_params=pltpu.CompilerParams(vmem_limit_bytes=VMEM_SMALL),
         name="stack",
     )(place, *parts)
-
-
-def stack_queries_kernel(*refs):
-    parts, q_ref, sems = refs[:4], refs[4], refs[5]
-    rows = parts[0].shape[0]
-    copies = []
-    for k in range(4):
-        copies.append(pltpu.make_async_copy(parts[k], q_ref.at[pl.ds(k * rows, rows)], sems.at[k]))
-    for copy in copies:
-        copy.start()
-    for copy in copies:
-        copy.wait()
-
-
-def stack_queries(parts):
-    rows, width = parts[0].shape
-    return pl.pallas_call(
-        stack_queries_kernel,
-        out_shape=jax.ShapeDtypeStruct((4 * rows, width), parts[0].dtype),
-        in_specs=[pl.BlockSpec(memory_space=pl.ANY)] * 4,
-        out_specs=pl.BlockSpec(memory_space=pltpu.VMEM),
-        scratch_shapes=[pltpu.SemaphoreType.DMA((4,))],
-        compiler_params=pltpu.CompilerParams(vmem_limit_bytes=VMEM_LIMIT),
-        name="stack_queries",
-    )(*parts)
 
 
 def join_kernel(at_ref, *refs):
@@ -182,7 +147,7 @@
         out_shape=jax.ShapeDtypeStruct((rows, 4 * width), parts[0].dtype),
         in_specs=[pl.BlockSpec(memory_space=pltpu.SMEM)] + [vmem] * 4,
         out_specs=vmem,
-        compiler_params=pltpu.CompilerParams(vmem_limit_bytes=VMEM_LIMIT),
+        compiler_params=pltpu.CompilerParams(vmem_limit_bytes=VMEM_SMALL),
         name="join",
     )(at, *parts)
 
@@ -369,7 +334,7 @@
         out_shape=[jax.ShapeDtypeStruct((brick // 4, width), jnp.bfloat16)] * 4,
         in_specs=[pl.BlockSpec(memory_space=pltpu.SMEM)] + [vmem] * 4,
         out_specs=[vmem] * 4,
-        compiler_params=pltpu.CompilerParams(vmem_limit_bytes=VMEM_LIMIT),
+        compiler_params=pltpu.CompilerParams(vmem_limit_bytes=VMEM_SMALL),
         name="merge",
     )(valid, *parts)
 
@@ -398,27 +363,24 @@
     valid = jnp.stack([time > 0, time < TIME_TILES - 1])
 
     lists = [send(key_tiles, list_pairs(by)) for by in (0, 1, -1)]
-    lists, qkv = lax.optimization_barrier((lists, qkv))
     lists = jnp.stack(lists)
     mask = named(lists, 2 * y + core, pair, time, xh)
     here = jnp.concatenate([jnp.ones((1,), bool), valid])
     mask = (mask & here[:, None, None, None]).astype(jnp.int32).reshape(-1)
 
     pieces = split(at, qkv)
-    kv_parts = [send(pieces[4 + k], spread_pairs(k)) for k in range(4)]
-    kv_parts[0], q_pieces = lax.optimization_barrier((kv_parts[0], pieces[:4]))
-    q_parts = [send(q_pieces[k], spread_pairs(k)) for k in range(4)]
-    kv_own, edge = stack(place, kv_parts)
+    parts = [send(pieces[k], spread_pairs(k)) for k in range(4)]
+    parts, mask = lax.optimization_barrier((parts, mask))
+    q_own, kv_own, edge = stack(place, parts)
+    edge_own = send(edge, edge_pairs())
     kv_core = send(kv_own, core_pairs())
     kv_column = send(kv_own, column_pairs())
-    edge_own = send(edge, edge_pairs())
-    q_own = stack_queries(q_parts)
-    q_prev = send(q_own, time_pairs(1))
-    q_next = send(q_own, time_pairs(-1))
 
     bodies = (kv_own, kv_core, kv_column)
     (o_body,) = attend(mask, (q_own,), bodies, heads, 0, 0, jnp.float32)
-    o_body, edge_own = lax.optimization_barrier((o_body, edge_own))
+    o_body, edge_own, q_away = lax.optimization_barrier((o_body, edge_own, q_own))
+    q_prev = send(q_away, time_pairs(1))
+    q_next = send(q_away, time_pairs(-1))
     edges = (edge_own, send(edge_own, core_pairs()), send(edge_own, column_pairs()))
     o_prev, o_next = attend(mask, (q_prev, q_next), bodies + edges, heads, 1, 0, jnp.bfloat16)
     o_before = send(o_next, time_pairs(1))

time: 147 us -> 146 us (level); the launches traced: 150 us -> 146 us
  starting transfers between devices: 80.4 us -> 56.6 us
  waiting for transfers between devices: 44 us -> 56.6 us
  Pallas kernels: 17.8 us -> 28.4 us
  local copies, waits for them, and re-layouts: 4.33 us -> 1.71 us
    ppermute x24 -> x20, starting transfers between devices: 80.4 us -> 56.6 us  [send(): return lax.ppermute(x, AXES, pairs)]
    ppermute x24 -> x20, waiting for transfers between devices: 44 us -> 56.6 us  [send(): return lax.ppermute(x, AXES, pairs)]
    pallas_call x3, Pallas kernels: 13.4 us -> 25.2 us  [attend(): pl.pallas_call(functools.partial(attend_kernel, sets=sets, tiles=tiles, f...]
    unnamed x10 -> x2, local copies, waits for them, and re-layouts: 4.09 us -> 1.47 us
  transfers between devices with their start and end apart: 24 -> 20, of which waited for: 9 -> 11; matrix products, arithmetic and copies ran while one was open for 2% -> 2% of each run, Pallas kernels for 6% -> 10%
where the time goes in v5:
time: 146 us
  starting transfers between devices  56.6 us (39%)
  waiting for transfers between devices  56.6 us (39%)
  Pallas kernels  28.4 us (19%)
  other arithmetic  2.48 us (2%)
  local copies, waits for them, and re-layouts  1.71 us (1%)
    ppermute x20, starting transfers between devices, send(): return lax.ppermute(x, AXES, pairs)  56.6 us
    ppermute x20, waiting for transfers between devices, send(): return lax.ppermute(x, AXES, pairs)  56.6 us
    pallas_call x3, Pallas kernels, attend(): pl.pallas_call(functools.partial(attend_kernel, sets=sets, tiles=tiles, f...  25.2 us
  transfers between devices with their start and end apart: 20, of which 11 were waited for; matrix products, arithmetic and copies ran while one was open for 2% of the time, Pallas kernels for 10%

profile of v5, /device:TPU:8, one launch (start us, length us, event | category | flops | bytes accessed | tf_op | source)
XLA Modules:
  0.0 146.1 jit_solution(18149228574753338976)
XLA Ops:
  0.0 1.3 collective-permute-start.4
  1.3 1.3 collective-permute-start.6
  2.6 4.5 %collective-permute-start.5 = (s32[3,2,27]{2,1,0:T(2,128)}, s32[3,2,27]{2,1,0:T(2,128)S(1)}, u32[]{:S(2)}, u32[]{:S(2)}) collective-permute-start(s32[3,2,27]{2,1,0:T(2,128)} %param.3), channel_id=1, source_target_pairs={{0,4},{1,6},{2,36},{3,38},{4,8},{5,10},{6,40},{7,42},{8,12},{9,14}... | collective-permute-start | bytes 1952 | tf_op jit(solution)/shard_map/ppermute | solution.py:80
  7.2 1.5 %copy-done = bf16[3,192,1536]{2,1,0:T(8,128)(2,1)S(1)} copy-done((bf16[3,192,1536]{2,1,0:T(8,128)(2,1)S(1)}, bf16[3,192,1536]{2,1,0:T(8,128)(2,1)}, u32[]{:S(2)}) %copy-start) | copy-done | bytes 1769496
  8.7 0.2 split.1
  8.8 0.7 collective-permute-start
  9.5 7.0 %collective-permute-start.1 = (bf16[3,192,384]{2,1,0:T(8,128)(2,1)S(1)}, bf16[3,192,384]{2,1,0:T(8,128)(2,1)S(1)}, u32[]{:S(2)}, u32[]{:S(2)}) collective-permute-start(bf16[3,192,384]{2,1,0:T(8,128)(2,1)S(1)} %get-tuple-element.27), channel_id=1, source_target_pairs={{0,2},{1,0},{2,34},{3,32},{4,6},{5,4},{6,38},{7,36},{8,10},{9,8},{... | collective-permute-start | bytes 1327112 | tf_op jit(solution)/shard_map/ppermute | solution.py:80
  16.5 0.6 pad_add_fusion.1
  17.1 0.0 collective-permute-done.4
  17.1 2.1 %collective-permute-start.2 = (bf16[3,192,384]{2,1,0:T(8,128)(2,1)S(1)}, bf16[3,192,384]{2,1,0:T(8,128)(2,1)S(1)}, u32[]{:S(2)}, u32[]{:S(2)}) collective-permute-start(bf16[3,192,384]{2,1,0:T(8,128)(2,1)S(1)} %get-tuple-element.28), channel_id=1, source_target_pairs={{0,32},{1,34},{2,0},{3,2},{4,36},{5,38},{6,4},{7,6},{8,40},{9,42},... | collective-permute-start | bytes 1327112 | tf_op jit(solution)/shard_map/ppermute | solution.py:80
  19.2 1.9 %collective-permute-start.3 = (bf16[3,192,384]{2,1,0:T(8,128)(2,1)S(1)}, bf16[3,192,384]{2,1,0:T(8,128)(2,1)S(1)}, u32[]{:S(2)}, u32[]{:S(2)}) collective-permute-start(bf16[3,192,384]{2,1,0:T(8,128)(2,1)S(1)} %get-tuple-element.29), channel_id=1, source_target_pairs={{0,34},{1,32},{2,2},{3,0},{4,38},{5,36},{6,6},{7,4},{8,42},{9,40},... | collective-permute-start | bytes 1327112 | tf_op jit(solution)/shard_map/ppermute | solution.py:80
  21.1 0.1 and_select_fusion.4
  21.3 1.0 fusion
  22.3 0.1 copy.7
  22.4 0.7 fusion.2
  23.1 0.1 reshape.250.mask_ref
  23.2 0.0 collective-permute-done.refs_0_
  23.2 3.9 %collective-permute-done.1.refs_1_ = bf16[3,192,384]{2,1,0:T(8,128)(2,1)S(1)} collective-permute-done((bf16[3,192,384]{2,1,0:T(8,128)(2,1)S(1)}, bf16[3,192,384]{2,1,0:T(8,128)(2,1)S(1)}, u32[]{:S(2)}, u32[]{:S(2)}) %collective-permute-start.1) | collective-permute-done | bytes 442400 | tf_op jit(solution)/shard_map/ppermute | solution.py:80
  27.1 9.6 %collective-permute-done.2.refs_2_ = bf16[3,192,384]{2,1,0:T(8,128)(2,1)S(1)} collective-permute-done((bf16[3,192,384]{2,1,0:T(8,128)(2,1)S(1)}, bf16[3,192,384]{2,1,0:T(8,128)(2,1)S(1)}, u32[]{:S(2)}, u32[]{:S(2)}) %collective-permute-start.2) | collective-permute-done | bytes 442400 | tf_op jit(solution)/shard_map/ppermute | solution.py:80
  36.7 1.0 stack.29
  37.7 2.5 %collective-permute-start.8 = (bf16[2,768,384]{2,1,0:T(8,128)(2,1)S(1)}, bf16[2,768,384]{2,1,0:T(8,128)(2,1)S(1)}, u32[]{:S(2)}, u32[]{:S(2)}) collective-permute-start(bf16[2,768,384]{2,1,0:T(8,128)(2,1)S(1)} %get-tuple-element.36.refs_1_.refs_2_), channel_id=1, source_target_pairs={{1,64},{3,66},{5,68},{7,70},{9,72},{11,74},{13,76},{15,78},{17,80}... | collective-permute-start | bytes 3538952 | tf_op jit(solution)/shard_map/ppermute | solution.py:80
  40.2 1.2 collective-permute-start.7
  41.4 7.2 %collective-permute-start.9 = (bf16[2,384,384]{2,1,0:T(8,128)(2,1)S(1)}, bf16[2,384,384]{2,1,0:T(8,128)(2,1)S(1)}, u32[]{:S(2)}, u32[]{:S(2)}) collective-permute-start(bf16[2,384,384]{2,1,0:T(8,128)(2,1)S(1)} %get-tuple-element.37), channel_id=1, source_target_pairs={{0,16},{1,17},{2,18},{3,19},{4,20},{5,21},{6,22},{7,23},{8,24},{9,... | collective-permute-start | bytes 1769480 | tf_op jit(solution)/shard_map/ppermute | solution.py:80
  48.6 6.6 %collective-permute-done.8.refs_3_.refs_4_ = bf16[2,768,384]{2,1,0:T(8,128)(2,1)S(1)} collective-permute-done((bf16[2,768,384]{2,1,0:T(8,128)(2,1)S(1)}, bf16[2,768,384]{2,1,0:T(8,128)(2,1)S(1)}, u32[]{:S(2)}, u32[]{:S(2)}) %collective-permute-start.8) | collective-permute-done | bytes 1179680 | tf_op jit(solution)/shard_map/ppermute | solution.py:80
  55.3 9.8 %attend_1_6.1.refs_0_ = f32[400,768]{1,0:T(8,128)S(1)} custom-call(s32[162]{0:T(256)S(1)} %reshape.250.mask_ref, bf16[768,384]{1,0:T(8,128)(2,1)S(1)} %get-tuple-element.40.refs_0_, bf16[2,768,384]{2,1,0:T(8,128)(2,1)S(1)} %get-tuple-element.36.refs_1_.refs_2_, bf16[2,768,384]{2,1,0:T(8,128)(2,1)S(1)} %collective-permute-done.7.refs_2_.refs_3_, ...), custom_call_target="tpu_custom_call" | custom-call | tf_op jit(solution)/shard_map/attend_1_6/pallas_call | solution.py:271
  65.1 8.4 %collective-permute-done.9.refs_1_.refs_5_ = bf16[2,384,384]{2,1,0:T(8,128)(2,1)S(1)} collective-permute-done((bf16[2,384,384]{2,1,0:T(8,128)(2,1)S(1)}, bf16[2,384,384]{2,1,0:T(8,128)(2,1)S(1)}, u32[]{:S(2)}, u32[]{:S(2)}) %collective-permute-start.9) | collective-permute-done | bytes 589856 | tf_op jit(solution)/shard_map/ppermute | solution.py:80
  73.5 1.3 collective-permute-start.13
  74.8 4.6 %collective-permute-start.12 = (bf16[768,384]{1,0:T(8,128)(2,1)S(1)}, bf16[768,384]{1,0:T(8,128)(2,1)S(1)}, u32[]{:S(2)}, u32[]{:S(2)}) collective-permute-start(bf16[768,384]{1,0:T(8,128)(2,1)S(1)} %get-tuple-element.40.refs_0_), channel_id=1, source_target_pairs={{0,4},{1,5},{2,6},{3,7},{4,8},{5,9},{6,10},{7,11},{8,12},{9,13},{1... | collective-permute-start | bytes 1769480 | tf_op jit(solution)/shard_map/ppermute | solution.py:80
  79.4 1.9 %collective-permute-start.11 = (bf16[2,384,384]{2,1,0:T(8,128)(2,1)S(1)}, bf16[2,384,384]{2,1,0:T(8,128)(2,1)S(1)}, u32[]{:S(2)}, u32[]{:S(2)}) collective-permute-start(bf16[2,384,384]{2,1,0:T(8,128)(2,1)S(1)} %collective-permute-done.9.refs_1_.refs_5_), channel_id=1, source_target_pairs={{1,64},{3,66},{5,68},{7,70},{9,72},{11,74},{13,76},{15,78},{17,80}... | collective-permute-start | bytes 1769480 | tf_op jit(solution)/shard_map/ppermute | solution.py:80
  81.3 1.5 %collective-permute-start.10 = (bf16[2,384,384]{2,1,0:T(8,128)(2,1)S(1)}, bf16[2,384,384]{2,1,0:T(8,128)(2,1)S(1)}, u32[]{:S(2)}, u32[]{:S(2)}) collective-permute-start(bf16[2,384,384]{2,1,0:T(8,128)(2,1)S(1)} %collective-permute-done.9.refs_1_.refs_5_), channel_id=1, source_target_pairs={{0,1},{1,0},{2,3},{3,2},{4,5},{5,4},{6,7},{7,6},{8,9},{9,8},{10,11... | collective-permute-start | bytes 1769480 | tf_op jit(solution)/shard_map/ppermute | solution.py:80
  82.8 7.0 %collective-permute-done.13.refs_1_ = bf16[768,384]{1,0:T(8,128)(2,1)S(1)} collective-permute-done((bf16[768,384]{1,0:T(8,128)(2,1)S(1)}, bf16[768,384]{1,0:T(8,128)(2,1)S(1)}, u32[]{:S(2)}, u32[]{:S(2)}) %collective-permute-start.13) | collective-permute-done | bytes 589856 | tf_op jit(solution)/shard_map/ppermute | solution.py:80
  89.8 1.2 collective-permute-done.12.refs_0_
  91.0 0.0 collective-permute-done.10.refs_2_.refs_6_
  91.0 11.3 %attend_2_9.1 = (bf16[400,768]{1,0:T(8,128)(2,1)S(1)}, bf16[400,768]{1,0:T(8,128)(2,1)S(1)}) custom-call(s32[162]{0:T(256)S(1)} %reshape.250.mask_ref, bf16[768,384]{1,0:T(8,128)(2,1)S(1)} %collective-permute-done.12.refs_0_, bf16[768,384]{1,0:T(8,128)(2,1)S(1)} %collective-permute-done.13.refs_1_, ...), custom_call_target="tpu_custom_call" | custom-call | tf_op jit(solution)/shard_map/attend_2_9/pallas_call | solution.py:271
  102.3 11.2 %collective-permute-start.14 = (bf16[400,768]{1,0:T(8,128)(2,1)S(1)}, bf16[400,768]{1,0:T(8,128)(2,1)S(1)}, u32[]{:S(2)}, u32[]{:S(2)}) collective-permute-start(bf16[400,768]{1,0:T(8,128)(2,1)S(1)} %get-tuple-element.41), channel_id=1, source_target_pairs={{0,4},{1,5},{2,6},{3,7},{4,8},{5,9},{6,10},{7,11},{8,12},{9,13},{1... | collective-permute-start | bytes 1843208 | tf_op jit(solution)/shard_map/ppermute | solution.py:80
  113.5 1.3 collective-permute-start.15
  114.8 0.1 add_convert_fusion.valid_ref
  114.9 4.0 %attend_1_3.1.refs_1_ = f32[400,768]{1,0:T(8,128)S(1)} custom-call(s32[162]{0:T(256)S(1)} %reshape.250.mask_ref, bf16[768,384]{1,0:T(8,128)(2,1)S(1)} %get-tuple-element.40.refs_0_, bf16[2,384,384]{2,1,0:T(8,128)(2,1)S(1)} %collective-permute-done.9.refs_1_.refs_5_, bf16[2,384,384]{2,1,0:T(8,128)(2,1)S(1)} %collective-permute-done.10.refs_2_.refs_6_, ...), custom_call_target="tpu_custom_call" | custom-call | tf_op jit(solution)/shard_map/attend_1_3/pallas_call | solution.py:271
  118.9 6.6 %collective-permute-done.14.refs_2_ = bf16[400,768]{1,0:T(8,128)(2,1)S(1)} collective-permute-done((bf16[400,768]{1,0:T(8,128)(2,1)S(1)}, bf16[400,768]{1,0:T(8,128)(2,1)S(1)}, u32[]{:S(2)}, u32[]{:S(2)}) %collective-permute-start.14) | collective-permute-done | bytes 614432 | tf_op jit(solution)/shard_map/ppermute | solution.py:80
  125.6 4.4 %collective-permute-done.15.refs_3_ = bf16[400,768]{1,0:T(8,128)(2,1)S(1)} collective-permute-done((bf16[400,768]{1,0:T(8,128)(2,1)S(1)}, bf16[400,768]{1,0:T(8,128)(2,1)S(1)}, u32[]{:S(2)}, u32[]{:S(2)}) %collective-permute-start.15) | collective-permute-done | bytes 614432 | tf_op jit(solution)/shard_map/ppermute | solution.py:80
  130.0 1.2 merge.1
  131.1 0.7 collective-permute-start.16
  131.8 2.6 %collective-permute-start.17 = (bf16[192,384]{1,0:T(8,128)(2,1)S(1)}, bf16[192,384]{1,0:T(8,128)(2,1)S(1)}, u32[]{:S(2)}, u32[]{:S(2)}) collective-permute-start(bf16[192,384]{1,0:T(8,128)(2,1)S(1)} %get-tuple-element.44), channel_id=1, source_target_pairs={{2,0},{0,1},{34,2},{32,3},{6,4},{4,5},{38,6},{36,7},{10,8},{8,9},{... | collective-permute-start | bytes 442376 | tf_op jit(solution)/shard_map/ppermute | solution.py:80
  134.4 1.9 %collective-permute-start.19 = (bf16[192,384]{1,0:T(8,128)(2,1)S(1)}, bf16[192,384]{1,0:T(8,128)(2,1)S(1)}, u32[]{:S(2)}, u32[]{:S(2)}) collective-permute-start(bf16[192,384]{1,0:T(8,128)(2,1)S(1)} %get-tuple-element.46), channel_id=1, source_target_pairs={{34,0},{32,1},{2,2},{0,3},{38,4},{36,5},{6,6},{4,7},{42,8},{40,9},... | collective-permute-start | bytes 442376 | tf_op jit(solution)/shard_map/ppermute | solution.py:80
  136.3 2.4 %collective-permute-done.17.refs_1_ = bf16[192,384]{1,0:T(8,128)(2,1)S(1)} collective-permute-done((bf16[192,384]{1,0:T(8,128)(2,1)S(1)}, bf16[192,384]{1,0:T(8,128)(2,1)S(1)}, u32[]{:S(2)}, u32[]{:S(2)}) %collective-permute-start.17) | collective-permute-done | bytes 147488 | tf_op jit(solution)/shard_map/ppermute | solution.py:80
  138.7 2.4 %collective-permute-done.18.refs_2_ = bf16[192,384]{1,0:T(8,128)(2,1)S(1)} collective-permute-done((bf16[192,384]{1,0:T(8,128)(2,1)S(1)}, bf16[192,384]{1,0:T(8,128)(2,1)S(1)}, u32[]{:S(2)}, u32[]{:S(2)}) %collective-permute-start.18) | collective-permute-done | bytes 147488 | tf_op jit(solution)/shard_map/ppermute | solution.py:80
  141.1 4.0 %collective-permute-done.19.refs_3_ = bf16[192,384]{1,0:T(8,128)(2,1)S(1)} collective-permute-done((bf16[192,384]{1,0:T(8,128)(2,1)S(1)}, bf16[192,384]{1,0:T(8,128)(2,1)S(1)}, u32[]{:S(2)}, u32[]{:S(2)}) %collective-permute-start.19) | collective-permute-done | bytes 147488 | tf_op jit(solution)/shard_map/ppermute | solution.py:80
  145.2 0.9 join.1
  (10 shorter events, 0.0 us)
Async XLA Ops:
  0.0 17.1 %collective-permute-start.4 = (s32[3,2,27]{2,1,0:T(2,128)}, s32[3,2,27]{2,1,0:T(2,128)S(1)}, u32[]{:S(2)}, u32[]{:S(2)}) collective-permute-start(s32[3,2,27]{2,1,0:T(2,128)} %param.3), channel_id=1, source_target_pairs={{0,0},{1,2},{2,32},{3,34},{4,4},{5,6},{6,36},{7,38},{8,8},{9,10},{... | collective-permute-start | bytes 1952 | tf_op jit(solution)/shard_map/ppermute | solution.py:80
  1.3 17.9 %collective-permute-start.6 = (s32[3,2,27]{2,1,0:T(2,128)}, s32[3,2,27]{2,1,0:T(2,128)S(1)}, u32[]{:S(2)}, u32[]{:S(2)}) collective-permute-start(s32[3,2,27]{2,1,0:T(2,128)} %param.3), channel_id=1, source_target_pairs={{4,0},{5,2},{6,32},{7,34},{8,4},{9,6},{10,36},{11,38},{12,8},{13,1... | collective-permute-start | bytes 1952 | tf_op jit(solution)/shard_map/ppermute | solution.py:80
  2.6 18.5 %collective-permute-start.5 = (s32[3,2,27]{2,1,0:T(2,128)}, s32[3,2,27]{2,1,0:T(2,128)S(1)}, u32[]{:S(2)}, u32[]{:S(2)}) collective-permute-start(s32[3,2,27]{2,1,0:T(2,128)} %param.3), channel_id=1, source_target_pairs={{0,4},{1,6},{2,36},{3,38},{4,8},{5,10},{6,40},{7,42},{8,12},{9,14}... | collective-permute-start | bytes 1952 | tf_op jit(solution)/shard_map/ppermute | solution.py:80
  7.2 1.5 %copy-start = (bf16[3,192,1536]{2,1,0:T(8,128)(2,1)S(1)}, bf16[3,192,1536]{2,1,0:T(8,128)(2,1)}, u32[]{:S(2)}) copy-start(bf16[3,192,1536]{2,1,0:T(8,128)(2,1)} %qkv_ref.1) | copy-start | bytes 5308420
  8.8 14.4 %collective-permute-start = (bf16[3,192,384]{2,1,0:T(8,128)(2,1)S(1)}, bf16[3,192,384]{2,1,0:T(8,128)(2,1)S(1)}, u32[]{:S(2)}, u32[]{:S(2)}) collective-permute-start(bf16[3,192,384]{2,1,0:T(8,128)(2,1)S(1)} %get-tuple-element.26), channel_id=1, source_target_pairs={{0,0},{1,2},{2,32},{3,34},{4,4},{5,6},{6,36},{7,38},{8,8},{9,10},{... | collective-permute-start | bytes 1327112 | tf_op jit(solution)/shard_map/ppermute | solution.py:80
  9.5 17.6 %collective-permute-start.1 = (bf16[3,192,384]{2,1,0:T(8,128)(2,1)S(1)}, bf16[3,192,384]{2,1,0:T(8,128)(2,1)S(1)}, u32[]{:S(2)}, u32[]{:S(2)}) collective-permute-start(bf16[3,192,384]{2,1,0:T(8,128)(2,1)S(1)} %get-tuple-element.27), channel_id=1, source_target_pairs={{0,2},{1,0},{2,34},{3,32},{4,6},{5,4},{6,38},{7,36},{8,10},{9,8},{... | collective-permute-start | bytes 1327112 | tf_op jit(solution)/shard_map/ppermute | solution.py:80
  17.1 19.6 %collective-permute-start.2 = (bf16[3,192,384]{2,1,0:T(8,128)(2,1)S(1)}, bf16[3,192,384]{2,1,0:T(8,128)(2,1)S(1)}, u32[]{:S(2)}, u32[]{:S(2)}) collective-permute-start(bf16[3,192,384]{2,1,0:T(8,128)(2,1)S(1)} %get-tuple-element.28), channel_id=1, source_target_pairs={{0,32},{1,34},{2,0},{3,2},{4,36},{5,38},{6,4},{7,6},{8,40},{9,42},... | collective-permute-start | bytes 1327112 | tf_op jit(solution)/shard_map/ppermute | solution.py:80
  19.2 17.5 %collective-permute-start.3 = (bf16[3,192,384]{2,1,0:T(8,128)(2,1)S(1)}, bf16[3,192,384]{2,1,0:T(8,128)(2,1)S(1)}, u32[]{:S(2)}, u32[]{:S(2)}) collective-permute-start(bf16[3,192,384]{2,1,0:T(8,128)(2,1)S(1)} %get-tuple-element.29), channel_id=1, source_target_pairs={{0,34},{1,32},{2,2},{3,0},{4,38},{5,36},{6,6},{7,4},{8,42},{9,40},... | collective-permute-start | bytes 1327112 | tf_op jit(solution)/shard_map/ppermute | solution.py:80
  37.7 17.5 %collective-permute-start.8 = (bf16[2,768,384]{2,1,0:T(8,128)(2,1)S(1)}, bf16[2,768,384]{2,1,0:T(8,128)(2,1)S(1)}, u32[]{:S(2)}, u32[]{:S(2)}) collective-permute-start(bf16[2,768,384]{2,1,0:T(8,128)(2,1)S(1)} %get-tuple-element.36.refs_1_.refs_2_), channel_id=1, source_target_pairs={{1,64},{3,66},{5,68},{7,70},{9,72},{11,74},{13,76},{15,78},{17,80}... | collective-permute-start | bytes 3538952 | tf_op jit(solution)/shard_map/ppermute | solution.py:80
  40.2 15.1 %collective-permute-start.7 = (bf16[2,768,384]{2,1,0:T(8,128)(2,1)S(1)}, bf16[2,768,384]{2,1,0:T(8,128)(2,1)S(1)}, u32[]{:S(2)}, u32[]{:S(2)}) collective-permute-start(bf16[2,768,384]{2,1,0:T(8,128)(2,1)S(1)} %get-tuple-element.36.refs_1_.refs_2_), channel_id=1, source_target_pairs={{0,1},{1,0},{2,3},{3,2},{4,5},{5,4},{6,7},{7,6},{8,9},{9,8},{10,11... | collective-permute-start | bytes 3538952 | tf_op jit(solution)/shard_map/ppermute | solution.py:80
  41.4 32.1 %collective-permute-start.9 = (bf16[2,384,384]{2,1,0:T(8,128)(2,1)S(1)}, bf16[2,384,384]{2,1,0:T(8,128)(2,1)S(1)}, u32[]{:S(2)}, u32[]{:S(2)}) collective-permute-start(bf16[2,384,384]{2,1,0:T(8,128)(2,1)S(1)} %get-tuple-element.37), channel_id=1, source_target_pairs={{0,16},{1,17},{2,18},{3,19},{4,20},{5,21},{6,22},{7,23},{8,24},{9,... | collective-permute-start | bytes 1769480 | tf_op jit(solution)/shard_map/ppermute | solution.py:80
  73.5 16.3 %collective-permute-start.13 = (bf16[768,384]{1,0:T(8,128)(2,1)S(1)}, bf16[768,384]{1,0:T(8,128)(2,1)S(1)}, u32[]{:S(2)}, u32[]{:S(2)}) collective-permute-start(bf16[768,384]{1,0:T(8,128)(2,1)S(1)} %get-tuple-element.40.refs_0_), channel_id=1, source_target_pairs={{4,0},{5,1},{6,2},{7,3},{8,4},{9,5},{10,6},{11,7},{12,8},{13,9},{1... | collective-permute-start | bytes 1769480 | tf_op jit(solution)/shard_map/ppermute | solution.py:80
  74.8 16.2 %collective-permute-start.12 = (bf16[768,384]{1,0:T(8,128)(2,1)S(1)}, bf16[768,384]{1,0:T(8,128)(2,1)S(1)}, u32[]{:S(2)}, u32[]{:S(2)}) collective-permute-start(bf16[768,384]{1,0:T(8,128)(2,1)S(1)} %get-tuple-element.40.refs_0_), channel_id=1, source_target_pairs={{0,4},{1,5},{2,6},{3,7},{4,8},{5,9},{6,10},{7,11},{8,12},{9,13},{1... | collective-permute-start | bytes 1769480 | tf_op jit(solution)/shard_map/ppermute | solution.py:80
  79.4 11.6 %collective-permute-start.11 = (bf16[2,384,384]{2,1,0:T(8,128)(2,1)S(1)}, bf16[2,384,384]{2,1,0:T(8,128)(2,1)S(1)}, u32[]{:S(2)}, u32[]{:S(2)}) collective-permute-start(bf16[2,384,384]{2,1,0:T(8,128)(2,1)S(1)} %collective-permute-done.9.refs_1_.refs_5_), channel_id=1, source_target_pairs={{1,64},{3,66},{5,68},{7,70},{9,72},{11,74},{13,76},{15,78},{17,80}... | collective-permute-start | bytes 1769480 | tf_op jit(solution)/shard_map/ppermute | solution.py:80
  81.3 9.7 %collective-permute-start.10 = (bf16[2,384,384]{2,1,0:T(8,128)(2,1)S(1)}, bf16[2,384,384]{2,1,0:T(8,128)(2,1)S(1)}, u32[]{:S(2)}, u32[]{:S(2)}) collective-permute-start(bf16[2,384,384]{2,1,0:T(8,128)(2,1)S(1)} %collective-permute-done.9.refs_1_.refs_5_), channel_id=1, source_target_pairs={{0,1},{1,0},{2,3},{3,2},{4,5},{5,4},{6,7},{7,6},{8,9},{9,8},{10,11... | collective-permute-start | bytes 1769480 | tf_op jit(solution)/shard_map/ppermute | solution.py:80
  102.3 23.2 %collective-permute-start.14 = (bf16[400,768]{1,0:T(8,128)(2,1)S(1)}, bf16[400,768]{1,0:T(8,128)(2,1)S(1)}, u32[]{:S(2)}, u32[]{:S(2)}) collective-permute-start(bf16[400,768]{1,0:T(8,128)(2,1)S(1)} %get-tuple-element.41), channel_id=1, source_target_pairs={{0,4},{1,5},{2,6},{3,7},{4,8},{5,9},{6,10},{7,11},{8,12},{9,13},{1... | collective-permute-start | bytes 1843208 | tf_op jit(solution)/shard_map/ppermute | solution.py:80
  113.5 16.5 %collective-permute-start.15 = (bf16[400,768]{1,0:T(8,128)(2,1)S(1)}, bf16[400,768]{1,0:T(8,128)(2,1)S(1)}, u32[]{:S(2)}, u32[]{:S(2)}) collective-permute-start(bf16[400,768]{1,0:T(8,128)(2,1)S(1)} %get-tuple-element.42), channel_id=1, source_target_pairs={{4,0},{5,1},{6,2},{7,3},{8,4},{9,5},{10,6},{11,7},{12,8},{13,9},{1... | collective-permute-start | bytes 1843208 | tf_op jit(solution)/shard_map/ppermute | solution.py:80
  131.1 5.2 %collective-permute-start.16 = (bf16[192,384]{1,0:T(8,128)(2,1)S(1)}, bf16[192,384]{1,0:T(8,128)(2,1)S(1)}, u32[]{:S(2)}, u32[]{:S(2)}) collective-permute-start(bf16[192,384]{1,0:T(8,128)(2,1)S(1)} %get-tuple-element.43), channel_id=1, source_target_pairs={{0,0},{2,1},{32,2},{34,3},{4,4},{6,5},{36,6},{38,7},{8,8},{10,9},{... | collective-permute-start | bytes 442376 | tf_op jit(solution)/shard_map/ppermute | solution.py:80
  131.8 6.9 %collective-permute-start.17 = (bf16[192,384]{1,0:T(8,128)(2,1)S(1)}, bf16[192,384]{1,0:T(8,128)(2,1)S(1)}, u32[]{:S(2)}, u32[]{:S(2)}) collective-permute-start(bf16[192,384]{1,0:T(8,128)(2,1)S(1)} %get-tuple-element.44), channel_id=1, source_target_pairs={{2,0},{0,1},{34,2},{32,3},{6,4},{4,5},{38,6},{36,7},{10,8},{8,9},{... | collective-permute-start | bytes 442376 | tf_op jit(solution)/shard_map/ppermute | solution.py:80
  134.4 6.8 %collective-permute-start.18 = (bf16[192,384]{1,0:T(8,128)(2,1)S(1)}, bf16[192,384]{1,0:T(8,128)(2,1)S(1)}, u32[]{:S(2)}, u32[]{:S(2)}) collective-permute-start(bf16[192,384]{1,0:T(8,128)(2,1)S(1)} %get-tuple-element.45), channel_id=1, source_target_pairs={{32,0},{34,1},{0,2},{2,3},{36,4},{38,5},{4,6},{6,7},{40,8},{42,9},... | collective-permute-start | bytes 442376 | tf_op jit(solution)/shard_map/ppermute | solution.py:80
  134.4 10.8 %collective-permute-start.19 = (bf16[192,384]{1,0:T(8,128)(2,1)S(1)}, bf16[192,384]{1,0:T(8,128)(2,1)S(1)}, u32[]{:S(2)}, u32[]{:S(2)}) collective-permute-start(bf16[192,384]{1,0:T(8,128)(2,1)S(1)} %get-tuple-element.46), channel_id=1, source_target_pairs={{34,0},{32,1},{2,2},{0,3},{38,4},{36,5},{6,6},{4,7},{42,8},{40,9},... | collective-permute-start | bytes 442376 | tf_op jit(solution)/shard_map/ppermute | solution.py:80
